TPU v7x, 128 devices: a whole 4x4x4 slice. The times are simulated.
128 devices in a mesh: rows: 32 (over x, z, core), rel: 4 (over y).
Axes of the slice: x: 4, y: 4, z: 4, core: 2. Of those that a mesh axis runs over, the one named last changes fastest.
Arguments:
- features: bfloat16 [16384, 256], P('rows'), may hold values from -6 to 6
- bases: bfloat16 [8, 256, 256], replicated, may hold values from -0.125 to 0.125
- root: bfloat16 [256, 256], replicated, may hold values from -0.375 to 0.375
- coeffs: float32 [800, 8], P('rel'), may hold values from -4 to 4
- tiles: bfloat16 [32, 4, 64, 128, 128], P('rows', 'rel'), as said below
- tile_dst: int32 [32, 4, 64], P('rows', 'rel'), may hold values from 0 to 3
- tile_src: int32 [32, 4, 64], P('rows', 'rel'), may hold values from 0 to 63
- tile_rel: int32 [32, 4, 64], P('rows', 'rel'), may hold values from 0 to 199
- tile_live: int32 [32, 4], P('rows', 'rel'), may hold values from 16 to 64, as said below
- send_list: int32 [32, 4, 32, 2], P('rows', 'rel'), may hold values from 0 to 3
- cotangent: bfloat16 [16384, 256], P('rows'), may hold values from -6 to 6
Outputs:
- output: bfloat16 [16384, 256], P('rows')
- feature_grad: float32 [16384, 256], P('rows')
- basis_grad: float32 [8, 256, 256], replicated
- root_grad: float32 [256, 256], replicated
Inputs may be any that keep to these rules, and one draw needn't show every extreme that they name: `tile_live`: at least one device uses all 64 tile slots. `tiles`: entries are zero or positive, at most 12 / sqrt(2048).
All inputs are finite; a program needn't handle non-finite values.
Results may differ from a plain program's by a relative error of at most 0.0029.
Values may be sent and summed in bfloat16 or wider, within the bound.
A program may use at most 128 MiB of HBM per device.

v0:
```python
import math

import jax
import jax.numpy as jnp
from jax import lax
from jax.sharding import PartitionSpec as P

SLOT_GRAD_LINK_DTYPE = jnp.float32


def a2a_psum(value, axes):
    count = 1
    for name in axes:
        count *= lax.axis_size(name)
    flat = value.reshape(count, -1)
    pieces = lax.all_to_all(flat, axes, 0, 0, tiled=True)
    reduced = jnp.sum(pieces, axis=0, keepdims=True)
    spread_out = jnp.broadcast_to(reduced, flat.shape)
    gathered = lax.all_to_all(spread_out, axes, 0, 0, tiled=True)
    return gathered.reshape(value.shape)


def on_device(
    features,
    bases,
    root,
    coeffs,
    tiles,
    tile_dst,
    tile_src,
    tile_rel,
    tile_live,
    send_list,
    cotangent,
):
    highest = lax.Precision.HIGHEST
    contract_first = (((0,), (0,)), ((), ()))
    feat_width = features.shape[1]
    size_block = tiles.shape[-1]
    blocks = features.reshape(-1, size_block, feat_width)
    local_blocks = blocks.shape[0]
    num_bases = bases.shape[0]
    slots_peer = send_list.shape[-1]
    row_devices = lax.axis_size("rows")
    total_slots = row_devices * slots_peer
    count_tiles = tiles.shape[2]
    adjacency = tiles[0, 0]
    dst_ids = tile_dst[0, 0]
    src_ids = tile_src[0, 0]
    rel_ids = tile_rel[0, 0]
    live_count = tile_live[0, 0]
    send_rows = send_list[0, 0]
    step_tiles = math.gcd(count_tiles, 64)
    steps_live = (live_count + step_tiles - 1) // step_tiles

    def tile_weights(first_tile):
        position = first_tile + jnp.arange(step_tiles)
        in_use = (position < live_count).astype(jnp.float32)
        rel_hot = (rel_ids[:, None] == jnp.arange(coeffs.shape[0])[None, :]).astype(jnp.float32)
        coef_rows = jnp.dot(rel_hot, coeffs, precision=highest)
        dst_hot = (dst_ids[:, None] == jnp.arange(local_blocks)[None, :]).astype(
            jnp.float32
        ) * in_use[:, None]
        return (dst_hot[:, :, None] * coef_rows[:, None, :]).reshape(
            step_tiles, local_blocks * num_bases
        )

    outgoing = blocks[send_rows]
    incoming = lax.all_to_all(outgoing, "rows", split_axis=0, concat_axis=0, tiled=True)

    cot_blocks = cotangent.reshape(local_blocks, size_block, feat_width)
    agg_grad = jnp.einsum("lng,bfg->lbnf", cot_blocks, bases, preferred_element_type=jnp.float32)
    agg_grad = agg_grad.reshape(local_blocks * num_bases, size_block * feat_width)

    def backward_step(block_index, running):
        first_tile = block_index * step_tiles
        weights = tile_weights(first_tile)
        spread = jnp.dot(weights, agg_grad, precision=highest).astype(jnp.bfloat16)
        spread = spread.reshape(step_tiles, size_block, feat_width)
        backward_term = jnp.einsum(
            "tij,tif->tjf", adjacency, spread, preferred_element_type=jnp.float32
        )
        slot_hot = (src_ids[:, None] == jnp.arange(total_slots)[None, :]).astype(jnp.float32)
        return running + lax.dot_general(
            slot_hot, backward_term.reshape(step_tiles, -1), contract_first, precision=highest
        )

    slot_zero = jnp.zeros((total_slots, size_block * feat_width), jnp.float32)
    slot_grads = lax.fori_loop(0, steps_live, backward_step, slot_zero)
    incoming, slot_grads = lax.optimization_barrier((incoming, slot_grads))

    returned = lax.all_to_all(
        slot_grads.astype(SLOT_GRAD_LINK_DTYPE).reshape(
            row_devices, slots_peer, size_block * feat_width
        ),
        "rows",
        split_axis=0,
        concat_axis=0,
        tiled=True,
    )

    received = incoming.reshape(total_slots, size_block, feat_width)

    def forward_step(block_index, running):
        first_tile = block_index * step_tiles
        sources = received[src_ids]
        messages = jnp.einsum(
            "tij,tjf->tif", adjacency, sources, preferred_element_type=jnp.float32
        )
        weights = tile_weights(first_tile)
        return running + lax.dot_general(
            weights, messages.reshape(step_tiles, -1), contract_first, precision=highest
        )

    zero_total = jnp.zeros((local_blocks * num_bases, size_block * feat_width), jnp.float32)
    partial_value = lax.fori_loop(0, steps_live, forward_step, zero_total)
    partial_value = partial_value.reshape(local_blocks, num_bases, size_block, feat_width)
    basis_f32 = bases.astype(jnp.float32)
    cot_f32 = cot_blocks.astype(jnp.float32)
    root_term = jnp.dot(features, root, preferred_element_type=jnp.float32)
    rel_devices = lax.axis_size("rel")
    part_rows = features.shape[0] // rel_devices
    first_row = lax.axis_index("rel") * part_rows
    feat_part = lax.dynamic_slice_in_dim(features, first_row, part_rows)
    cot_part = lax.dynamic_slice_in_dim(cotangent, first_row, part_rows)
    root_local = lax.dot_general(
        feat_part, cot_part, contract_first, preferred_element_type=jnp.float32
    )
    projected_part = jnp.einsum("lbnf,bfg->lng", partial_value, basis_f32, precision=highest)
    basis_local = jnp.einsum("lbnf,lng->bfg", partial_value, cot_f32, precision=highest)
    returned, projected_part, basis_local, root_local = lax.optimization_barrier(
        (returned, projected_part, basis_local, root_local)
    )

    projected = a2a_psum(projected_part, ("rel",))
    output = (projected.reshape(-1, feat_width) + root_term).astype(jnp.bfloat16)
    grads_flat = jnp.concatenate([basis_local.reshape(-1), root_local.reshape(-1)])
    grads_flat = a2a_psum(grads_flat, ("rows", "rel"))
    basis_grad = grads_flat[: basis_local.size].reshape(basis_local.shape)
    root_grad = grads_flat[basis_local.size :].reshape(root_local.shape)

    block_hot = (send_rows.reshape(-1)[None, :] == jnp.arange(local_blocks)[:, None]).astype(
        jnp.float32
    )
    own_grads = jnp.dot(
        block_hot, returned.astype(jnp.float32).reshape(total_slots, -1), precision=highest
    )
    summed = a2a_psum(own_grads, ("rel",))
    root_back = lax.dot_general(
        cotangent, root, (((1,), (1,)), ((), ())), preferred_element_type=jnp.float32
    )
    feature_grad = summed.reshape(-1, feat_width) + root_back
    return (output, feature_grad, basis_grad, root_grad)


def solution(mesh):
    return jax.shard_map(
        on_device,
        mesh=mesh,
        in_specs=(
            P("rows", None),
            P(),
            P(),
            P("rel", None),
            P("rows", "rel", None, None, None),
            P("rows", "rel", None),
            P("rows", "rel", None),
            P("rows", "rel", None),
            P("rows", "rel"),
            P("rows", "rel", None, None),
            P("rows", None),
        ),
        out_specs=(P("rows", None), P("rows", None), P(), P()),
        check_vma=False,
    )
```

profile of v0, /device:TPU:1, one launch (start us, length us, event | category | flops | bytes accessed | tf_op | source)
XLA Modules:
  0.0 369.4 jit_solution(5121115384269204709)
XLA Ops:
  1.6 3.7 %gather_fusion = bf16[64,128,256]{2,1,0:T(8,128)(2,1)} fusion(bf16[4,128,256]{2,1,0:T(8,128)(2,1)} %bitcast.127, s32[1024]{0:T(1024)S(1)} %pad_clamp_fusion.1), kind=kCustom, calls=%fused_computation | custom fusion | bytes 8388864 | tf_op jit(solution)/shard_map/gather | solution.py:68
  5.3 9.6 %all-to-all-start = ((bf16[32,2,128,256]{3,2,1,0:T(8,128)(2,1)}), bf16[32,2,128,256]{3,2,1,0:T(8,128)(2,1)}, u32[]{:S(2)}, u32[]{:S(2)}) async-start(bf16[32,2,128,256]{3,2,1,0:T(8,128)(2,1)} %bitcast.128), calls=%async_computation | async-start | bytes 8388608 | tf_op jit(solution)/shard_map/all_to_all | solution.py:69
  18.3 5.5 %copy.65 = f32[4,8,128,256]{3,1,2,0:T(8,128)} copy(f32[4,8,128,256]{2,3,0,1:T(8,128)} %convolution_bitcast_fusion.2) | data formatting | bytes 8388608
  24.1 3.9 %broadcast_in_dim.16 = f32[64,32768]{1,0:T(8,128)} broadcast(f32[]{:T(128)} %constant.58.clone.1), dimensions={} | broadcast | bytes 8388612 | tf_op jit(solution)/shard_map/broadcast_in_dim | solution.py:88
  28.0 38.3 %while.24 = (s32[]{:T(128)}, f32[64,32768]{1,0:T(8,128)}, s32[]{:T(128)}, s32[1,1,64]{2,1,0:T(1,128)S(1)}, s32[1,1,64]{2,1,0:T(1,128)S(1)}, /*index=5*/s32[]{:T(...) while((s32[]{:T(128)}, f32[64,32768]{1,0:T(8,128)}, ...), condition=%wide.region_1.2_spmd, body=%wide.region_0.1_spmd.sunk | while | flops 2956991232 | bytes 73405576 | solution.py:89
  28.9 8.6 %convolution_convert_fusion.2 = bf16[64,32768]{1,0:T(8,128)(2,1)S(1)} fusion(f32[32,32768]{1,0:T(8,128)} %get-tuple-element.418, f32[64,8]{0,1:T(8,128)S(1)} %get-tuple-element.417, f32[64,4]{0,1:T(4,128)S(1)} %fusion.65), kind=kOutput, calls=%fused_computation.3.clone.1 | convolution fusion | flops 807405568 | bytes 8391680 | tf_op jit(solution)/shard_map/while/body/dot_general | solution.py:78
  38.5 4.6 %convolution_bitcast_fusion.4 = f32[64,128,256]{1,2,0:T(8,128)} fusion(bf16[64,128,256]{2,1,0:T(8,128)(2,1)S(1)} %bitcast.121, bf16[64,128,128]{2,1,0:T(8,128)(2,1)S(1)} %get-tuple-element.419), kind=kOutput, calls=%fused_computation.4.clone.1 | convolution fusion | flops 536870912 | bytes 14680064 | tf_op jit(solution)/shard_map/while/body/tij,tif->tjf/dot_general | solution.py:80
  43.1 9.2 %copy.82 = f32[8,8,128,256]{3,1,2,0:T(8,128)} copy(f32[8,8,128,256]{2,3,1,0:T(8,128)} %bitcast.119) | data formatting | bytes 16777216 | tf_op jit(solution)/shard_map/while
  52.3 14.0 %convolution_add_fusion.6 = f32[64,32768]{1,0:T(8,128)} fusion(f32[64,32768]{1,0:T(8,128)} %get-tuple-element.401, f32[64,32768]{1,0:T(8,128)} %bitcast.118, s32[64]{0:T(128)S(1)} %bitcast.138), kind=kOutput, calls=%fused_computation.2.clone.1 | convolution fusion | flops 1612713984 | bytes 25166080 | tf_op jit(solution)/shard_map/while/body/dot_general | solution.py:84
  67.1 10.6 %reshape.280 = f32[32,2,32768]{2,1,0:T(2,128)} reshape(f32[64,32768]{1,0:T(8,128)} %get-tuple-element.242) | data formatting | bytes 16777216 | tf_op jit(solution)/shard_map/reshape | solution.py:93
  77.6 7.2 %all-to-all-start.1 = ((f32[32,2,32768]{2,1,0:T(2,128)}), f32[32,2,32768]{2,1,0:T(2,128)}, u32[]{:S(2)}, u32[]{:S(2)}) async-start(f32[32,2,32768]{2,1,0:T(2,128)} %reshape.280), calls=%async_computation.1 | async-start | bytes 16777216 | tf_op jit(solution)/shard_map/all_to_all | solution.py:92
  86.8 4.9 %gather_fusion.1 = bf16[64,128,256]{2,1,0:T(8,128)(2,1)} fusion(bf16[64,128,256]{2,1,0:T(8,128)(2,1)} %bitcast.17, s32[1024]{0:T(1024)S(1)} %pad_clamp_fusion), kind=kCustom, calls=%fused_computation.1 | custom fusion | bytes 8388864 | tf_op jit(solution)/shard_map/while/body/gather | solution.py:106
  94.0 20.8 %while.25 = (s32[]{:T(128)}, f32[32,32768]{1,0:T(8,128)}, s32[]{:T(128)}, s32[1,1,64]{2,1,0:T(1,128)S(1)}, s32[]{:T(128)}, /*index=5*/f32[64,8]{0,1:T(8,128)S(1)...) while((s32[]{:T(128)}, f32[32,32768]{1,0:T(8,128)}, s32[]{:T(128)}, ...), condition=%wide.region_3.4_spmd, body=%wide.region_2.3_spmd.sunk | while | flops 1343228672 | bytes 48239488 | solution.py:116
  94.0 3.4 fusion.70
  97.4 7.9 %copy.83 = f32[8,8,128,256]{3,1,2,0:T(8,128)} copy(f32[8,8,128,256]{3,2,1,0:T(8,128)S(1)} %bitcast.120) | data formatting | bytes 16777216 | tf_op jit(solution)/shard_map/while
  106.0 8.4 %convolution_add_fusion.7 = f32[32,32768]{1,0:T(8,128)} fusion(f32[32,32768]{1,0:T(8,128)} %get-tuple-element.433, f32[64,32768]{1,0:T(8,128)} %bitcast.117, f32[64,8]{0,1:T(8,128)S(1)} %get-tuple-element.447, f32[64,4]{0,1:T(4,128)S(1)} %fusion.71), kind=kOutput, calls=%fused_computation.14.clone.1 | convolution fusion | flops 806356992 | bytes 16780288 | tf_op jit(solution)/shard_map/while/body/dot_general | solution.py:111
  114.8 6.4 %fusion.15 = f32[8,256,256]{2,1,0:T(8,128)S(1)} fusion(bf16[4,128,256,1]{2,1,0,3:T(8,128)(2,1)} %bitcast.132, f32[4,8,128,256]{3,1,2,0:T(8,128)} %bitcast.123), kind=kOutput, calls=%fused_computation.29 | convolution fusion | flops 3221225472 | bytes 6553600 | tf_op jit(solution)/shard_map/lbnf,lng->bfg/dot_general | solution.py:130
  121.3 3.8 %fusion.18 = f32[4,128,256]{2,1,0:T(8,128)} fusion(f32[4,8,128,256]{3,1,2,0:T(8,128)S(1)} %bitcast.124, bf16[8,256,256]{2,1,0:T(8,128)(2,1)S(1)} %copy-done), kind=kOutput, calls=%fused_computation.30 | convolution fusion | flops 3221225472 | bytes 5767168 | tf_op jit(solution)/shard_map/lbnf,bfg->lng/dot_general | solution.py:129
  125.1 67.0 %all-to-all-done.1 = f32[32,2,32768]{2,1,0:T(2,128)} async-done(((f32[32,2,32768]{2,1,0:T(2,128)}), f32[32,2,32768]{2,1,0:T(2,128)}, u32[]{:S(2)}, u32[]{:S(2)}) %all-to-all-start.1) | async-done | bytes 8388640 | tf_op jit(solution)/shard_map/all_to_all | solution.py:92
  194.4 4.4 %all-to-all-start.2 = ((f32[4,1,32768]{2,1,0:T(1,128)}), f32[4,1,32768]{2,1,0:T(1,128)}, u32[]{:S(2)}, u32[]{:S(2)}) async-start(f32[4,1,32768]{2,1,0:T(1,128)} %all_to_all.47), calls=%async_computation.2 | async-start | bytes 1048576 | tf_op jit(solution)/shard_map/all_to_all | solution.py:16
  198.8 10.8 %reshape.284 = f32[64,32768]{1,0:T(8,128)} reshape(f32[32,2,32768]{2,1,0:T(2,128)} %all-to-all-done.1) | data formatting | bytes 16777216 | tf_op jit(solution)/shard_map/reshape | solution.py:146
  209.6 6.2 %convolution_bitcast_fusion.1 = f32[4,1,32768]{2,0,1:T(4,128)S(1)} fusion(f32[64,32768]{1,0:T(8,128)} %reshape.284, s32[64]{0:T(128)S(1)} %eq.116), kind=kOutput, calls=%fused_computation.22 | convolution fusion | flops 100663552 | bytes 8913152 | tf_op jit(solution)/shard_map/dot_general | solution.py:145
  217.1 4.2 %all-to-all-start.4 = ((f32[4,1,32768]{2,1,0:T(1,128)}), f32[4,1,32768]{2,1,0:T(1,128)}, u32[]{:S(2)}, u32[]{:S(2)}) async-start(f32[4,1,32768]{2,1,0:T(1,128)} %copy.55), calls=%async_computation.4 | async-start | bytes 1048576 | tf_op jit(solution)/shard_map/all_to_all | solution.py:16
  229.5 3.5 all-to-all-start.3
  236.2 3.7 all-to-all-done.3
  239.9 24.5 %all-to-all-start.6 = ((f32[128,1,4608]{2,1,0:T(1,128)}), f32[128,1,4608]{2,1,0:T(1,128)}, u32[]{:S(2)}, u32[]{:S(2)}) async-start(f32[128,1,4608]{2,1,0:T(1,128)} %bitcast.129), calls=%async_computation.6 | async-start | bytes 4718592 | tf_op jit(solution)/shard_map/all_to_all | solution.py:16
  265.9 31.9 %all-to-all-done.6 = f32[128,1,4608]{2,1,0:T(1,128)} async-done(((f32[128,1,4608]{2,1,0:T(1,128)}), f32[128,1,4608]{2,1,0:T(1,128)}, u32[]{:S(2)}, u32[]{:S(2)}) %all-to-all-start.6) | async-done | bytes 2359328 | tf_op jit(solution)/shard_map/all_to_all | solution.py:16
  298.9 3.5 all-to-all-start.5
  305.4 6.4 %all-to-all-done.5 = f32[4,1,32768]{2,1,0:T(1,128)S(1)} async-done(((f32[4,1,32768]{2,1,0:T(1,128)}), f32[4,1,32768]{2,1,0:T(1,128)S(1)}, u32[]{:S(2)}, u32[]{:S(2)}) %all-to-all-start.5) | async-done | bytes 524320 | tf_op jit(solution)/shard_map/all_to_all | solution.py:19
  314.4 6.0 %all-to-all-start.7 = ((f32[128,1,4608]{2,1,0:T(1,128)}), f32[128,1,4608]{2,1,0:T(1,128)}, u32[]{:S(2)}, u32[]{:S(2)}) async-start(f32[128,1,4608]{2,1,0:T(1,128)} %broadcast_in_dim.20), calls=%async_computation.7 | async-start | bytes 4718592 | tf_op jit(solution)/shard_map/all_to_all | solution.py:19
  326.2 27.7 %all-to-all-done.7 = f32[128,1,4608]{2,1,0:T(1,128)} async-done(((f32[128,1,4608]{2,1,0:T(1,128)}), f32[128,1,4608]{2,1,0:T(1,128)}, u32[]{:S(2)}, u32[]{:S(2)}) %all-to-all-start.7) | async-done | bytes 2359328 | tf_op jit(solution)/shard_map/all_to_all | solution.py:19
  353.9 7.3 %reduce.5 = f32[128,4608]{1,0:T(8,128)S(1)} reduce(f32[128,1,4608]{2,1,0:T(1,128)} %all-to-all-done.7, f32[]{:T(128)} %constant.73), dimensions={1}, to_apply=%all_to_all.46.reduce_sub_computation | reduce | bytes 4718596 | tf_op jit(solution)/shard_map/all_to_all | solution.py:19
  (65 shorter events, 48.2 us)
Async XLA Ops:
  0.6 15.0 %copy-start = (bf16[8,256,256]{2,1,0:T(8,128)(2,1)S(1)}, bf16[8,256,256]{2,1,0:T(8,128)(2,1)}, u32[]{:S(2)}) copy-start(bf16[8,256,256]{2,1,0:T(8,128)(2,1)} %param.16) | copy-start | bytes 3145732
  5.3 10.3 %copy-start.4 = (bf16[512,256]{1,0:T(8,128)(2,1)S(1)}, bf16[512,256]{1,0:T(8,128)(2,1)}, u32[]{:S(2)}) copy-start(bf16[512,256]{1,0:T(8,128)(2,1)} %param.25) | copy-start | bytes 786436
  5.3 61.7 %all-to-all-start = ((bf16[32,2,128,256]{3,2,1,0:T(8,128)(2,1)}), bf16[32,2,128,256]{3,2,1,0:T(8,128)(2,1)}, u32[]{:S(2)}, u32[]{:S(2)}) async-start(bf16[32,2,128,256]{3,2,1,0:T(8,128)(2,1)} %bitcast.128), calls=%async_computation | async-start | bytes 8388608 | tf_op jit(solution)/shard_map/all_to_all | solution.py:69
  18.3 5.5 %copy-start.10 = (f32[200,8]{0,1:T(8,128)S(1)}, f32[200,8]{0,1:T(8,128)}, u32[]{:S(2)}) copy-start(f32[200,8]{0,1:T(8,128)} %param.18) | copy-start | bytes 19204
  18.3 5.5 %copy-start.11 = (s32[1,1,64]{2,1,0:T(1,128)S(1)}, s32[1,1,64]{2,1,0:T(1,128)}, u32[]{:S(2)}) copy-start(s32[1,1,64]{2,1,0:T(1,128)} %param.22) | copy-start | bytes 772
  24.1 3.9 %copy-start.2 = (bf16[1,1,64,128,128]{4,3,2,1,0:T(8,128)(2,1)S(1)}, bf16[1,1,64,128,128]{4,3,2,1,0:T(8,128)(2,1)}, u32[]{:S(2)}) copy-start(bf16[1,1,64,128,128]{4,3,2,1,0:T(8,128)(2,1)} %param.19) | copy-start | bytes 6291460
  24.1 3.9 %copy-start.7 = (s32[1,1,64]{2,1,0:T(1,128)S(1)}, s32[1,1,64]{2,1,0:T(1,128)}, u32[]{:S(2)}) copy-start(s32[1,1,64]{2,1,0:T(1,128)} %param.20) | copy-start | bytes 772
  24.1 3.9 %copy-start.8 = (s32[1,1,64]{2,1,0:T(1,128)S(1)}, s32[1,1,64]{2,1,0:T(1,128)}, u32[]{:S(2)}) copy-start(s32[1,1,64]{2,1,0:T(1,128)} %param.21) | copy-start | bytes 772
  77.6 7.2 %copy-start.9 = (s32[1,1,32,2]{2,3,1,0:T(2,128)S(1)}, s32[1,1,32,2]{2,3,1,0:T(2,128)}, u32[]{:S(2)}) copy-start(s32[1,1,32,2]{2,3,1,0:T(2,128)} %param.24) | copy-start | bytes 772
  77.6 7.5 %copy-start.3 = (bf16[512,256]{1,0:T(8,128)(2,1)S(1)}, bf16[512,256]{1,0:T(8,128)(2,1)}, u32[]{:S(2)}) copy-start(bf16[512,256]{1,0:T(8,128)(2,1)} %param.15) | copy-start | bytes 786436
  77.6 114.4 %all-to-all-start.1 = ((f32[32,2,32768]{2,1,0:T(2,128)}), f32[32,2,32768]{2,1,0:T(2,128)}, u32[]{:S(2)}, u32[]{:S(2)}) async-start(f32[32,2,32768]{2,1,0:T(2,128)} %reshape.280), calls=%async_computation.1 | async-start | bytes 16777216 | tf_op jit(solution)/shard_map/all_to_all | solution.py:92
  114.8 6.4 %copy-start.1 = (f32[32,32768]{1,0:T(8,128)S(1)}, f32[32,32768]{1,0:T(8,128)}, u32[]{:S(2)}) copy-start(f32[32,32768]{1,0:T(8,128)} %get-tuple-element.244) | copy-start | bytes 12582916
  194.4 22.7 %all-to-all-start.2 = ((f32[4,1,32768]{2,1,0:T(1,128)}), f32[4,1,32768]{2,1,0:T(1,128)}, u32[]{:S(2)}, u32[]{:S(2)}) async-start(f32[4,1,32768]{2,1,0:T(1,128)} %all_to_all.47), calls=%async_computation.2 | async-start | bytes 1048576 | tf_op jit(solution)/shard_map/all_to_all | solution.py:16
  217.1 11.3 %all-to-all-start.4 = ((f32[4,1,32768]{2,1,0:T(1,128)}), f32[4,1,32768]{2,1,0:T(1,128)}, u32[]{:S(2)}, u32[]{:S(2)}) async-start(f32[4,1,32768]{2,1,0:T(1,128)} %copy.55), calls=%async_computation.4 | async-start | bytes 1048576 | tf_op jit(solution)/shard_map/all_to_all | solution.py:16
  229.5 10.4 %all-to-all-start.3 = ((f32[4,1,32768]{2,1,0:T(1,128)}), f32[4,1,32768]{2,1,0:T(1,128)S(1)}, u32[]{:S(2)}, u32[]{:S(2)}) async-start(f32[4,1,32768]{2,1,0:T(1,128)} %broadcast_in_dim.18), calls=%async_computation.3 | async-start | bytes 1048576 | tf_op jit(solution)/shard_map/all_to_all | solution.py:19
  239.9 58.0 %all-to-all-start.6 = ((f32[128,1,4608]{2,1,0:T(1,128)}), f32[128,1,4608]{2,1,0:T(1,128)}, u32[]{:S(2)}, u32[]{:S(2)}) async-start(f32[128,1,4608]{2,1,0:T(1,128)} %bitcast.129), calls=%async_computation.6 | async-start | bytes 4718592 | tf_op jit(solution)/shard_map/all_to_all | solution.py:16
  298.9 12.9 %all-to-all-start.5 = ((f32[4,1,32768]{2,1,0:T(1,128)}), f32[4,1,32768]{2,1,0:T(1,128)S(1)}, u32[]{:S(2)}, u32[]{:S(2)}) async-start(f32[4,1,32768]{2,1,0:T(1,128)} %broadcast_in_dim.19), calls=%async_computation.5 | async-start | bytes 1048576 | tf_op jit(solution)/shard_map/all_to_all | solution.py:19
  314.4 9.7 %copy-start.6 = (bf16[256,256]{1,0:T(8,128)(2,1)S(1)}, bf16[256,256]{1,0:T(8,128)(2,1)}, u32[]{:S(2)}) copy-start(bf16[256,256]{1,0:T(8,128)(2,1)} %param.17) | copy-start | bytes 393220
  314.4 10.7 %copy-start.5 = (bf16[512,256]{1,0:T(8,128)(2,1)S(1)}, bf16[512,256]{1,0:T(8,128)(2,1)}, u32[]{:S(2)}) copy-start(bf16[512,256]{1,0:T(8,128)(2,1)} %param.25) | copy-start | bytes 786436
  314.4 39.4 %all-to-all-start.7 = ((f32[128,1,4608]{2,1,0:T(1,128)}), f32[128,1,4608]{2,1,0:T(1,128)}, u32[]{:S(2)}, u32[]{:S(2)}) async-start(f32[128,1,4608]{2,1,0:T(1,128)} %broadcast_in_dim.20), calls=%async_computation.7 | async-start | bytes 4718592 | tf_op jit(solution)/shard_map/all_to_all | solution.py:19
where the time goes:
time: 374 us; the launch traced here: 369 us
  waiting for transfers between devices  139 us (37%)
  local copies, waits for them, and re-layouts  81.7 us (22%)
  starting transfers between devices  62.9 us (17%)
  matrix products  62 us (17%)
  other arithmetic  21.6 us (6%)
    all_to_all x1, waiting for transfers between devices, on_device(): lax.all_to_all(slot_grads.astype(SLOT_GRAD_LINK_DTYPE).reshape(row_device...  67 us
    all_to_all x3, waiting for transfers between devices, a2a_psum(): gathered = lax.all_to_all(spread_out, axes, 0, 0, tiled=True)  37.8 us
    all_to_all x3, waiting for transfers between devices, a2a_psum(): pieces = lax.all_to_all(flat, axes, 0, 0, tiled=True)  33.3 us
    all_to_all x3, starting transfers between devices, a2a_psum(): pieces = lax.all_to_all(flat, axes, 0, 0, tiled=True)  33.2 us
    while x3, local copies, waits for them, and re-layouts  18.2 us
    dot_general x1, matrix products, backward_step(): lax.dot_general(slot_hot, backward_term.reshape(step_tiles, -1), contract...  14 us
    all_to_all x3, starting transfers between devices, a2a_psum(): gathered = lax.all_to_all(spread_out, axes, 0, 0, tiled=True)  12.9 us
    reshape x1, local copies, waits for them, and re-layouts, on_device(): returned.astype(jnp.float32).reshape(total_slots, -1)  10.8 us
  transfers between devices with their start and end apart: 8, of which 7 were waited for; matrix products, arithmetic and copies ran while one was open for 35% of the time, Pallas kernels for 0%

commit v1 on v0

--- a/solution.py
+++ b/solution.py
@@ -5,7 +5,7 @@
 from jax import lax
 from jax.sharding import PartitionSpec as P
 
-SLOT_GRAD_LINK_DTYPE = jnp.float32
+SLOT_GRAD_LINK_DTYPE = jnp.bfloat16
 
 
 def a2a_psum(value, axes):

time: 374 us -> 303 us (0.81)
  waiting for transfers between devices: 139 us -> 85.9 us
  starting transfers between devices: 62.9 us -> 48.6 us
  local copies, waits for them, and re-layouts: 81.7 us -> 75.2 us
  other arithmetic: 21.6 us -> 27.4 us
    all_to_all x1, waiting for transfers between devices: 67 us -> 13.8 us  [on_device(): lax.all_to_all(slot_grads.astype(SLOT_GRAD_LINK_DTYPE).reshape(row_device...]
    all_to_all x3, starting transfers between devices: 33.2 us -> 18.7 us  [a2a_psum(): pieces = lax.all_to_all(flat, axes, 0, 0, tiled=True)]
    convert_element_type x0 -> x1, other arithmetic: none -> 5.74 us  [on_device(): slot_grads.astype(SLOT_GRAD_LINK_DTYPE)]
  transfers between devices with their start and end apart: 8 -> 8, of which waited for: 7 -> 6; matrix products, arithmetic and copies ran while one was open for 35% -> 40% of each run, Pallas kernels for 0% -> 0%
where the time goes in v1:
time: 303 us; the launch traced here: 298 us
  waiting for transfers between devices  85.9 us (28%)
  local copies, waits for them, and re-layouts  75.2 us (25%)
  matrix products  58.7 us (19%)
  starting transfers between devices  48.6 us (16%)
  other arithmetic  27.4 us (9%)
    all_to_all x3, waiting for transfers between devices, a2a_psum(): gathered = lax.all_to_all(spread_out, axes, 0, 0, tiled=True)  37.9 us
    all_to_all x3, waiting for transfers between devices, a2a_psum(): pieces = lax.all_to_all(flat, axes, 0, 0, tiled=True)  34.1 us
    all_to_all x3, starting transfers between devices, a2a_psum(): pieces = lax.all_to_all(flat, axes, 0, 0, tiled=True)  18.7 us
    while x3, local copies, waits for them, and re-layouts  18.2 us
    dot_general x1, matrix products, backward_step(): lax.dot_general(slot_hot, backward_term.reshape(step_tiles, -1), contract...  14 us
    all_to_all x1, waiting for transfers between devices, on_device(): lax.all_to_all(slot_grads.astype(SLOT_GRAD_LINK_DTYPE).reshape(row_device...  13.8 us
    all_to_all x3, starting transfers between devices, a2a_psum(): gathered = lax.all_to_all(spread_out, axes, 0, 0, tiled=True)  12.7 us
    all_to_all x3, other arithmetic, a2a_psum(): gathered = lax.all_to_all(spread_out, axes, 0, 0, tiled=True)  10.3 us
  transfers between devices with their start and end apart: 8, of which 6 were waited for; matrix products, arithmetic and copies ran while one was open for 40% of the time, Pallas kernels for 0%

profile of v1, /device:TPU:1, one launch (start us, length us, event | category | flops | bytes accessed | tf_op | source)
XLA Modules:
  0.0 298.5 jit_solution(10253159790060920928)
XLA Ops:
  1.6 3.7 %gather_fusion = bf16[64,128,256]{2,1,0:T(8,128)(2,1)} fusion(bf16[4,128,256]{2,1,0:T(8,128)(2,1)} %bitcast.127, s32[1024]{0:T(1024)S(1)} %pad_clamp_fusion.1), kind=kCustom, calls=%fused_computation | custom fusion | bytes 8388864 | tf_op jit(solution)/shard_map/gather | solution.py:68
  5.3 9.6 %all-to-all-start = ((bf16[32,2,128,256]{3,2,1,0:T(8,128)(2,1)}), bf16[32,2,128,256]{3,2,1,0:T(8,128)(2,1)}, u32[]{:S(2)}, u32[]{:S(2)}) async-start(bf16[32,2,128,256]{3,2,1,0:T(8,128)(2,1)} %bitcast.128), calls=%async_computation | async-start | bytes 8388608 | tf_op jit(solution)/shard_map/all_to_all | solution.py:69
  18.3 5.5 %copy.65 = f32[4,8,128,256]{3,1,2,0:T(8,128)} copy(f32[4,8,128,256]{2,3,0,1:T(8,128)} %convolution_bitcast_fusion.2) | data formatting | bytes 8388608
  24.1 3.9 %broadcast_in_dim.16 = f32[64,32768]{1,0:T(8,128)} broadcast(f32[]{:T(128)} %constant.58.clone.1), dimensions={} | broadcast | bytes 8388612 | tf_op jit(solution)/shard_map/broadcast_in_dim | solution.py:88
  28.0 38.6 %while.24 = (s32[]{:T(128)}, f32[64,32768]{1,0:T(8,128)}, s32[]{:T(128)}, s32[1,1,64]{2,1,0:T(1,128)S(1)}, s32[1,1,64]{2,1,0:T(1,128)S(1)}, /*index=5*/s32[]{:T(...) while((s32[]{:T(128)}, f32[64,32768]{1,0:T(8,128)}, ...), condition=%wide.region_1.2_spmd, body=%wide.region_0.1_spmd.sunk | while | flops 2956991232 | bytes 73405576 | solution.py:89
  29.2 8.6 %convolution_convert_fusion.2 = bf16[64,32768]{1,0:T(8,128)(2,1)S(1)} fusion(f32[32,32768]{1,0:T(8,128)} %get-tuple-element.418, f32[64,8]{0,1:T(8,128)S(1)} %get-tuple-element.417, f32[64,4]{0,1:T(4,128)S(1)} %fusion.65), kind=kOutput, calls=%fused_computation.3.clone.1 | convolution fusion | flops 807405568 | bytes 8391680 | tf_op jit(solution)/shard_map/while/body/dot_general | solution.py:78
  38.8 4.6 %convolution_bitcast_fusion.4 = f32[64,128,256]{1,2,0:T(8,128)} fusion(bf16[64,128,256]{2,1,0:T(8,128)(2,1)S(1)} %bitcast.121, bf16[64,128,128]{2,1,0:T(8,128)(2,1)S(1)} %get-tuple-element.419), kind=kOutput, calls=%fused_computation.4.clone.1 | convolution fusion | flops 536870912 | bytes 14680064 | tf_op jit(solution)/shard_map/while/body/tij,tif->tjf/dot_general | solution.py:80
  43.4 9.2 %copy.82 = f32[8,8,128,256]{3,1,2,0:T(8,128)} copy(f32[8,8,128,256]{2,3,1,0:T(8,128)} %bitcast.119) | data formatting | bytes 16777216 | tf_op jit(solution)/shard_map/while
  52.6 14.0 %convolution_add_fusion.6 = f32[64,32768]{1,0:T(8,128)} fusion(f32[64,32768]{1,0:T(8,128)} %get-tuple-element.401, f32[64,32768]{1,0:T(8,128)} %bitcast.118, s32[64]{0:T(128)S(1)} %bitcast.138), kind=kOutput, calls=%fused_computation.2.clone.1 | convolution fusion | flops 1612713984 | bytes 25166080 | tf_op jit(solution)/shard_map/while/body/dot_general | solution.py:84
  68.4 5.7 %convert_element_type.38 = bf16[64,32768]{1,0:T(8,128)(2,1)} convert(f32[64,32768]{1,0:T(8,128)} %get-tuple-element.242) | non-fusion elementwise | flops 2097152 | bytes 12582912 | tf_op jit(solution)/shard_map/convert_element_type | solution.py:93
  74.2 7.7 %reshape.280 = bf16[32,2,32768]{2,1,0:T(2,128)(2,1)} reshape(bf16[64,32768]{1,0:T(8,128)(2,1)} %convert_element_type.38) | data formatting | bytes 8388608 | tf_op jit(solution)/shard_map/reshape | solution.py:93
  81.8 7.6 %all-to-all-start.1 = ((bf16[32,2,32768]{2,1,0:T(2,128)(2,1)}), bf16[32,2,32768]{2,1,0:T(2,128)(2,1)}, u32[]{:S(2)}, u32[]{:S(2)}) async-start(bf16[32,2,32768]{2,1,0:T(2,128)(2,1)} %reshape.280), calls=%async_computation.1 | async-start | bytes 8388608 | tf_op jit(solution)/shard_map/all_to_all | solution.py:92
  89.4 4.9 %gather_fusion.1 = bf16[64,128,256]{2,1,0:T(8,128)(2,1)} fusion(bf16[64,128,256]{2,1,0:T(8,128)(2,1)} %bitcast.17, s32[1024]{0:T(1024)S(1)} %pad_clamp_fusion), kind=kCustom, calls=%fused_computation.1 | custom fusion | bytes 8388864 | tf_op jit(solution)/shard_map/while/body/gather | solution.py:106
  96.6 20.9 %while.25 = (s32[]{:T(128)}, f32[32,32768]{1,0:T(8,128)}, s32[]{:T(128)}, s32[1,1,64]{2,1,0:T(1,128)S(1)}, s32[]{:T(128)}, /*index=5*/f32[64,8]{0,1:T(8,128)S(1)...) while((s32[]{:T(128)}, f32[32,32768]{1,0:T(8,128)}, s32[]{:T(128)}, ...), condition=%wide.region_3.4_spmd, body=%wide.region_2.3_spmd.sunk | while | flops 1343228672 | bytes 48239488 | solution.py:116
  96.6 3.4 %fusion.70 = f32[64,128,256]{2,1,0:T(8,128)S(1)} fusion(bf16[64,128,128]{2,1,0:T(8,128)(2,1)S(1)} %get-tuple-element.448, bf16[64,128,256]{2,1,0:T(8,128)(2,1)} %get-tuple-element.449), kind=kOutput, calls=%fused_computation.50.clone.1 | convolution fusion | flops 536870912 | bytes 14680064 | tf_op jit(solution)/shard_map/while/body/tij,tjf->tif/dot_general | solution.py:107
  100.0 7.9 %copy.83 = f32[8,8,128,256]{3,1,2,0:T(8,128)} copy(f32[8,8,128,256]{3,2,1,0:T(8,128)S(1)} %bitcast.120) | data formatting | bytes 16777216 | tf_op jit(solution)/shard_map/while
  108.7 8.4 %convolution_add_fusion.7 = f32[32,32768]{1,0:T(8,128)} fusion(f32[32,32768]{1,0:T(8,128)} %get-tuple-element.433, f32[64,32768]{1,0:T(8,128)} %bitcast.117, f32[64,8]{0,1:T(8,128)S(1)} %get-tuple-element.447, f32[64,4]{0,1:T(4,128)S(1)} %fusion.71), kind=kOutput, calls=%fused_computation.14.clone.1 | convolution fusion | flops 806356992 | bytes 16780288 | tf_op jit(solution)/shard_map/while/body/dot_general | solution.py:111
  117.5 6.4 %fusion.15 = f32[8,256,256]{2,1,0:T(8,128)S(1)} fusion(bf16[4,128,256,1]{2,1,0,3:T(8,128)(2,1)} %bitcast.132, f32[4,8,128,256]{3,1,2,0:T(8,128)} %bitcast.123), kind=kOutput, calls=%fused_computation.29 | convolution fusion | flops 3221225472 | bytes 6553600 | tf_op jit(solution)/shard_map/lbnf,lng->bfg/dot_general | solution.py:130
  123.9 3.8 %fusion.18 = f32[4,128,256]{2,1,0:T(8,128)} fusion(f32[4,8,128,256]{3,1,2,0:T(8,128)S(1)} %bitcast.124, bf16[8,256,256]{2,1,0:T(8,128)(2,1)S(1)} %copy-done), kind=kOutput, calls=%fused_computation.30 | convolution fusion | flops 3221225472 | bytes 5767168 | tf_op jit(solution)/shard_map/lbnf,bfg->lng/dot_general | solution.py:129
  127.7 13.8 %all-to-all-done.1 = bf16[32,2,32768]{2,1,0:T(2,128)(2,1)} async-done(((bf16[32,2,32768]{2,1,0:T(2,128)(2,1)}), bf16[32,2,32768]{2,1,0:T(2,128)(2,1)}, u32[]{:S(2)}, u32[]{:S(2)}) %all-to-all-start.1) | async-done | bytes 4194336 | tf_op jit(solution)/shard_map/all_to_all | solution.py:92
  143.9 4.2 %all-to-all-start.2 = ((f32[4,1,32768]{2,1,0:T(1,128)}), f32[4,1,32768]{2,1,0:T(1,128)}, u32[]{:S(2)}, u32[]{:S(2)}) async-start(f32[4,1,32768]{2,1,0:T(1,128)} %all_to_all.47), calls=%async_computation.2 | async-start | bytes 1048576 | tf_op jit(solution)/shard_map/all_to_all | solution.py:16
  148.3 7.2 %reshape.284 = bf16[64,32768]{1,0:T(8,128)(2,1)} reshape(bf16[32,2,32768]{2,1,0:T(2,128)(2,1)} %all-to-all-done.1) | data formatting | bytes 8388608 | tf_op jit(solution)/shard_map/reshape | solution.py:146
  159.7 4.2 %all-to-all-start.4 = ((f32[4,1,32768]{2,1,0:T(1,128)}), f32[4,1,32768]{2,1,0:T(1,128)}, u32[]{:S(2)}, u32[]{:S(2)}) async-start(f32[4,1,32768]{2,1,0:T(1,128)} %copy.55), calls=%async_computation.4 | async-start | bytes 1048576 | tf_op jit(solution)/shard_map/all_to_all | solution.py:16
  172.9 3.6 %all-to-all-start.3 = ((f32[4,1,32768]{2,1,0:T(1,128)}), f32[4,1,32768]{2,1,0:T(1,128)S(1)}, u32[]{:S(2)}, u32[]{:S(2)}) async-start(f32[4,1,32768]{2,1,0:T(1,128)} %broadcast_in_dim.18), calls=%async_computation.3 | async-start | bytes 1048576 | tf_op jit(solution)/shard_map/all_to_all | solution.py:19
  179.8 3.6 %all-to-all-done.3 = f32[4,1,32768]{2,1,0:T(1,128)S(1)} async-done(((f32[4,1,32768]{2,1,0:T(1,128)}), f32[4,1,32768]{2,1,0:T(1,128)S(1)}, u32[]{:S(2)}, u32[]{:S(2)}) %all-to-all-start.3) | async-done | bytes 524320 | tf_op jit(solution)/shard_map/all_to_all | solution.py:19
  183.4 10.3 %all-to-all-start.6 = ((f32[128,1,4608]{2,1,0:T(1,128)}), f32[128,1,4608]{2,1,0:T(1,128)}, u32[]{:S(2)}, u32[]{:S(2)}) async-start(f32[128,1,4608]{2,1,0:T(1,128)} %bitcast.129), calls=%async_computation.6 | async-start | bytes 4718592 | tf_op jit(solution)/shard_map/all_to_all | solution.py:16
  195.3 31.9 %all-to-all-done.6 = f32[128,1,4608]{2,1,0:T(1,128)} async-done(((f32[128,1,4608]{2,1,0:T(1,128)}), f32[128,1,4608]{2,1,0:T(1,128)}, u32[]{:S(2)}, u32[]{:S(2)}) %all-to-all-start.6) | async-done | bytes 2359328 | tf_op jit(solution)/shard_map/all_to_all | solution.py:16
  228.3 3.5 %all-to-all-start.5 = ((f32[4,1,32768]{2,1,0:T(1,128)}), f32[4,1,32768]{2,1,0:T(1,128)S(1)}, u32[]{:S(2)}, u32[]{:S(2)}) async-start(f32[4,1,32768]{2,1,0:T(1,128)} %broadcast_in_dim.19), calls=%async_computation.5 | async-start | bytes 1048576 | tf_op jit(solution)/shard_map/all_to_all | solution.py:19
  234.7 6.4 %all-to-all-done.5 = f32[4,1,32768]{2,1,0:T(1,128)S(1)} async-done(((f32[4,1,32768]{2,1,0:T(1,128)}), f32[4,1,32768]{2,1,0:T(1,128)S(1)}, u32[]{:S(2)}, u32[]{:S(2)}) %all-to-all-start.5) | async-done | bytes 524320 | tf_op jit(solution)/shard_map/all_to_all | solution.py:19
  243.8 5.6 %all-to-all-start.7 = ((f32[128,1,4608]{2,1,0:T(1,128)}), f32[128,1,4608]{2,1,0:T(1,128)}, u32[]{:S(2)}, u32[]{:S(2)}) async-start(f32[128,1,4608]{2,1,0:T(1,128)} %broadcast_in_dim.20), calls=%async_computation.7 | async-start | bytes 4718592 | tf_op jit(solution)/shard_map/all_to_all | solution.py:19
  255.1 27.9 %all-to-all-done.7 = f32[128,1,4608]{2,1,0:T(1,128)} async-done(((f32[128,1,4608]{2,1,0:T(1,128)}), f32[128,1,4608]{2,1,0:T(1,128)}, u32[]{:S(2)}, u32[]{:S(2)}) %all-to-all-start.7) | async-done | bytes 2359328 | tf_op jit(solution)/shard_map/all_to_all | solution.py:19
  283.0 7.3 %reduce.5 = f32[128,4608]{1,0:T(8,128)S(1)} reduce(f32[128,1,4608]{2,1,0:T(1,128)} %all-to-all-done.7, f32[]{:T(128)} %constant.73), dimensions={1}, to_apply=%all_to_all.46.reduce_sub_computation | reduce | bytes 4718596 | tf_op jit(solution)/shard_map/all_to_all | solution.py:19
  (66 shorter events, 51.2 us)
Async XLA Ops:
  0.6 15.0 %copy-start = (bf16[8,256,256]{2,1,0:T(8,128)(2,1)S(1)}, bf16[8,256,256]{2,1,0:T(8,128)(2,1)}, u32[]{:S(2)}) copy-start(bf16[8,256,256]{2,1,0:T(8,128)(2,1)} %param.16) | copy-start | bytes 3145732
  5.3 10.3 %copy-start.4 = (bf16[512,256]{1,0:T(8,128)(2,1)S(1)}, bf16[512,256]{1,0:T(8,128)(2,1)}, u32[]{:S(2)}) copy-start(bf16[512,256]{1,0:T(8,128)(2,1)} %param.25) | copy-start | bytes 786436
  5.3 63.1 %all-to-all-start = ((bf16[32,2,128,256]{3,2,1,0:T(8,128)(2,1)}), bf16[32,2,128,256]{3,2,1,0:T(8,128)(2,1)}, u32[]{:S(2)}, u32[]{:S(2)}) async-start(bf16[32,2,128,256]{3,2,1,0:T(8,128)(2,1)} %bitcast.128), calls=%async_computation | async-start | bytes 8388608 | tf_op jit(solution)/shard_map/all_to_all | solution.py:69
  18.3 5.5 %copy-start.10 = (f32[200,8]{0,1:T(8,128)S(1)}, f32[200,8]{0,1:T(8,128)}, u32[]{:S(2)}) copy-start(f32[200,8]{0,1:T(8,128)} %param.18) | copy-start | bytes 19204
  18.3 5.5 %copy-start.11 = (s32[1,1,64]{2,1,0:T(1,128)S(1)}, s32[1,1,64]{2,1,0:T(1,128)}, u32[]{:S(2)}) copy-start(s32[1,1,64]{2,1,0:T(1,128)} %param.22) | copy-start | bytes 772
  24.1 3.9 %copy-start.2 = (bf16[1,1,64,128,128]{4,3,2,1,0:T(8,128)(2,1)S(1)}, bf16[1,1,64,128,128]{4,3,2,1,0:T(8,128)(2,1)}, u32[]{:S(2)}) copy-start(bf16[1,1,64,128,128]{4,3,2,1,0:T(8,128)(2,1)} %param.19) | copy-start | bytes 6291460
  24.1 3.9 %copy-start.7 = (s32[1,1,64]{2,1,0:T(1,128)S(1)}, s32[1,1,64]{2,1,0:T(1,128)}, u32[]{:S(2)}) copy-start(s32[1,1,64]{2,1,0:T(1,128)} %param.20) | copy-start | bytes 772
  24.1 3.9 %copy-start.8 = (s32[1,1,64]{2,1,0:T(1,128)S(1)}, s32[1,1,64]{2,1,0:T(1,128)}, u32[]{:S(2)}) copy-start(s32[1,1,64]{2,1,0:T(1,128)} %param.21) | copy-start | bytes 772
  28.0 38.7 %copy-start.3 = (bf16[512,256]{1,0:T(8,128)(2,1)S(1)}, bf16[512,256]{1,0:T(8,128)(2,1)}, u32[]{:S(2)}) copy-start(bf16[512,256]{1,0:T(8,128)(2,1)} %param.15) | copy-start | bytes 786436
  81.8 59.7 %all-to-all-start.1 = ((bf16[32,2,32768]{2,1,0:T(2,128)(2,1)}), bf16[32,2,32768]{2,1,0:T(2,128)(2,1)}, u32[]{:S(2)}, u32[]{:S(2)}) async-start(bf16[32,2,32768]{2,1,0:T(2,128)(2,1)} %reshape.280), calls=%async_computation.1 | async-start | bytes 8388608 | tf_op jit(solution)/shard_map/all_to_all | solution.py:92
  117.5 6.4 %copy-start.1 = (f32[32,32768]{1,0:T(8,128)S(1)}, f32[32,32768]{1,0:T(8,128)}, u32[]{:S(2)}) copy-start(f32[32,32768]{1,0:T(8,128)} %get-tuple-element.244) | copy-start | bytes 12582916
  123.9 24.2 %copy-start.9 = (s32[1,1,32,2]{2,3,1,0:T(2,128)S(1)}, s32[1,1,32,2]{2,3,1,0:T(2,128)}, u32[]{:S(2)}) copy-start(s32[1,1,32,2]{2,3,1,0:T(2,128)} %param.24) | copy-start | bytes 772
  143.9 15.8 %all-to-all-start.2 = ((f32[4,1,32768]{2,1,0:T(1,128)}), f32[4,1,32768]{2,1,0:T(1,128)}, u32[]{:S(2)}, u32[]{:S(2)}) async-start(f32[4,1,32768]{2,1,0:T(1,128)} %all_to_all.47), calls=%async_computation.2 | async-start | bytes 1048576 | tf_op jit(solution)/shard_map/all_to_all | solution.py:16
  159.7 12.1 %all-to-all-start.4 = ((f32[4,1,32768]{2,1,0:T(1,128)}), f32[4,1,32768]{2,1,0:T(1,128)}, u32[]{:S(2)}, u32[]{:S(2)}) async-start(f32[4,1,32768]{2,1,0:T(1,128)} %copy.55), calls=%async_computation.4 | async-start | bytes 1048576 | tf_op jit(solution)/shard_map/all_to_all | solution.py:16
  172.9 10.5 %all-to-all-start.3 = ((f32[4,1,32768]{2,1,0:T(1,128)}), f32[4,1,32768]{2,1,0:T(1,128)S(1)}, u32[]{:S(2)}, u32[]{:S(2)}) async-start(f32[4,1,32768]{2,1,0:T(1,128)} %broadcast_in_dim.18), calls=%async_computation.3 | async-start | bytes 1048576 | tf_op jit(solution)/shard_map/all_to_all | solution.py:19
  183.4 43.8 %all-to-all-start.6 = ((f32[128,1,4608]{2,1,0:T(1,128)}), f32[128,1,4608]{2,1,0:T(1,128)}, u32[]{:S(2)}, u32[]{:S(2)}) async-start(f32[128,1,4608]{2,1,0:T(1,128)} %bitcast.129), calls=%async_computation.6 | async-start | bytes 4718592 | tf_op jit(solution)/shard_map/all_to_all | solution.py:16
  228.3 12.9 %all-to-all-start.5 = ((f32[4,1,32768]{2,1,0:T(1,128)}), f32[4,1,32768]{2,1,0:T(1,128)S(1)}, u32[]{:S(2)}, u32[]{:S(2)}) async-start(f32[4,1,32768]{2,1,0:T(1,128)} %broadcast_in_dim.19), calls=%async_computation.5 | async-start | bytes 1048576 | tf_op jit(solution)/shard_map/all_to_all | solution.py:19
  243.8 9.3 %copy-start.6 = (bf16[256,256]{1,0:T(8,128)(2,1)S(1)}, bf16[256,256]{1,0:T(8,128)(2,1)}, u32[]{:S(2)}) copy-start(bf16[256,256]{1,0:T(8,128)(2,1)} %param.17) | copy-start | bytes 393220
  243.8 10.3 %copy-start.5 = (bf16[512,256]{1,0:T(8,128)(2,1)S(1)}, bf16[512,256]{1,0:T(8,128)(2,1)}, u32[]{:S(2)}) copy-start(bf16[512,256]{1,0:T(8,128)(2,1)} %param.25) | copy-start | bytes 786436
  243.8 39.2 %all-to-all-start.7 = ((f32[128,1,4608]{2,1,0:T(1,128)}), f32[128,1,4608]{2,1,0:T(1,128)}, u32[]{:S(2)}, u32[]{:S(2)}) async-start(f32[128,1,4608]{2,1,0:T(1,128)} %broadcast_in_dim.20), calls=%async_computation.7 | async-start | bytes 4718592 | tf_op jit(solution)/shard_map/all_to_all | solution.py:19

commit v2 on v1

--- a/solution.py
+++ b/solution.py
@@ -12,11 +12,10 @@
     count = 1
     for name in axes:
         count *= lax.axis_size(name)
-    flat = value.reshape(count, -1)
-    pieces = lax.all_to_all(flat, axes, 0, 0, tiled=True)
+    chunked = value.reshape((count, value.shape[0] // count) + value.shape[1:])
+    pieces = lax.all_to_all(chunked, axes, 0, 0, tiled=True)
     reduced = jnp.sum(pieces, axis=0, keepdims=True)
-    spread_out = jnp.broadcast_to(reduced, flat.shape)
-    gathered = lax.all_to_all(spread_out, axes, 0, 0, tiled=True)
+    gathered = lax.all_to_all(jnp.broadcast_to(reduced, chunked.shape), axes, 0, 0, tiled=True)
     return gathered.reshape(value.shape)
 
 
@@ -70,28 +69,29 @@
 
     cot_blocks = cotangent.reshape(local_blocks, size_block, feat_width)
     agg_grad = jnp.einsum("lng,bfg->lbnf", cot_blocks, bases, preferred_element_type=jnp.float32)
-    agg_grad = agg_grad.reshape(local_blocks * num_bases, size_block * feat_width)
+    agg_grad = agg_grad.reshape(local_blocks * num_bases, size_block, feat_width)
 
     def backward_step(block_index, running):
         first_tile = block_index * step_tiles
         weights = tile_weights(first_tile)
-        spread = jnp.dot(weights, agg_grad, precision=highest).astype(jnp.bfloat16)
-        spread = spread.reshape(step_tiles, size_block, feat_width)
+        spread = lax.dot_general(
+            weights, agg_grad, (((1,), (0,)), ((), ())), precision=highest
+        ).astype(jnp.bfloat16)
         backward_term = jnp.einsum(
             "tij,tif->tjf", adjacency, spread, preferred_element_type=jnp.float32
         )
         slot_hot = (src_ids[:, None] == jnp.arange(total_slots)[None, :]).astype(jnp.float32)
         return running + lax.dot_general(
-            slot_hot, backward_term.reshape(step_tiles, -1), contract_first, precision=highest
+            slot_hot, backward_term, contract_first, precision=highest
         )
 
-    slot_zero = jnp.zeros((total_slots, size_block * feat_width), jnp.float32)
+    slot_zero = jnp.zeros((total_slots, size_block, feat_width), jnp.float32)
     slot_grads = lax.fori_loop(0, steps_live, backward_step, slot_zero)
     incoming, slot_grads = lax.optimization_barrier((incoming, slot_grads))
 
     returned = lax.all_to_all(
         slot_grads.astype(SLOT_GRAD_LINK_DTYPE).reshape(
-            row_devices, slots_peer, size_block * feat_width
+            row_devices, slots_peer * size_block, feat_width
         ),
         "rows",
         split_axis=0,
@@ -109,43 +109,41 @@
         )
         weights = tile_weights(first_tile)
         return running + lax.dot_general(
-            weights, messages.reshape(step_tiles, -1), contract_first, precision=highest
+            weights, messages, contract_first, precision=highest
         )
 
-    zero_total = jnp.zeros((local_blocks * num_bases, size_block * feat_width), jnp.float32)
+    zero_total = jnp.zeros((local_blocks * num_bases, size_block, feat_width), jnp.float32)
     partial_value = lax.fori_loop(0, steps_live, forward_step, zero_total)
     partial_value = partial_value.reshape(local_blocks, num_bases, size_block, feat_width)
     basis_f32 = bases.astype(jnp.float32)
     cot_f32 = cot_blocks.astype(jnp.float32)
     root_term = jnp.dot(features, root, preferred_element_type=jnp.float32)
-    rel_devices = lax.axis_size("rel")
-    part_rows = features.shape[0] // rel_devices
-    first_row = lax.axis_index("rel") * part_rows
-    feat_part = lax.dynamic_slice_in_dim(features, first_row, part_rows)
-    cot_part = lax.dynamic_slice_in_dim(cotangent, first_row, part_rows)
     root_local = lax.dot_general(
-        feat_part, cot_part, contract_first, preferred_element_type=jnp.float32
+        features, cotangent, contract_first, preferred_element_type=jnp.float32
     )
     projected_part = jnp.einsum("lbnf,bfg->lng", partial_value, basis_f32, precision=highest)
     basis_local = jnp.einsum("lbnf,lng->bfg", partial_value, cot_f32, precision=highest)
-    returned, projected_part, basis_local, root_local = lax.optimization_barrier(
-        (returned, projected_part, basis_local, root_local)
+    projected = lax.psum(projected_part, "rel")
+    root_grad = lax.psum(root_local, "rows")
+    returned, basis_local, projected, root_grad = lax.optimization_barrier(
+        (returned, basis_local, projected, root_grad)
     )
 
-    projected = a2a_psum(projected_part, ("rel",))
     output = (projected.reshape(-1, feat_width) + root_term).astype(jnp.bfloat16)
-    grads_flat = jnp.concatenate([basis_local.reshape(-1), root_local.reshape(-1)])
-    grads_flat = a2a_psum(grads_flat, ("rows", "rel"))
-    basis_grad = grads_flat[: basis_local.size].reshape(basis_local.shape)
-    root_grad = grads_flat[basis_local.size :].reshape(root_local.shape)
+    basis_grad = a2a_psum(
+        basis_local.reshape(-1, basis_local.shape[-1]), ("rows", "rel")
+    ).reshape(basis_local.shape)
 
     block_hot = (send_rows.reshape(-1)[None, :] == jnp.arange(local_blocks)[:, None]).astype(
         jnp.float32
     )
-    own_grads = jnp.dot(
-        block_hot, returned.astype(jnp.float32).reshape(total_slots, -1), precision=highest
+    own_grads = lax.dot_general(
+        block_hot,
+        returned.astype(jnp.float32).reshape(total_slots, size_block, feat_width),
+        (((1,), (0,)), ((), ())),
+        precision=highest,
     )
-    summed = a2a_psum(own_grads, ("rel",))
+    summed = a2a_psum(own_grads.reshape(-1, feat_width), ("rel",))
     root_back = lax.dot_general(
         cotangent, root, (((1,), (1,)), ((), ())), preferred_element_type=jnp.float32
     )

time: 303 us -> 338 us (1.12)
  waiting for transfers between devices: 85.9 us -> 142 us
  other arithmetic: 27.4 us -> 3.37 us
  local copies, waits for them, and re-layouts: 75.2 us -> 51.5 us
  matrix products: 58.7 us -> 72.7 us
  between operations: 1.7 us -> 15.2 us
  starting transfers between devices: 48.6 us -> 36.9 us
  blocking collectives: 0 us -> 10.3 us
    psum x0 -> x2, waiting for transfers between devices: none -> 75.8 us  [the longest x1 43.3 us: on_device(): projected = lax.psum(projected_part, 'rel')]
    reshape x3 -> x0, local copies, waits for them, and re-layouts: 15.2 us -> none  [the longest x1 7.66 us: on_device(): slot_grads.astype(SLOT_GRAD_LINK_DTYPE)]
    all_to_all x1, waiting for transfers between devices: 13.8 us -> 0.01 us  [on_device(): lax.all_to_all(slot_grads.astype(SLOT_GRAD_LINK_DTYPE).reshape(row_device...]
    all_to_all x6 -> x3, starting transfers between devices: 31.4 us -> 19.8 us  [the longest x1 11.2 us: a2a_psum(): pieces = lax.all_to_all(chunked, axes, 0, 0, tiled=True)]
    while x3 -> x1, local copies, waits for them, and re-layouts: 18.2 us -> 6.72 us  [on_device(): slot_grads = lax.fori_loop(0, steps_live, backward_step, slot_zero)]
    all_to_all x0 -> x1, blocking collectives: none -> 10.3 us  [a2a_psum(): pieces = lax.all_to_all(chunked, axes, 0, 0, tiled=True)]
    all_to_all x3 -> x0, other arithmetic: 10.3 us -> none  [a2a_psum(): gathered = lax.all_to_all(spread_out, axes, 0, 0, tiled=True)]
    optimization_barrier x0 -> x1, local copies, waits for them, and re-layouts: none -> 9.79 us  [on_device(): incoming, slot_grads = lax.optimization_barrier((incoming, slot_grads))]
  transfers between devices with their start and end apart: 8 -> 7, of which waited for: 6 -> 5; matrix products, arithmetic and copies ran while one was open for 40% -> 34% of each run, Pallas kernels for 0% -> 0%
where the time goes in v2:
time: 338 us; the launch traced here: 333 us
  waiting for transfers between devices  142 us (42%)
  matrix products  72.7 us (22%)
  local copies, waits for them, and re-layouts  51.5 us (15%)
  starting transfers between devices  36.9 us (11%)
  between operations  15.2 us (4%)
  blocking collectives  10.3 us (3%)
    psum x1, waiting for transfers between devices, on_device(): projected = lax.psum(projected_part, 'rel')  43.3 us
    all_to_all x2, waiting for transfers between devices, a2a_psum(): lax.all_to_all(jnp.broadcast_to(reduced, chunked.shape), axes, 0, 0, tile...  36.2 us
    psum x1, waiting for transfers between devices, on_device(): root_grad = lax.psum(root_local, 'rows')  32.5 us
    all_to_all x1, waiting for transfers between devices, a2a_psum(): pieces = lax.all_to_all(chunked, axes, 0, 0, tiled=True)  29.9 us
    dot_general x1, matrix products, backward_step(): lax.dot_general(slot_hot, backward_term, contract_first, precision=highest)  14.3 us
    all_to_all x1, starting transfers between devices, a2a_psum(): pieces = lax.all_to_all(chunked, axes, 0, 0, tiled=True)  11.2 us
    dot_general x1, matrix products, forward_step(): lax.dot_general(weights, messages, contract_first, precision=highest)  11 us
    all_to_all x1, blocking collectives, a2a_psum(): pieces = lax.all_to_all(chunked, axes, 0, 0, tiled=True)  10.3 us
  transfers between devices with their start and end apart: 7, of which 5 were waited for; matrix products, arithmetic and copies ran while one was open for 34% of the time, Pallas kernels for 0%

profile of v2, /device:TPU:1, one launch (start us, length us, event | category | flops | bytes accessed | tf_op | source)
XLA Modules:
  0.0 332.7 jit_solution(2039542238447856538)
XLA Ops:
  8.2 3.7 %gather_fusion = bf16[64,128,256]{2,1,0:T(8,128)(2,1)} fusion(bf16[4,128,256]{2,1,0:T(8,128)(2,1)} %bitcast.103, s32[1024]{0:T(1024)S(1)} %pad_clamp_fusion.1), kind=kCustom, calls=%fused_computation | custom fusion | bytes 8388864 | tf_op jit(solution)/shard_map/gather | solution.py:67
  11.9 9.6 %all-to-all-start = ((bf16[32,2,128,256]{3,2,1,0:T(8,128)(2,1)}), bf16[32,2,128,256]{3,2,1,0:T(8,128)(2,1)}, u32[]{:S(2)}, u32[]{:S(2)}) async-start(bf16[32,2,128,256]{3,2,1,0:T(8,128)(2,1)} %bitcast.105), calls=%async_computation | async-start | bytes 8388608 | tf_op jit(solution)/shard_map/all_to_all | solution.py:68
  23.2 2.7 convolution_bitcast_fusion
  26.0 5.3 %copy.31 = f32[4,8,128,256]{3,2,1,0:T(8,128)} copy(f32[4,8,128,256]{2,3,0,1:T(8,128)} %convolution_bitcast_fusion) | data formatting | bytes 8388608 | tf_op jit(solution)/shard_map/lng,bfg->lbnf/transpose | solution.py:71
  31.3 6.7 %copy.32 = f32[32,128,256]{2,0,1:T(8,128)} copy(f32[32,128,256]{2,1,0:T(8,128)} %bitcast.106) | data formatting | bytes 8388608 | tf_op jit(solution)/shard_map/while | solution.py:89
  38.3 4.3 %broadcast_in_dim.8 = f32[64,128,256]{2,0,1:T(8,128)} broadcast(f32[]{:T(128)} %constant.53.clone.1), dimensions={} | broadcast | bytes 8388612 | tf_op jit(solution)/shard_map/broadcast_in_dim | solution.py:88
  42.6 40.0 %while.24 = (s32[]{:T(128)}, f32[64,128,256]{2,0,1:T(8,128)}, s32[]{:T(128)}, s32[1,1,64]{2,1,0:T(1,128)S(1)}, s32[1,1,64]{2,1,0:T(1,128)S(1)}, /*index=5*/s32[]...) while((s32[]{:T(128)}, f32[64,128,256]{2,0,1:T(8,128)}, ...), condition=%wide.region_1.2_spmd, body=%wide.region_0.1_spmd.sunk | while | flops 2956991232 | bytes 65016960 | solution.py:89
  43.8 8.6 %convolution_convert_fusion.2 = bf16[64,128,256]{2,0,1:T(8,128)(2,1)S(1)} fusion(f32[32,128,256]{2,0,1:T(8,128)} %get-tuple-element.427, f32[64,8]{0,1:T(8,128)S(1)} %get-tuple-element.426, f32[64,4]{0,1:T(4,128)S(1)} %fusion.81), kind=kOutput, calls=%fused_computation.6.clone.1 | convolution fusion | flops 807405568 | bytes 8391680 | tf_op jit(solution)/shard_map/while/body/dot_general | solution.py:77
  52.4 6.6 %fusion.82 = f32[64,128,256]{1,2,0:T(8,128)} fusion(bf16[64,128,128]{2,1,0:T(8,128)(2,1)S(1)} %get-tuple-element.428, bf16[64,128,256]{2,0,1:T(8,128)(2,1)S(1)} %convolution_convert_fusion.2), kind=kOutput, calls=%fused_computation.5.clone.1 | convolution fusion | flops 536870912 | bytes 14680064 | tf_op jit(solution)/shard_map/while/body/tij,tif->tjf/dot_general | solution.py:80
  59.0 9.2 %copy.66 = f32[64,128,256]{2,0,1:T(8,128)} copy(f32[64,128,256]{1,2,0:T(8,128)} %fusion.82) | data formatting | bytes 16777216 | tf_op jit(solution)/shard_map/while/body/tij,tif->tjf/dot_general | solution.py:80
  68.1 14.3 %convolution_add_fusion.4 = f32[64,128,256]{2,0,1:T(8,128)} fusion(f32[64,128,256]{2,0,1:T(8,128)} %get-tuple-element.410, f32[64,128,256]{2,0,1:T(8,128)} %copy.66, s32[64]{0:T(128)S(1)} %bitcast.113), kind=kOutput, calls=%fused_computation.4.clone.1 | convolution fusion | flops 1612713984 | bytes 25166080 | tf_op jit(solution)/shard_map/while/body/dot_general | solution.py:84
  82.6 9.8 %copy.61 = bf16[64,128,256]{2,1,0:T(8,128)(2,1)} copy(f32[64,128,256]{2,0,1:T(8,128)} %get-tuple-element.242) | data formatting | bytes 12582912 | tf_op jit(solution)/shard_map/optimization_barrier | solution.py:90
  92.4 7.4 %all-to-all-start.1 = ((bf16[32,256,256]{2,1,0:T(8,128)(2,1)}), bf16[32,256,256]{2,1,0:T(8,128)(2,1)}, u32[]{:S(2)}, u32[]{:S(2)}) async-start(bf16[32,256,256]{2,1,0:T(8,128)(2,1)} %bitcast.104), calls=%async_computation.1 | async-start | bytes 8388608 | tf_op jit(solution)/shard_map/all_to_all | solution.py:92
  99.9 5.0 %gather_fusion.1 = bf16[64,128,256]{2,1,0:T(8,128)(2,1)} fusion(bf16[64,128,256]{2,1,0:T(8,128)(2,1)} %bitcast.22, s32[1024]{0:T(1024)S(1)} %pad_clamp_fusion), kind=kCustom, calls=%fused_computation.1 | custom fusion | bytes 8388864 | tf_op jit(solution)/shard_map/while/body/gather | solution.py:106
  104.8 2.4 broadcast_in_dim.15
  107.3 15.3 %while.25 = (s32[]{:T(128)}, f32[32,128,256]{2,0,1:T(8,128)}, s32[]{:T(128)}, s32[1,1,64]{2,1,0:T(1,128)S(1)}, s32[]{:T(128)}, /*index=5*/f32[64,8]{0,1:T(8,128)...) while((s32[]{:T(128)}, f32[32,128,256]{2,0,1:T(8,128)}, ...), condition=%wide.region_3.4_spmd, body=%wide.region_2.3_spmd.sunk | while | flops 1343228672 | bytes 31462264 | solution.py:116
  108.0 3.5 %fusion.87 = f32[64,128,256]{2,1,0:T(8,128)S(1)} fusion(bf16[64,128,128]{2,1,0:T(8,128)(2,1)S(1)} %get-tuple-element.457, bf16[64,128,256]{2,1,0:T(8,128)(2,1)} %get-tuple-element.458), kind=kOutput, calls=%fused_computation.53.clone.1 | convolution fusion | flops 536870912 | bytes 14680064 | tf_op jit(solution)/shard_map/while/body/tij,tjf->tif/dot_general | solution.py:107
  111.4 11.0 %fusion.89 = f32[32,128,256]{2,0,1:T(8,128)} fusion(f32[32,128,256]{2,0,1:T(8,128)} %get-tuple-element.442, f32[64,128,256]{2,1,0:T(8,128)S(1)} %fusion.87, f32[64,8]{0,1:T(8,128)S(1)} %get-tuple-element.456, f32[64,4]{0,1:T(4,128)S(1)} %fusion.88), kind=kOutput, calls=%fused_computation.19.clone.1 | convolution fusion | flops 806356992 | bytes 16780288 | tf_op jit(solution)/shard_map/while/body/dot_general | solution.py:111
  122.6 7.3 %fusion.32 = f32[4,128,256]{2,1,0:T(8,128)} fusion(f32[4,8,128,256]{3,1,0,2:T(8,128)} %bitcast.25, bf16[8,256,256]{2,1,0:T(8,128)(2,1)S(1)} %copy-done), kind=kOutput, calls=%fused_computation.36 | convolution fusion | flops 3221225472 | bytes 5767168 | tf_op jit(solution)/shard_map/lbnf,bfg->lng/dot_general | solution.py:124
  130.2 8.6 %fusion.29 = f32[8,256,256]{2,1,0:T(8,128)} fusion(bf16[4,128,256,1]{2,1,0,3:T(8,128)(2,1)S(1)} %bitcast.109, f32[4,8,128,256]{3,1,0,2:T(8,128)} %bitcast.25), kind=kOutput, calls=%fused_computation.35 | convolution fusion | flops 3221225472 | bytes 6553600 | tf_op jit(solution)/shard_map/lbnf,lng->bfg/dot_general | solution.py:125
  138.8 32.5 %all-reduce.5.cloned.1.call-done = f32[256,256]{1,0:T(8,128)} async-done(((f32[256,256]{1,0:T(8,128)}), f32[256,256]{1,0:T(8,128)}) %all-reduce.5.cloned.1.call-update) | async-done | bytes 262160 | tf_op jit(solution)/shard_map/psum | solution.py:127
  171.3 43.3 %all-reduce.3.cloned.1.call-done = f32[4,128,256]{2,1,0:T(8,128)} async-done(((f32[4,128,256]{2,1,0:T(8,128)}), f32[4,128,256]{2,1,0:T(8,128)}) %all-reduce.3.cloned.1.call-update) | async-done | bytes 524304 | tf_op jit(solution)/shard_map/psum | solution.py:126
  214.6 4.8 %fusion.23 = f32[4,128,256]{2,0,1:T(4,128)S(1)} fusion(bf16[64,128,256]{2,1,0:T(8,128)(2,1)} %bitcast.33, s32[64]{0:T(128)S(1)} %eq.116), kind=kOutput, calls=%fused_computation.28 | convolution fusion | flops 16777472 | bytes 4718848 | tf_op jit(solution)/shard_map/dot_general | solution.py:140
  219.5 10.3 %all_to_all.30 = f32[4,128,256]{2,1,0:T(8,128)} all-to-all(f32[4,128,256]{2,1,0:T(8,128)S(1)} %copy.38), channel_id=1, replica_groups=mesh['rows'=32,'rel'=4] {'rel'}, dimensions={0} | all-to-all | bytes 1048576 | tf_op jit(solution)/shard_map/all_to_all | solution.py:16
  229.8 11.2 %all-to-all-start.4 = ((f32[128,16,256]{2,1,0:T(8,128)}), f32[128,16,256]{2,1,0:T(8,128)S(1)}, u32[]{:S(2)}, u32[]{:S(2)}) async-start(f32[128,16,256]{2,1,0:T(8,128)} %bitcast.35), calls=%async_computation.4 | async-start | bytes 4194304 | tf_op jit(solution)/shard_map/all_to_all | solution.py:16
  242.1 29.9 %all-to-all-done.4 = f32[128,16,256]{2,1,0:T(8,128)S(1)} async-done(((f32[128,16,256]{2,1,0:T(8,128)}), f32[128,16,256]{2,1,0:T(8,128)S(1)}, u32[]{:S(2)}, u32[]{:S(2)}) %all-to-all-start.4) | async-done | bytes 2097184 | tf_op jit(solution)/shard_map/all_to_all | solution.py:16
  272.8 4.1 %all-to-all-start.3 = ((f32[4,128,256]{2,1,0:T(8,128)}), f32[4,128,256]{2,1,0:T(8,128)}, u32[]{:S(2)}, u32[]{:S(2)}) async-start(f32[4,128,256]{2,1,0:T(8,128)} %broadcast_in_dim.16), calls=%async_computation.3 | async-start | bytes 1048576 | tf_op jit(solution)/shard_map/all_to_all | solution.py:18
  277.2 9.3 %all-to-all-done.3 = f32[4,128,256]{2,1,0:T(8,128)} async-done(((f32[4,128,256]{2,1,0:T(8,128)}), f32[4,128,256]{2,1,0:T(8,128)}, u32[]{:S(2)}, u32[]{:S(2)}) %all-to-all-start.3) | async-done | bytes 524320 | tf_op jit(solution)/shard_map/all_to_all | solution.py:18
  288.0 4.4 %all-to-all-start.5 = ((f32[128,16,256]{2,1,0:T(8,128)}), f32[128,16,256]{2,1,0:T(8,128)S(1)}, u32[]{:S(2)}, u32[]{:S(2)}) async-start(f32[128,16,256]{2,1,0:T(8,128)} %broadcast_in_dim.17), calls=%async_computation.5 | async-start | bytes 4194304 | tf_op jit(solution)/shard_map/all_to_all | solution.py:18
  292.5 2.0 fusion.35
  294.5 2.2 convolution_add_fusion.1
  296.7 26.9 %all-to-all-done.5 = f32[128,16,256]{2,1,0:T(8,128)S(1)} async-done(((f32[128,16,256]{2,1,0:T(8,128)}), f32[128,16,256]{2,1,0:T(8,128)S(1)}, u32[]{:S(2)}, u32[]{:S(2)}) %all-to-all-start.5) | async-done | bytes 2097184 | tf_op jit(solution)/shard_map/all_to_all | solution.py:18
  (53 shorter events, 9.6 us)
Async XLA Ops:
  7.2 16.1 %copy-start = (bf16[8,256,256]{2,1,0:T(8,128)(2,1)S(1)}, bf16[8,256,256]{2,1,0:T(8,128)(2,1)}, u32[]{:S(2)}) copy-start(bf16[8,256,256]{2,1,0:T(8,128)(2,1)} %param.16) | copy-start | bytes 3145732
  11.9 9.7 %copy-start.2 = (bf16[512,256]{1,0:T(8,128)(2,1)S(1)}, bf16[512,256]{1,0:T(8,128)(2,1)}, u32[]{:S(2)}) copy-start(bf16[512,256]{1,0:T(8,128)(2,1)} %param.15) | copy-start | bytes 786436
  11.9 9.7 %copy-start.4 = (bf16[512,256]{1,0:T(8,128)(2,1)S(1)}, bf16[512,256]{1,0:T(8,128)(2,1)}, u32[]{:S(2)}) copy-start(bf16[512,256]{1,0:T(8,128)(2,1)} %param.25) | copy-start | bytes 786436
  11.9 70.7 %all-to-all-start = ((bf16[32,2,128,256]{3,2,1,0:T(8,128)(2,1)}), bf16[32,2,128,256]{3,2,1,0:T(8,128)(2,1)}, u32[]{:S(2)}, u32[]{:S(2)}) async-start(bf16[32,2,128,256]{3,2,1,0:T(8,128)(2,1)} %bitcast.105), calls=%async_computation | async-start | bytes 8388608 | tf_op jit(solution)/shard_map/all_to_all | solution.py:68
  21.5 149.8 %all-reduce.5.cloned.1.call-start = ((), (), s32[]{:S(2)}) async-start(), calls=%async_computation.7 | async-start | bytes 524288 | tf_op jit(solution)/shard_map/psum | solution.py:127
  31.3 6.7 %copy-start.11 = (f32[200,8]{0,1:T(8,128)S(1)}, f32[200,8]{0,1:T(8,128)}, u32[]{:S(2)}) copy-start(f32[200,8]{0,1:T(8,128)} %param.18) | copy-start | bytes 19204
  31.3 6.7 %copy-start.12 = (s32[1,1,64]{2,1,0:T(1,128)S(1)}, s32[1,1,64]{2,1,0:T(1,128)}, u32[]{:S(2)}) copy-start(s32[1,1,64]{2,1,0:T(1,128)} %param.22) | copy-start | bytes 772
  38.2 4.3 %copy-start.1 = (bf16[1,1,64,128,128]{4,3,2,1,0:T(8,128)(2,1)S(1)}, bf16[1,1,64,128,128]{4,3,2,1,0:T(8,128)(2,1)}, u32[]{:S(2)}) copy-start(bf16[1,1,64,128,128]{4,3,2,1,0:T(8,128)(2,1)} %param.19) | copy-start | bytes 6291460
  38.2 4.3 %copy-start.8 = (s32[1,1,64]{2,1,0:T(1,128)S(1)}, s32[1,1,64]{2,1,0:T(1,128)}, u32[]{:S(2)}) copy-start(s32[1,1,64]{2,1,0:T(1,128)} %param.20) | copy-start | bytes 772
  38.2 4.3 %copy-start.9 = (s32[1,1,64]{2,1,0:T(1,128)S(1)}, s32[1,1,64]{2,1,0:T(1,128)}, u32[]{:S(2)}) copy-start(s32[1,1,64]{2,1,0:T(1,128)} %param.21) | copy-start | bytes 772
  92.4 122.2 %all-to-all-start.1 = ((bf16[32,256,256]{2,1,0:T(8,128)(2,1)}), bf16[32,256,256]{2,1,0:T(8,128)(2,1)}, u32[]{:S(2)}, u32[]{:S(2)}) async-start(bf16[32,256,256]{2,1,0:T(8,128)(2,1)} %bitcast.104), calls=%async_computation.1 | async-start | bytes 8388608 | tf_op jit(solution)/shard_map/all_to_all | solution.py:92
  99.8 114.8 %all-reduce.3.cloned.1.call-start = ((), (), s32[]{:S(2)}) async-start(), calls=%async_computation.6 | async-start | bytes 1048576 | tf_op jit(solution)/shard_map/psum | solution.py:126
  122.6 7.3 %copy-start.10 = (s32[1,1,32,2]{2,3,1,0:T(2,128)S(1)}, s32[1,1,32,2]{2,3,1,0:T(2,128)}, u32[]{:S(2)}) copy-start(s32[1,1,32,2]{2,3,1,0:T(2,128)} %param.24) | copy-start | bytes 772
  122.6 7.5 %copy-start.5 = (bf16[512,256]{1,0:T(8,128)(2,1)S(1)}, bf16[512,256]{1,0:T(8,128)(2,1)}, u32[]{:S(2)}) copy-start(bf16[512,256]{1,0:T(8,128)(2,1)} %param.25) | copy-start | bytes 786436
  229.8 42.2 %all-to-all-start.4 = ((f32[128,16,256]{2,1,0:T(8,128)}), f32[128,16,256]{2,1,0:T(8,128)S(1)}, u32[]{:S(2)}, u32[]{:S(2)}) async-start(f32[128,16,256]{2,1,0:T(8,128)} %bitcast.35), calls=%async_computation.4 | async-start | bytes 4194304 | tf_op jit(solution)/shard_map/all_to_all | solution.py:16
  272.8 13.6 %all-to-all-start.3 = ((f32[4,128,256]{2,1,0:T(8,128)}), f32[4,128,256]{2,1,0:T(8,128)}, u32[]{:S(2)}, u32[]{:S(2)}) async-start(f32[4,128,256]{2,1,0:T(8,128)} %broadcast_in_dim.16), calls=%async_computation.3 | async-start | bytes 1048576 | tf_op jit(solution)/shard_map/all_to_all | solution.py:18
  277.0 15.5 %copy-start.3 = (bf16[512,256]{1,0:T(8,128)(2,1)S(1)}, bf16[512,256]{1,0:T(8,128)(2,1)}, u32[]{:S(2)}) copy-start(bf16[512,256]{1,0:T(8,128)(2,1)} %param.15) | copy-start | bytes 786436
  277.0 15.5 %copy-start.6 = (bf16[256,256]{1,0:T(8,128)(2,1)S(1)}, bf16[256,256]{1,0:T(8,128)(2,1)}, u32[]{:S(2)}) copy-start(bf16[256,256]{1,0:T(8,128)(2,1)} %param.17) | copy-start | bytes 393220
  288.0 35.6 %all-to-all-start.5 = ((f32[128,16,256]{2,1,0:T(8,128)}), f32[128,16,256]{2,1,0:T(8,128)S(1)}, u32[]{:S(2)}, u32[]{:S(2)}) async-start(f32[128,16,256]{2,1,0:T(8,128)} %broadcast_in_dim.17), calls=%async_computation.5 | async-start | bytes 4194304 | tf_op jit(solution)/shard_map/all_to_all | solution.py:18
  294.5 30.4 %copy-start.7 = (f32[256,256]{1,0:T(8,128)S(1)}, f32[256,256]{1,0:T(8,128)}, u32[]{:S(2)}) copy-start(f32[256,256]{1,0:T(8,128)} %all-reduce.5.cloned.1.call-done) | copy-start | bytes 786436
Sparse Core Ops, SparseCore 0:
  26.1 145.1 all-reduce.4
  174.2 40.3 all-reduce.2

commit v3 on v2

--- a/solution.py
+++ b/solution.py
@@ -123,13 +123,11 @@
     )
     projected_part = jnp.einsum("lbnf,bfg->lng", partial_value, basis_f32, precision=highest)
     basis_local = jnp.einsum("lbnf,lng->bfg", partial_value, cot_f32, precision=highest)
-    projected = lax.psum(projected_part, "rel")
-    root_grad = lax.psum(root_local, "rows")
-    returned, basis_local, projected, root_grad = lax.optimization_barrier(
-        (returned, basis_local, projected, root_grad)
+    root_grad = a2a_psum(root_local, ("rows",))
+    returned, basis_local, projected_part = lax.optimization_barrier(
+        (returned, basis_local, projected_part)
     )
 
-    output = (projected.reshape(-1, feat_width) + root_term).astype(jnp.bfloat16)
     basis_grad = a2a_psum(
         basis_local.reshape(-1, basis_local.shape[-1]), ("rows", "rel")
     ).reshape(basis_local.shape)
@@ -143,7 +141,13 @@
         (((1,), (0,)), ((), ())),
         precision=highest,
     )
-    summed = a2a_psum(own_grads.reshape(-1, feat_width), ("rel",))
+    both = jnp.concatenate(
+        [projected_part.reshape(-1, feat_width), own_grads.reshape(-1, feat_width)]
+    )
+    summed_both = a2a_psum(both, ("rel",))
+    projected = summed_both[: features.shape[0]]
+    summed = summed_both[features.shape[0] :]
+    output = (projected + root_term).astype(jnp.bfloat16)
     root_back = lax.dot_general(
         cotangent, root, (((1,), (1,)), ((), ())), preferred_element_type=jnp.float32
     )

time: 338 us -> 291 us (0.86)
  waiting for transfers between devices: 142 us -> 94.5 us
  between operations: 15.2 us -> 1.82 us
  blocking collectives: 10.3 us -> 18.8 us
  starting transfers between devices: 36.9 us -> 44.9 us
  local copies, waits for them, and re-layouts: 51.5 us -> 47.2 us
    psum x2 -> x0, waiting for transfers between devices: 75.8 us -> none  [the longest x1 43.3 us: on_device(): projected = lax.psum(projected_part, 'rel')]
    all_to_all x1, waiting for transfers between devices: 0.01 us -> 14.3 us  [on_device(): lax.all_to_all(slot_grads.astype(SLOT_GRAD_LINK_DTYPE).reshape(row_device...]
    all_to_all x2 -> x3, waiting for transfers between devices: 36.2 us -> 45.9 us  [a2a_psum(): lax.all_to_all(jnp.broadcast_to(reduced, chunked.shape), axes, 0, 0, tile...]
    all_to_all x1, blocking collectives: 10.3 us -> 18.8 us  [a2a_psum(): pieces = lax.all_to_all(chunked, axes, 0, 0, tiled=True)]
    all_to_all x2 -> x3, starting transfers between devices: 8.59 us -> 16.1 us  [a2a_psum(): lax.all_to_all(jnp.broadcast_to(reduced, chunked.shape), axes, 0, 0, tile...]
    while x1 -> x0, local copies, waits for them, and re-layouts: 6.72 us -> none  [on_device(): slot_grads = lax.fori_loop(0, steps_live, backward_step, slot_zero)]
    all_to_all x1, waiting for transfers between devices: 0.01 us -> 4.62 us  [on_device(): lax.all_to_all(outgoing, 'rows', split_axis=0, concat_axis=0, tiled=True)]
    all_to_all x1 -> x2, starting transfers between devices: 11.2 us -> 14.2 us  [a2a_psum(): pieces = lax.all_to_all(chunked, axes, 0, 0, tiled=True)]
  transfers between devices with their start and end apart: 7 -> 7, of which waited for: 5 -> 6; matrix products, arithmetic and copies ran while one was open for 34% -> 38% of each run, Pallas kernels for 0% -> 0%
where the time goes in v3:
time: 291 us; the launch traced here: 287 us
  waiting for transfers between devices  94.5 us (32%)
  matrix products  75.2 us (26%)
  local copies, waits for them, and re-layouts  47.2 us (16%)
  starting transfers between devices  44.9 us (15%)
  blocking collectives  18.8 us (6%)
  other arithmetic  3.67 us (1%)
    all_to_all x3, waiting for transfers between devices, a2a_psum(): lax.all_to_all(jnp.broadcast_to(reduced, chunked.shape), axes, 0, 0, tile...  45.9 us
    all_to_all x2, waiting for transfers between devices, a2a_psum(): pieces = lax.all_to_all(chunked, axes, 0, 0, tiled=True)  29.8 us
    all_to_all x1, blocking collectives, a2a_psum(): pieces = lax.all_to_all(chunked, axes, 0, 0, tiled=True)  18.8 us
    all_to_all x3, starting transfers between devices, a2a_psum(): lax.all_to_all(jnp.broadcast_to(reduced, chunked.shape), axes, 0, 0, tile...  16.1 us
    all_to_all x1, waiting for transfers between devices, on_device(): lax.all_to_all(slot_grads.astype(SLOT_GRAD_LINK_DTYPE).reshape(row_device...  14.3 us
    dot_general x1, matrix products, backward_step(): lax.dot_general(slot_hot, backward_term, contract_first, precision=highest)  14.2 us
    all_to_all x2, starting transfers between devices, a2a_psum(): pieces = lax.all_to_all(chunked, axes, 0, 0, tiled=True)  14.2 us
    dot_general x1, matrix products, backward_step(): lax.dot_general(weights, agg_grad, (((1,), (0,)), ((), ())), precision=hi...  11.5 us
  transfers between devices with their start and end apart: 7, of which 6 were waited for; matrix products, arithmetic and copies ran while one was open for 38% of the time, Pallas kernels for 0%

profile of v3, /device:TPU:1, one launch (start us, length us, event | category | flops | bytes accessed | tf_op | source)
XLA Modules:
  0.0 286.9 jit_solution(11418143379224189728)
XLA Ops:
  2.7 9.4 %all-to-all-start.6 = ((f32[32,8,256]{2,1,0:T(8,128)}), f32[32,8,256]{2,1,0:T(8,128)S(1)}, u32[]{:S(2)}, u32[]{:S(2)}) async-start(f32[32,8,256]{2,1,0:T(8,128)} %convolution_bitcast_fusion.1), calls=%async_computation.6 | async-start | bytes 524288 | tf_op jit(solution)/shard_map/all_to_all | solution.py:16
  13.1 3.6 %convolution_bitcast_fusion = f32[4,8,128,256]{2,3,0,1:T(8,128)} fusion(bf16[4,128,256,1]{2,1,0,3:T(8,128)(2,1)} %bitcast.112, bf16[8,256,256]{2,1,0:T(8,128)(2,1)S(1)} %copy-done), kind=kOutput, calls=%fused_computation.36 | convolution fusion | flops 536870912 | bytes 5505024 | tf_op jit(solution)/shard_map/lng,bfg->lbnf/dot_general | solution.py:71
  17.4 5.4 %copy.21 = f32[4,8,128,256]{3,2,1,0:T(8,128)} copy(f32[4,8,128,256]{2,3,0,1:T(8,128)} %convolution_bitcast_fusion) | data formatting | bytes 8388608 | tf_op jit(solution)/shard_map/lng,bfg->lbnf/transpose | solution.py:71
  22.8 2.9 %gather_fusion = bf16[64,128,256]{2,1,0:T(8,128)(2,1)} fusion(bf16[4,128,256]{2,1,0:T(8,128)(2,1)S(1)} %bitcast.107, s32[1024]{0:T(1024)S(1)} %pad_clamp_fusion.1), kind=kCustom, calls=%fused_computation | custom fusion | bytes 8388864 | tf_op jit(solution)/shard_map/gather | solution.py:67
  25.9 7.5 %all-to-all-start = ((bf16[32,2,128,256]{3,2,1,0:T(8,128)(2,1)}), bf16[32,2,128,256]{3,2,1,0:T(8,128)(2,1)}, u32[]{:S(2)}, u32[]{:S(2)}) async-start(bf16[32,2,128,256]{3,2,1,0:T(8,128)(2,1)} %bitcast.109), calls=%async_computation | async-start | bytes 8388608 | tf_op jit(solution)/shard_map/all_to_all | solution.py:68
  33.4 4.3 %broadcast_in_dim.16 = f32[64,128,256]{2,0,1:T(8,128)} broadcast(f32[]{:T(128)} %constant.53.clone.1), dimensions={} | broadcast | bytes 8388612 | tf_op jit(solution)/shard_map/broadcast_in_dim | solution.py:88
  37.7 42.9 %while.24 = (s32[]{:T(128)}, f32[64,128,256]{2,0,1:T(8,128)}, s32[]{:T(128)}, s32[1,1,64]{2,1,0:T(1,128)S(1)}, s32[1,1,64]{2,1,0:T(1,128)S(1)}, /*index=5*/s32[]...) while((s32[]{:T(128)}, f32[64,128,256]{2,0,1:T(8,128)}, ...), condition=%wide.region_1.2_spmd, body=%wide.region_0.1_spmd.sunk | while | flops 2954894080 | bytes 65016960 | solution.py:89
  38.9 11.5 %fusion.83 = bf16[64,128,256]{2,0,1:T(8,128)(2,1)S(1)} fusion(f32[32,128,256]{2,1,0:T(8,128)} %get-tuple-element.418, f32[64,8]{0,1:T(8,128)S(1)} %get-tuple-element.417, f32[64,4]{0,1:T(4,128)S(1)} %fusion.82), kind=kOutput, calls=%fused_computation.6.clone.1 | convolution fusion | flops 805308416 | bytes 8391680 | tf_op jit(solution)/shard_map/while/body/dot_general | solution.py:77
  50.4 6.6 %fusion.84 = f32[64,256,128]{2,1,0:T(8,128)} fusion(bf16[64,128,128]{2,1,0:T(8,128)(2,1)S(1)} %get-tuple-element.419, bf16[64,128,256]{2,0,1:T(8,128)(2,1)S(1)} %fusion.83), kind=kOutput, calls=%fused_computation.5.clone.1 | convolution fusion | flops 536870912 | bytes 14680064 | tf_op jit(solution)/shard_map/while/body/tij,tif->tjf/dot_general | solution.py:80
  57.0 9.2 %copy.61 = f32[64,256,128]{1,0,2:T(8,128)} copy(f32[64,256,128]{2,1,0:T(8,128)} %fusion.84) | data formatting | bytes 16777216 | tf_op jit(solution)/shard_map/while/body/tij,tif->tjf/dot_general | solution.py:80
  66.2 14.2 %fusion.85 = f32[64,128,256]{2,0,1:T(8,128)} fusion(f32[64,128,256]{2,0,1:T(8,128)} %get-tuple-element.401, f32[64,256,128]{1,0,2:T(8,128)} %copy.61, s32[64]{0:T(128)S(1)} %bitcast.121), kind=kOutput, calls=%fused_computation.8.clone.1 | convolution fusion | flops 1612713984 | bytes 25166080 | tf_op jit(solution)/shard_map/while/body/dot_general | solution.py:84
  80.9 4.6 %all-to-all-done = bf16[32,2,128,256]{3,2,1,0:T(8,128)(2,1)} async-done(((bf16[32,2,128,256]{3,2,1,0:T(8,128)(2,1)}), bf16[32,2,128,256]{3,2,1,0:T(8,128)(2,1)}, u32[]{:S(2)}, u32[]{:S(2)}) %all-to-all-start) | async-done | bytes 4194336 | tf_op jit(solution)/shard_map/all_to_all | solution.py:68
  85.5 9.8 %copy.54 = bf16[64,128,256]{2,1,0:T(8,128)(2,1)} copy(f32[64,128,256]{2,0,1:T(8,128)} %get-tuple-element.241) | data formatting | bytes 12582912 | tf_op jit(solution)/shard_map/optimization_barrier | solution.py:90
  95.3 7.1 %all-to-all-start.1 = ((bf16[32,256,256]{2,1,0:T(8,128)(2,1)}), bf16[32,256,256]{2,1,0:T(8,128)(2,1)}, u32[]{:S(2)}, u32[]{:S(2)}) async-start(bf16[32,256,256]{2,1,0:T(8,128)(2,1)} %bitcast.108), calls=%async_computation.1 | async-start | bytes 8388608 | tf_op jit(solution)/shard_map/all_to_all | solution.py:92
  102.4 5.0 %gather_fusion.1 = bf16[64,128,256]{2,1,0:T(8,128)(2,1)} fusion(bf16[64,128,256]{2,1,0:T(8,128)(2,1)} %bitcast.22, s32[1024]{0:T(1024)S(1)} %pad_clamp_fusion), kind=kCustom, calls=%fused_computation.1 | custom fusion | bytes 8388864 | tf_op jit(solution)/shard_map/while/body/gather | solution.py:106
  107.3 2.5 broadcast_in_dim.17
  109.8 15.3 %while.25 = (s32[]{:T(128)}, f32[32,128,256]{2,0,1:T(8,128)}, s32[]{:T(128)}, s32[1,1,64]{2,1,0:T(1,128)S(1)}, s32[]{:T(128)}, /*index=5*/f32[64,8]{0,1:T(8,128)...) while((s32[]{:T(128)}, f32[32,128,256]{2,0,1:T(8,128)}, ...), condition=%wide.region_3.4_spmd, body=%wide.region_2.3_spmd.sunk | while | flops 1343228672 | bytes 31462264 | solution.py:116
  110.5 3.4 %fusion.90 = f32[64,128,256]{2,1,0:T(8,128)S(1)} fusion(bf16[64,128,128]{2,1,0:T(8,128)(2,1)S(1)} %get-tuple-element.448, bf16[64,128,256]{2,1,0:T(8,128)(2,1)} %get-tuple-element.449), kind=kOutput, calls=%fused_computation.58.clone.1 | convolution fusion | flops 536870912 | bytes 14680064 | tf_op jit(solution)/shard_map/while/body/tij,tjf->tif/dot_general | solution.py:107
  113.9 11.0 %fusion.92 = f32[32,128,256]{2,0,1:T(8,128)} fusion(f32[32,128,256]{2,0,1:T(8,128)} %get-tuple-element.433, f32[64,128,256]{2,1,0:T(8,128)S(1)} %fusion.90, f32[64,8]{0,1:T(8,128)S(1)} %get-tuple-element.447, f32[64,4]{0,1:T(4,128)S(1)} %fusion.91), kind=kOutput, calls=%fused_computation.21.clone.1 | convolution fusion | flops 806356992 | bytes 16780288 | tf_op jit(solution)/shard_map/while/body/dot_general | solution.py:111
  125.2 8.6 %fusion.32 = f32[8,256,256]{2,1,0:T(8,128)} fusion(bf16[4,128,256,1]{2,1,0,3:T(8,128)(2,1)S(1)} %bitcast.113, f32[4,8,128,256]{3,1,0,2:T(8,128)} %bitcast.25), kind=kOutput, calls=%fused_computation.37 | convolution fusion | flops 3221225472 | bytes 6553600 | tf_op jit(solution)/shard_map/lbnf,lng->bfg/dot_general | solution.py:125
  133.8 6.4 %fusion.35 = f32[4,128,256]{2,1,0:T(8,128)S(1)} fusion(f32[4,8,128,256]{3,1,0,2:T(8,128)} %bitcast.25, bf16[8,256,256]{2,1,0:T(8,128)(2,1)S(1)} %copy-done), kind=kOutput, calls=%fused_computation.38 | convolution fusion | flops 3221225472 | bytes 5767168 | tf_op jit(solution)/shard_map/lbnf,bfg->lng/dot_general | solution.py:124
  140.2 14.3 %all-to-all-done.1 = bf16[32,256,256]{2,1,0:T(8,128)(2,1)} async-done(((bf16[32,256,256]{2,1,0:T(8,128)(2,1)}), bf16[32,256,256]{2,1,0:T(8,128)(2,1)}, u32[]{:S(2)}, u32[]{:S(2)}) %all-to-all-start.1) | async-done | bytes 4194336 | tf_op jit(solution)/shard_map/all_to_all | solution.py:92
  155.2 7.4 %all-to-all-start.7 = ((f32[32,8,256]{2,1,0:T(8,128)}), f32[32,8,256]{2,1,0:T(8,128)S(1)}, u32[]{:S(2)}, u32[]{:S(2)}) async-start(f32[32,8,256]{2,1,0:T(8,128)} %broadcast_in_dim.20), calls=%async_computation.7 | async-start | bytes 524288 | tf_op jit(solution)/shard_map/all_to_all | solution.py:18
  162.6 4.5 %fusion.26 = f32[4,128,256]{2,0,1:T(4,128)S(1)} fusion(bf16[64,128,256]{2,1,0:T(8,128)(2,1)} %bitcast.33, s32[64]{0:T(128)S(1)} %eq.116), kind=kOutput, calls=%fused_computation.30 | convolution fusion | flops 16777472 | bytes 4718848 | tf_op jit(solution)/shard_map/dot_general | solution.py:138
  167.3 4.1 %all-to-all-done.7 = f32[32,8,256]{2,1,0:T(8,128)S(1)} async-done(((f32[32,8,256]{2,1,0:T(8,128)}), f32[32,8,256]{2,1,0:T(8,128)S(1)}, u32[]{:S(2)}, u32[]{:S(2)}) %all-to-all-start.7) | async-done | bytes 262176 | tf_op jit(solution)/shard_map/all_to_all | solution.py:18
  171.4 18.8 %all_to_all.40 = f32[4,256,256]{2,1,0:T(8,128)} all-to-all(f32[4,256,256]{2,1,0:T(8,128)S(1)} %bitcast.111), channel_id=1, replica_groups=mesh['rows'=32,'rel'=4] {'rel'}, dimensions={0} | all-to-all | bytes 2097152 | tf_op jit(solution)/shard_map/all_to_all | solution.py:16
  190.2 4.8 %all-to-all-start.4 = ((f32[128,16,256]{2,1,0:T(8,128)}), f32[128,16,256]{2,1,0:T(8,128)S(1)}, u32[]{:S(2)}, u32[]{:S(2)}) async-start(f32[128,16,256]{2,1,0:T(8,128)} %bitcast.38), calls=%async_computation.4 | async-start | bytes 4194304 | tf_op jit(solution)/shard_map/all_to_all | solution.py:16
  196.3 29.8 %all-to-all-done.4 = f32[128,16,256]{2,1,0:T(8,128)S(1)} async-done(((f32[128,16,256]{2,1,0:T(8,128)}), f32[128,16,256]{2,1,0:T(8,128)S(1)}, u32[]{:S(2)}, u32[]{:S(2)}) %all-to-all-start.4) | async-done | bytes 2097184 | tf_op jit(solution)/shard_map/all_to_all | solution.py:16
  227.2 4.2 %all-to-all-start.3 = ((f32[4,256,256]{2,1,0:T(8,128)}), f32[4,256,256]{2,1,0:T(8,128)}, u32[]{:S(2)}, u32[]{:S(2)}) async-start(f32[4,256,256]{2,1,0:T(8,128)} %broadcast_in_dim.18), calls=%async_computation.3 | async-start | bytes 2097152 | tf_op jit(solution)/shard_map/all_to_all | solution.py:18
  231.6 14.9 %all-to-all-done.3 = f32[4,256,256]{2,1,0:T(8,128)} async-done(((f32[4,256,256]{2,1,0:T(8,128)}), f32[4,256,256]{2,1,0:T(8,128)}, u32[]{:S(2)}, u32[]{:S(2)}) %all-to-all-start.3) | async-done | bytes 1048608 | tf_op jit(solution)/shard_map/all_to_all | solution.py:18
  248.1 4.4 %all-to-all-start.5 = ((f32[128,16,256]{2,1,0:T(8,128)}), f32[128,16,256]{2,1,0:T(8,128)S(1)}, u32[]{:S(2)}, u32[]{:S(2)}) async-start(f32[128,16,256]{2,1,0:T(8,128)} %broadcast_in_dim.19), calls=%async_computation.5 | async-start | bytes 4194304 | tf_op jit(solution)/shard_map/all_to_all | solution.py:18
  256.8 26.8 %all-to-all-done.5 = f32[128,16,256]{2,1,0:T(8,128)S(1)} async-done(((f32[128,16,256]{2,1,0:T(8,128)}), f32[128,16,256]{2,1,0:T(8,128)S(1)}, u32[]{:S(2)}, u32[]{:S(2)}) %all-to-all-start.5) | async-done | bytes 2097184 | tf_op jit(solution)/shard_map/all_to_all | solution.py:18
  (52 shorter events, 17.1 us)
Async XLA Ops:
  0.6 12.4 %copy-start = (bf16[8,256,256]{2,1,0:T(8,128)(2,1)S(1)}, bf16[8,256,256]{2,1,0:T(8,128)(2,1)}, u32[]{:S(2)}) copy-start(bf16[8,256,256]{2,1,0:T(8,128)(2,1)} %param.16) | copy-start | bytes 3145732
  2.7 23.1 %all-to-all-start.6 = ((f32[32,8,256]{2,1,0:T(8,128)}), f32[32,8,256]{2,1,0:T(8,128)S(1)}, u32[]{:S(2)}, u32[]{:S(2)}) async-start(f32[32,8,256]{2,1,0:T(8,128)} %convolution_bitcast_fusion.1), calls=%async_computation.6 | async-start | bytes 524288 | tf_op jit(solution)/shard_map/all_to_all | solution.py:16
  17.4 5.4 %copy-start.2 = (bf16[512,256]{1,0:T(8,128)(2,1)S(1)}, bf16[512,256]{1,0:T(8,128)(2,1)}, u32[]{:S(2)}) copy-start(bf16[512,256]{1,0:T(8,128)(2,1)} %param.15) | copy-start | bytes 786436
  22.8 2.9 %copy-start.10 = (f32[200,8]{0,1:T(8,128)S(1)}, f32[200,8]{0,1:T(8,128)}, u32[]{:S(2)}) copy-start(f32[200,8]{0,1:T(8,128)} %param.18) | copy-start | bytes 19204
  22.8 2.9 %copy-start.11 = (s32[1,1,64]{2,1,0:T(1,128)S(1)}, s32[1,1,64]{2,1,0:T(1,128)}, u32[]{:S(2)}) copy-start(s32[1,1,64]{2,1,0:T(1,128)} %param.22) | copy-start | bytes 772
  25.9 59.6 %all-to-all-start = ((bf16[32,2,128,256]{3,2,1,0:T(8,128)(2,1)}), bf16[32,2,128,256]{3,2,1,0:T(8,128)(2,1)}, u32[]{:S(2)}, u32[]{:S(2)}) async-start(bf16[32,2,128,256]{3,2,1,0:T(8,128)(2,1)} %bitcast.109), calls=%async_computation | async-start | bytes 8388608 | tf_op jit(solution)/shard_map/all_to_all | solution.py:68
  33.4 4.3 %copy-start.1 = (bf16[1,1,64,128,128]{4,3,2,1,0:T(8,128)(2,1)S(1)}, bf16[1,1,64,128,128]{4,3,2,1,0:T(8,128)(2,1)}, u32[]{:S(2)}) copy-start(bf16[1,1,64,128,128]{4,3,2,1,0:T(8,128)(2,1)} %param.19) | copy-start | bytes 6291460
  33.4 4.3 %copy-start.7 = (s32[1,1,64]{2,1,0:T(1,128)S(1)}, s32[1,1,64]{2,1,0:T(1,128)}, u32[]{:S(2)}) copy-start(s32[1,1,64]{2,1,0:T(1,128)} %param.20) | copy-start | bytes 772
  33.4 4.3 %copy-start.8 = (s32[1,1,64]{2,1,0:T(1,128)S(1)}, s32[1,1,64]{2,1,0:T(1,128)}, u32[]{:S(2)}) copy-start(s32[1,1,64]{2,1,0:T(1,128)} %param.21) | copy-start | bytes 772
  37.7 42.9 %copy-start.9 = (s32[1,1,32,2]{2,3,1,0:T(2,128)S(1)}, s32[1,1,32,2]{2,3,1,0:T(2,128)}, u32[]{:S(2)}) copy-start(s32[1,1,32,2]{2,3,1,0:T(2,128)} %param.24) | copy-start | bytes 772
  95.3 59.2 %all-to-all-start.1 = ((bf16[32,256,256]{2,1,0:T(8,128)(2,1)}), bf16[32,256,256]{2,1,0:T(8,128)(2,1)}, u32[]{:S(2)}, u32[]{:S(2)}) async-start(bf16[32,256,256]{2,1,0:T(8,128)(2,1)} %bitcast.108), calls=%async_computation.1 | async-start | bytes 8388608 | tf_op jit(solution)/shard_map/all_to_all | solution.py:92
  109.8 15.4 %copy-start.4 = (bf16[512,256]{1,0:T(8,128)(2,1)S(1)}, bf16[512,256]{1,0:T(8,128)(2,1)}, u32[]{:S(2)}) copy-start(bf16[512,256]{1,0:T(8,128)(2,1)} %param.25) | copy-start | bytes 786436
  155.2 16.2 %all-to-all-start.7 = ((f32[32,8,256]{2,1,0:T(8,128)}), f32[32,8,256]{2,1,0:T(8,128)S(1)}, u32[]{:S(2)}, u32[]{:S(2)}) async-start(f32[32,8,256]{2,1,0:T(8,128)} %broadcast_in_dim.20), calls=%async_computation.7 | async-start | bytes 524288 | tf_op jit(solution)/shard_map/all_to_all | solution.py:18
  171.4 18.8 %copy-start.5 = (f32[32,8,256]{2,1,0:T(8,128)}, f32[32,8,256]{2,1,0:T(8,128)S(1)}, u32[]{:S(2)}) copy-start(f32[32,8,256]{2,1,0:T(8,128)S(1)} %all-to-all-done.7) | copy-start | bytes 786436
  190.2 35.9 %all-to-all-start.4 = ((f32[128,16,256]{2,1,0:T(8,128)}), f32[128,16,256]{2,1,0:T(8,128)S(1)}, u32[]{:S(2)}, u32[]{:S(2)}) async-start(f32[128,16,256]{2,1,0:T(8,128)} %bitcast.38), calls=%async_computation.4 | async-start | bytes 4194304 | tf_op jit(solution)/shard_map/all_to_all | solution.py:16
  227.2 19.4 %all-to-all-start.3 = ((f32[4,256,256]{2,1,0:T(8,128)}), f32[4,256,256]{2,1,0:T(8,128)}, u32[]{:S(2)}, u32[]{:S(2)}) async-start(f32[4,256,256]{2,1,0:T(8,128)} %broadcast_in_dim.18), calls=%async_computation.3 | async-start | bytes 2097152 | tf_op jit(solution)/shard_map/all_to_all | solution.py:18
  231.6 22.2 %copy-start.3 = (bf16[512,256]{1,0:T(8,128)(2,1)S(1)}, bf16[512,256]{1,0:T(8,128)(2,1)}, u32[]{:S(2)}) copy-start(bf16[512,256]{1,0:T(8,128)(2,1)} %param.15) | copy-start | bytes 786436
  231.6 22.3 %copy-start.6 = (bf16[256,256]{1,0:T(8,128)(2,1)S(1)}, bf16[256,256]{1,0:T(8,128)(2,1)}, u32[]{:S(2)}) copy-start(bf16[256,256]{1,0:T(8,128)(2,1)} %param.17) | copy-start | bytes 393220
  248.1 35.6 %all-to-all-start.5 = ((f32[128,16,256]{2,1,0:T(8,128)}), f32[128,16,256]{2,1,0:T(8,128)S(1)}, u32[]{:S(2)}, u32[]{:S(2)}) async-start(f32[128,16,256]{2,1,0:T(8,128)} %broadcast_in_dim.19), calls=%async_computation.5 | async-start | bytes 4194304 | tf_op jit(solution)/shard_map/all_to_all | solution.py:18

commit v4 on v3

--- a/solution.py
+++ b/solution.py
@@ -17,6 +17,17 @@
     reduced = jnp.sum(pieces, axis=0, keepdims=True)
     gathered = lax.all_to_all(jnp.broadcast_to(reduced, chunked.shape), axes, 0, 0, tiled=True)
     return gathered.reshape(value.shape)
+
+
+def split_hi_lo(value):
+    high = value.astype(jnp.bfloat16)
+    low = (value - high.astype(jnp.float32)).astype(jnp.bfloat16)
+    return jnp.concatenate([high, low], axis=1)
+
+
+def join_hi_lo(pair):
+    half = pair.shape[1] // 2
+    return pair[:, :half].astype(jnp.float32) + pair[:, half:].astype(jnp.float32)
 
 
 def on_device(
@@ -64,8 +75,17 @@
             step_tiles, local_blocks * num_bases
         )
 
-    outgoing = blocks[send_rows]
+    root_local = lax.dot_general(
+        features, cotangent, contract_first, preferred_element_type=jnp.float32
+    )
+    root_rows = root_local.shape[0] // row_devices
+    root_chunks = root_local.reshape(row_devices, root_rows, feat_width)
+    outgoing = blocks[send_rows].reshape(row_devices, slots_peer * size_block, feat_width)
+    outgoing = jnp.concatenate([outgoing, split_hi_lo(root_chunks)], axis=1)
     incoming = lax.all_to_all(outgoing, "rows", split_axis=0, concat_axis=0, tiled=True)
+    block_rows = slots_peer * size_block
+    root_mine = jnp.sum(join_hi_lo(incoming[:, block_rows:]), axis=0, keepdims=True)
+    incoming = incoming[:, :block_rows]
 
     cot_blocks = cotangent.reshape(local_blocks, size_block, feat_width)
     agg_grad = jnp.einsum("lng,bfg->lbnf", cot_blocks, bases, preferred_element_type=jnp.float32)
@@ -87,17 +107,16 @@
 
     slot_zero = jnp.zeros((total_slots, size_block, feat_width), jnp.float32)
     slot_grads = lax.fori_loop(0, steps_live, backward_step, slot_zero)
-    incoming, slot_grads = lax.optimization_barrier((incoming, slot_grads))
+    incoming, slot_grads, root_mine = lax.optimization_barrier((incoming, slot_grads, root_mine))
 
-    returned = lax.all_to_all(
-        slot_grads.astype(SLOT_GRAD_LINK_DTYPE).reshape(
-            row_devices, slots_peer * size_block, feat_width
-        ),
-        "rows",
-        split_axis=0,
-        concat_axis=0,
-        tiled=True,
+    slot_out = slot_grads.astype(SLOT_GRAD_LINK_DTYPE).reshape(
+        row_devices, slots_peer * size_block, feat_width
     )
+    root_bcast = jnp.broadcast_to(root_mine, (row_devices,) + root_mine.shape[1:])
+    slot_out = jnp.concatenate([slot_out, split_hi_lo(root_bcast)], axis=1)
+    returned = lax.all_to_all(slot_out, "rows", split_axis=0, concat_axis=0, tiled=True)
+    root_grad = join_hi_lo(returned[:, block_rows:]).reshape(root_local.shape)
+    returned = returned[:, :block_rows]
 
     received = incoming.reshape(total_slots, size_block, feat_width)
 
@@ -118,12 +137,8 @@
     basis_f32 = bases.astype(jnp.float32)
     cot_f32 = cot_blocks.astype(jnp.float32)
     root_term = jnp.dot(features, root, preferred_element_type=jnp.float32)
-    root_local = lax.dot_general(
-        features, cotangent, contract_first, preferred_element_type=jnp.float32
-    )
     projected_part = jnp.einsum("lbnf,bfg->lng", partial_value, basis_f32, precision=highest)
     basis_local = jnp.einsum("lbnf,lng->bfg", partial_value, cot_f32, precision=highest)
-    root_grad = a2a_psum(root_local, ("rows",))
     returned, basis_local, projected_part = lax.optimization_barrier(
         (returned, basis_local, projected_part)
     )

time: 291 us -> 278 us (0.955)
  starting transfers between devices: 44.9 us -> 33.8 us
  other arithmetic: 3.67 us -> 12.8 us
  waiting for transfers between devices: 94.5 us -> 87 us
  matrix products: 75.2 us -> 71.5 us
    all_to_all x3 -> x2, starting transfers between devices: 16.1 us -> 8.69 us  [a2a_psum(): lax.all_to_all(jnp.broadcast_to(reduced, chunked.shape), axes, 0, 0, tile...]
    slice x0 -> x2, local copies, waits for them, and re-layouts: none -> 7.38 us  [the longest x1 4.92 us: on_device(): incoming = incoming[:, :block_rows]]
    all_to_all x2 -> x1, starting transfers between devices: 14.2 us -> 8.12 us  [a2a_psum(): pieces = lax.all_to_all(chunked, axes, 0, 0, tiled=True)]
    concatenate x0 -> x2, other arithmetic: none -> 6.07 us  [the longest x1 3.8 us: on_device(): outgoing = jnp.concatenate([outgoing, split_hi_lo(root_chunks)], axis=1)]
    all_to_all x3 -> x2, waiting for transfers between devices: 45.9 us -> 40.1 us  [a2a_psum(): lax.all_to_all(jnp.broadcast_to(reduced, chunked.shape), axes, 0, 0, tile...]
    optimization_barrier x1, local copies, waits for them, and re-layouts: 9.78 us -> 4.45 us  [on_device(): lax.optimization_barrier((incoming, slot_grads, root_mine))]
    all_to_all x1, waiting for transfers between devices: 4.62 us -> 0.01 us  [on_device(): lax.all_to_all(outgoing, 'rows', split_axis=0, concat_axis=0, tiled=True)]
    all_to_all x1, waiting for transfers between devices: 14.3 us -> 17.3 us  [on_device(): lax.all_to_all(slot_out, 'rows', split_axis=0, concat_axis=0, tiled=True)]
  transfers between devices with their start and end apart: 7 -> 5, of which waited for: 6 -> 4; matrix products, arithmetic and copies ran while one was open for 38% -> 37% of each run, Pallas kernels for 0% -> 0%
where the time goes in v4:
time: 278 us; the launch traced here: 274 us
  waiting for transfers between devices  87 us (31%)
  matrix products  71.5 us (26%)
  local copies, waits for them, and re-layouts  47.8 us (17%)
  starting transfers between devices  33.8 us (12%)
  blocking collectives  18.3 us (7%)
  other arithmetic  12.8 us (5%)
    all_to_all x2, waiting for transfers between devices, a2a_psum(): lax.all_to_all(jnp.broadcast_to(reduced, chunked.shape), axes, 0, 0, tile...  40.1 us
    all_to_all x1, waiting for transfers between devices, a2a_psum(): pieces = lax.all_to_all(chunked, axes, 0, 0, tiled=True)  29.6 us
    all_to_all x1, blocking collectives, a2a_psum(): pieces = lax.all_to_all(chunked, axes, 0, 0, tiled=True)  18.3 us
    all_to_all x1, waiting for transfers between devices, on_device(): lax.all_to_all(slot_out, 'rows', split_axis=0, concat_axis=0, tiled=True)  17.3 us
    dot_general x1, matrix products, backward_step(): lax.dot_general(slot_hot, backward_term, contract_first, precision=highest)  14.2 us
    dot_general x1, matrix products, backward_step(): lax.dot_general(weights, agg_grad, (((1,), (0,)), ((), ())), precision=hi...  11.5 us
    dot_general x1, matrix products, forward_step(): lax.dot_general(weights, messages, contract_first, precision=highest)  11 us
    all_to_all x1, starting transfers between devices, on_device(): lax.all_to_all(outgoing, 'rows', split_axis=0, concat_axis=0, tiled=True)  9.6 us
  transfers between devices with their start and end apart: 5, of which 4 were waited for; matrix products, arithmetic and copies ran while one was open for 37% of the time, Pallas kernels for 0%

profile of v4, /device:TPU:1, one launch (start us, length us, event | category | flops | bytes accessed | tf_op | source)
XLA Modules:
  0.0 273.9 jit_solution(13975579814351659379)
XLA Ops:
  2.9 3.7 %gather_fusion = bf16[64,128,256]{2,1,0:T(8,128)(2,1)} fusion(bf16[4,128,256]{2,1,0:T(8,128)(2,1)} %bitcast.115, s32[1024]{0:T(1024)S(1)} %pad_clamp_fusion.1), kind=kCustom, calls=%fused_computation | custom fusion | bytes 8388864 | tf_op jit(solution)/shard_map/gather | solution.py:83
  6.7 3.8 %pad_maximum_fusion = bf16[32,272,256]{2,1,0:T(8,128)(2,1)} fusion(bf16[32,8,256]{2,1,0:T(8,128)(2,1)S(1)} %get-tuple-element.285, bf16[32,8,256]{2,1,0:T(8,128)(2,1)S(1)} %get-tuple-element.286, bf16[32,256,256]{2,1,0:T(8,128)(2,1)} %bitcast.118), kind=kLoop, calls=%fused_computation.30 | loop fusion | flops 13369344 | bytes 8912896 | tf_op jit(solution)/shard_map/concatenate | solution.py:84
  10.5 9.6 %all-to-all-start = ((bf16[32,272,256]{2,1,0:T(8,128)(2,1)}), bf16[32,272,256]{2,1,0:T(8,128)(2,1)}, u32[]{:S(2)}, u32[]{:S(2)}) async-start(bf16[32,272,256]{2,1,0:T(8,128)(2,1)} %pad_maximum_fusion), calls=%async_computation | async-start | bytes 8912896 | tf_op jit(solution)/shard_map/all_to_all | solution.py:85
  20.8 2.7 convolution_bitcast_fusion
  23.5 5.4 %copy.21 = f32[4,8,128,256]{3,2,1,0:T(8,128)} copy(f32[4,8,128,256]{2,3,0,1:T(8,128)} %convolution_bitcast_fusion) | data formatting | bytes 8388608 | tf_op jit(solution)/shard_map/lng,bfg->lbnf/transpose | solution.py:91
  29.1 4.3 %broadcast_in_dim.22 = f32[64,128,256]{2,0,1:T(8,128)} broadcast(f32[]{:T(128)} %constant.53.clone.1), dimensions={} | broadcast | bytes 8388612 | tf_op jit(solution)/shard_map/broadcast_in_dim | solution.py:108
  33.4 42.8 %while.24 = (s32[]{:T(128)}, f32[64,128,256]{2,0,1:T(8,128)}, s32[]{:T(128)}, s32[1,1,64]{2,1,0:T(1,128)S(1)}, s32[1,1,64]{2,1,0:T(1,128)S(1)}, /*index=5*/s32[]...) while((s32[]{:T(128)}, f32[64,128,256]{2,0,1:T(8,128)}, ...), condition=%wide.region_1.2_spmd, body=%wide.region_0.1_spmd.sunk | while | flops 2954894080 | bytes 65016960 | solution.py:109
  34.6 11.5 %fusion.84 = bf16[64,128,256]{2,0,1:T(8,128)(2,1)S(1)} fusion(f32[32,128,256]{2,1,0:T(8,128)} %get-tuple-element.424, f32[64,8]{0,1:T(8,128)S(1)} %get-tuple-element.423, f32[64,4]{0,1:T(4,128)S(1)} %fusion.83), kind=kOutput, calls=%fused_computation.6.clone.1 | convolution fusion | flops 805308416 | bytes 8391680 | tf_op jit(solution)/shard_map/while/body/dot_general | solution.py:97
  46.1 6.6 %fusion.85 = f32[64,256,128]{2,1,0:T(8,128)} fusion(bf16[64,128,128]{2,1,0:T(8,128)(2,1)S(1)} %get-tuple-element.425, bf16[64,128,256]{2,0,1:T(8,128)(2,1)S(1)} %fusion.84), kind=kOutput, calls=%fused_computation.5.clone.1 | convolution fusion | flops 536870912 | bytes 14680064 | tf_op jit(solution)/shard_map/while/body/tij,tif->tjf/dot_general | solution.py:100
  52.7 9.2 %copy.61 = f32[64,256,128]{1,0,2:T(8,128)} copy(f32[64,256,128]{2,1,0:T(8,128)} %fusion.85) | data formatting | bytes 16777216 | tf_op jit(solution)/shard_map/while/body/tij,tif->tjf/dot_general | solution.py:100
  61.9 14.2 %fusion.86 = f32[64,128,256]{2,0,1:T(8,128)} fusion(f32[64,128,256]{2,0,1:T(8,128)} %get-tuple-element.407, f32[64,256,128]{1,0,2:T(8,128)} %copy.61, s32[64]{0:T(128)S(1)} %bitcast.131), kind=kOutput, calls=%fused_computation.8.clone.1 | convolution fusion | flops 1612713984 | bytes 25166080 | tf_op jit(solution)/shard_map/while/body/dot_general | solution.py:104
  76.5 4.9 %slice.50 = bf16[32,256,256]{2,1,0:T(8,128)(2,1)} slice(bf16[32,272,256]{2,1,0:T(8,128)(2,1)} %all-to-all-done), slice={[0:32], [0:256], [0:256]} | slice | bytes 8388608 | tf_op jit(solution)/shard_map/slice | solution.py:88
  82.7 4.5 %copy.54 = bf16[64,128,256]{2,1,0:T(8,128)(2,1)S(1)} copy(f32[64,128,256]{2,0,1:T(8,128)S(1)} %copy-done.1) | data formatting | bytes 12582912 | tf_op jit(solution)/shard_map/optimization_barrier | solution.py:110
  87.2 2.3 pad_maximum_fusion.1
  89.5 7.4 %all-to-all-start.1 = ((bf16[32,272,256]{2,1,0:T(8,128)(2,1)}), bf16[32,272,256]{2,1,0:T(8,128)(2,1)}, u32[]{:S(2)}, u32[]{:S(2)}) async-start(bf16[32,272,256]{2,1,0:T(8,128)(2,1)} %pad_maximum_fusion.1), calls=%async_computation.1 | async-start | bytes 8912896 | tf_op jit(solution)/shard_map/all_to_all | solution.py:117
  96.9 5.1 %gather_fusion.1 = bf16[64,128,256]{2,1,0:T(8,128)(2,1)} fusion(bf16[64,128,256]{2,1,0:T(8,128)(2,1)} %bitcast.117, s32[1024]{0:T(1024)S(1)} %pad_clamp_fusion), kind=kCustom, calls=%fused_computation.1 | custom fusion | bytes 8388864 | tf_op jit(solution)/shard_map/while/body/gather | solution.py:125
  102.0 2.4 broadcast_in_dim.33
  104.4 15.3 %while.25 = (s32[]{:T(128)}, f32[32,128,256]{2,0,1:T(8,128)}, s32[]{:T(128)}, s32[1,1,64]{2,1,0:T(1,128)S(1)}, s32[]{:T(128)}, /*index=5*/f32[64,8]{0,1:T(8,128)...) while((s32[]{:T(128)}, f32[32,128,256]{2,0,1:T(8,128)}, ...), condition=%wide.region_4.5_spmd, body=%wide.region_3.4_spmd.sunk | while | flops 1343228672 | bytes 31462264 | solution.py:135
  105.1 3.4 %fusion.91 = f32[64,128,256]{2,1,0:T(8,128)S(1)} fusion(bf16[64,128,128]{2,1,0:T(8,128)(2,1)S(1)} %get-tuple-element.454, bf16[64,128,256]{2,1,0:T(8,128)(2,1)} %get-tuple-element.455), kind=kOutput, calls=%fused_computation.66.clone.1 | convolution fusion | flops 536870912 | bytes 14680064 | tf_op jit(solution)/shard_map/while/body/tij,tjf->tif/dot_general | solution.py:126
  108.6 11.0 %fusion.93 = f32[32,128,256]{2,0,1:T(8,128)} fusion(f32[32,128,256]{2,0,1:T(8,128)} %get-tuple-element.439, f32[64,128,256]{2,1,0:T(8,128)S(1)} %fusion.91, f32[64,8]{0,1:T(8,128)S(1)} %get-tuple-element.453, f32[64,4]{0,1:T(4,128)S(1)} %fusion.92), kind=kOutput, calls=%fused_computation.21.clone.1 | convolution fusion | flops 806356992 | bytes 16780288 | tf_op jit(solution)/shard_map/while/body/dot_general | solution.py:130
  119.8 8.6 %fusion.32 = f32[8,256,256]{2,1,0:T(8,128)} fusion(bf16[4,128,256,1]{2,1,0,3:T(8,128)(2,1)S(1)} %bitcast.123, f32[4,8,128,256]{3,1,0,2:T(8,128)} %bitcast.28), kind=kOutput, calls=%fused_computation.39 | convolution fusion | flops 3221225472 | bytes 6553600 | tf_op jit(solution)/shard_map/lbnf,lng->bfg/dot_general | solution.py:141
  128.4 6.4 %fusion.35 = f32[4,128,256]{2,1,0:T(8,128)S(1)} fusion(f32[4,8,128,256]{3,1,0,2:T(8,128)} %bitcast.28, bf16[8,256,256]{2,1,0:T(8,128)(2,1)S(1)} %copy-done), kind=kOutput, calls=%fused_computation.40 | convolution fusion | flops 3221225472 | bytes 5767168 | tf_op jit(solution)/shard_map/lbnf,bfg->lng/dot_general | solution.py:140
  134.8 17.3 %all-to-all-done.1 = bf16[32,272,256]{2,1,0:T(8,128)(2,1)} async-done(((bf16[32,272,256]{2,1,0:T(8,128)(2,1)}), bf16[32,272,256]{2,1,0:T(8,128)(2,1)}, u32[]{:S(2)}, u32[]{:S(2)}) %all-to-all-start.1) | async-done | bytes 4456480 | tf_op jit(solution)/shard_map/all_to_all | solution.py:117
  152.1 2.5 slice.53
  154.6 2.6 fusion.26
  157.4 18.3 %all_to_all.30 = f32[4,256,256]{2,1,0:T(8,128)} all-to-all(f32[4,256,256]{2,1,0:T(8,128)S(1)} %bitcast.121), channel_id=1, replica_groups=mesh['rows'=32,'rel'=4] {'rel'}, dimensions={0} | all-to-all | bytes 2097152 | tf_op jit(solution)/shard_map/all_to_all | solution.py:16
  175.7 8.1 %all-to-all-start.4 = ((f32[128,16,256]{2,1,0:T(8,128)}), f32[128,16,256]{2,1,0:T(8,128)S(1)}, u32[]{:S(2)}, u32[]{:S(2)}) async-start(f32[128,16,256]{2,1,0:T(8,128)} %bitcast.41), calls=%async_computation.4 | async-start | bytes 4194304 | tf_op jit(solution)/shard_map/all_to_all | solution.py:16
  185.1 29.6 %all-to-all-done.4 = f32[128,16,256]{2,1,0:T(8,128)S(1)} async-done(((f32[128,16,256]{2,1,0:T(8,128)}), f32[128,16,256]{2,1,0:T(8,128)S(1)}, u32[]{:S(2)}, u32[]{:S(2)}) %all-to-all-start.4) | async-done | bytes 2097184 | tf_op jit(solution)/shard_map/all_to_all | solution.py:16
  215.8 4.2 %all-to-all-start.3 = ((f32[4,256,256]{2,1,0:T(8,128)}), f32[4,256,256]{2,1,0:T(8,128)}, u32[]{:S(2)}, u32[]{:S(2)}) async-start(f32[4,256,256]{2,1,0:T(8,128)} %broadcast_in_dim.34), calls=%async_computation.3 | async-start | bytes 2097152 | tf_op jit(solution)/shard_map/all_to_all | solution.py:18
  220.3 14.9 %all-to-all-done.3 = f32[4,256,256]{2,1,0:T(8,128)} async-done(((f32[4,256,256]{2,1,0:T(8,128)}), f32[4,256,256]{2,1,0:T(8,128)}, u32[]{:S(2)}, u32[]{:S(2)}) %all-to-all-start.3) | async-done | bytes 1048608 | tf_op jit(solution)/shard_map/all_to_all | solution.py:18
  236.8 4.4 %all-to-all-start.5 = ((f32[128,16,256]{2,1,0:T(8,128)}), f32[128,16,256]{2,1,0:T(8,128)S(1)}, u32[]{:S(2)}, u32[]{:S(2)}) async-start(f32[128,16,256]{2,1,0:T(8,128)} %broadcast_in_dim.35), calls=%async_computation.5 | async-start | bytes 4194304 | tf_op jit(solution)/shard_map/all_to_all | solution.py:18
  247.2 25.2 %all-to-all-done.5 = f32[128,16,256]{2,1,0:T(8,128)S(1)} async-done(((f32[128,16,256]{2,1,0:T(8,128)}), f32[128,16,256]{2,1,0:T(8,128)S(1)}, u32[]{:S(2)}, u32[]{:S(2)}) %all-to-all-start.5) | async-done | bytes 2097184 | tf_op jit(solution)/shard_map/all_to_all | solution.py:18
  (54 shorter events, 16.9 us)
Async XLA Ops:
  0.6 20.1 %copy-start = (bf16[8,256,256]{2,1,0:T(8,128)(2,1)S(1)}, bf16[8,256,256]{2,1,0:T(8,128)(2,1)}, u32[]{:S(2)}) copy-start(bf16[8,256,256]{2,1,0:T(8,128)(2,1)} %param.16) | copy-start | bytes 3145732
  10.5 10.3 %copy-start.4 = (bf16[512,256]{1,0:T(8,128)(2,1)S(1)}, bf16[512,256]{1,0:T(8,128)(2,1)}, u32[]{:S(2)}) copy-start(bf16[512,256]{1,0:T(8,128)(2,1)} %param.25) | copy-start | bytes 786436
  10.5 66.0 %all-to-all-start = ((bf16[32,272,256]{2,1,0:T(8,128)(2,1)}), bf16[32,272,256]{2,1,0:T(8,128)(2,1)}, u32[]{:S(2)}, u32[]{:S(2)}) async-start(bf16[32,272,256]{2,1,0:T(8,128)(2,1)} %pad_maximum_fusion), calls=%async_computation | async-start | bytes 8912896 | tf_op jit(solution)/shard_map/all_to_all | solution.py:85
  23.5 5.4 %copy-start.10 = (f32[200,8]{0,1:T(8,128)S(1)}, f32[200,8]{0,1:T(8,128)}, u32[]{:S(2)}) copy-start(f32[200,8]{0,1:T(8,128)} %param.18) | copy-start | bytes 19204
  23.5 5.4 %copy-start.11 = (s32[1,1,64]{2,1,0:T(1,128)S(1)}, s32[1,1,64]{2,1,0:T(1,128)}, u32[]{:S(2)}) copy-start(s32[1,1,64]{2,1,0:T(1,128)} %param.22) | copy-start | bytes 772
  29.1 4.3 %copy-start.2 = (bf16[1,1,64,128,128]{4,3,2,1,0:T(8,128)(2,1)S(1)}, bf16[1,1,64,128,128]{4,3,2,1,0:T(8,128)(2,1)}, u32[]{:S(2)}) copy-start(bf16[1,1,64,128,128]{4,3,2,1,0:T(8,128)(2,1)} %param.19) | copy-start | bytes 6291460
  29.1 4.3 %copy-start.7 = (s32[1,1,64]{2,1,0:T(1,128)S(1)}, s32[1,1,64]{2,1,0:T(1,128)}, u32[]{:S(2)}) copy-start(s32[1,1,64]{2,1,0:T(1,128)} %param.20) | copy-start | bytes 772
  29.1 4.3 %copy-start.8 = (s32[1,1,64]{2,1,0:T(1,128)S(1)}, s32[1,1,64]{2,1,0:T(1,128)}, u32[]{:S(2)}) copy-start(s32[1,1,64]{2,1,0:T(1,128)} %param.21) | copy-start | bytes 772
  33.4 42.9 %copy-start.9 = (s32[1,1,32,2]{2,3,1,0:T(2,128)S(1)}, s32[1,1,32,2]{2,3,1,0:T(2,128)}, u32[]{:S(2)}) copy-start(s32[1,1,32,2]{2,3,1,0:T(2,128)} %param.24) | copy-start | bytes 772
  76.5 6.2 %copy-start.1 = (f32[64,128,256]{2,0,1:T(8,128)S(1)}, f32[64,128,256]{2,0,1:T(8,128)}, u32[]{:S(2)}) copy-start(f32[64,128,256]{2,0,1:T(8,128)} %get-tuple-element.242) | copy-start | bytes 25165828
  89.5 62.7 %all-to-all-start.1 = ((bf16[32,272,256]{2,1,0:T(8,128)(2,1)}), bf16[32,272,256]{2,1,0:T(8,128)(2,1)}, u32[]{:S(2)}, u32[]{:S(2)}) async-start(bf16[32,272,256]{2,1,0:T(8,128)(2,1)} %pad_maximum_fusion.1), calls=%async_computation.1 | async-start | bytes 8912896 | tf_op jit(solution)/shard_map/all_to_all | solution.py:117
  104.4 15.3 %copy-start.5 = (bf16[512,256]{1,0:T(8,128)(2,1)S(1)}, bf16[512,256]{1,0:T(8,128)(2,1)}, u32[]{:S(2)}) copy-start(bf16[512,256]{1,0:T(8,128)(2,1)} %param.25) | copy-start | bytes 786436
  175.7 39.1 %all-to-all-start.4 = ((f32[128,16,256]{2,1,0:T(8,128)}), f32[128,16,256]{2,1,0:T(8,128)S(1)}, u32[]{:S(2)}, u32[]{:S(2)}) async-start(f32[128,16,256]{2,1,0:T(8,128)} %bitcast.41), calls=%async_computation.4 | async-start | bytes 4194304 | tf_op jit(solution)/shard_map/all_to_all | solution.py:16
  215.8 19.4 %all-to-all-start.3 = ((f32[4,256,256]{2,1,0:T(8,128)}), f32[4,256,256]{2,1,0:T(8,128)}, u32[]{:S(2)}, u32[]{:S(2)}) async-start(f32[4,256,256]{2,1,0:T(8,128)} %broadcast_in_dim.34), calls=%async_computation.3 | async-start | bytes 2097152 | tf_op jit(solution)/shard_map/all_to_all | solution.py:18
  220.3 23.9 %copy-start.3 = (bf16[512,256]{1,0:T(8,128)(2,1)S(1)}, bf16[512,256]{1,0:T(8,128)(2,1)}, u32[]{:S(2)}) copy-start(bf16[512,256]{1,0:T(8,128)(2,1)} %param.15) | copy-start | bytes 786436
  220.3 24.0 %copy-start.6 = (bf16[256,256]{1,0:T(8,128)(2,1)S(1)}, bf16[256,256]{1,0:T(8,128)(2,1)}, u32[]{:S(2)}) copy-start(bf16[256,256]{1,0:T(8,128)(2,1)} %param.17) | copy-start | bytes 393220
  236.8 35.6 %all-to-all-start.5 = ((f32[128,16,256]{2,1,0:T(8,128)}), f32[128,16,256]{2,1,0:T(8,128)S(1)}, u32[]{:S(2)}, u32[]{:S(2)}) async-start(f32[128,16,256]{2,1,0:T(8,128)} %broadcast_in_dim.35), calls=%async_computation.5 | async-start | bytes 4194304 | tf_op jit(solution)/shard_map/all_to_all | solution.py:18

commit v5 on v4

--- a/solution.py
+++ b/solution.py
@@ -20,7 +20,7 @@
 
 
 def split_hi_lo(value):
-    high = value.astype(jnp.bfloat16)
+    high = lax.optimization_barrier(value.astype(jnp.bfloat16))
     low = (value - high.astype(jnp.float32)).astype(jnp.bfloat16)
     return jnp.concatenate([high, low], axis=1)
 

time: 278 us -> 277 us (level)
  no operation moved by 1% of the time
where the time goes in v5:
time: 277 us; the launch traced here: 273 us
  waiting for transfers between devices  87 us (31%)
  matrix products  71.6 us (26%)
  local copies, waits for them, and re-layouts  46.8 us (17%)
  starting transfers between devices  33.8 us (12%)
  blocking collectives  18.3 us (7%)
  other arithmetic  12.7 us (5%)
    all_to_all x2, waiting for transfers between devices, a2a_psum(): lax.all_to_all(jnp.broadcast_to(reduced, chunked.shape), axes, 0, 0, tile...  40.1 us
    all_to_all x1, waiting for transfers between devices, a2a_psum(): pieces = lax.all_to_all(chunked, axes, 0, 0, tiled=True)  29.6 us
    all_to_all x1, blocking collectives, a2a_psum(): pieces = lax.all_to_all(chunked, axes, 0, 0, tiled=True)  18.3 us
    all_to_all x1, waiting for transfers between devices, on_device(): lax.all_to_all(slot_out, 'rows', split_axis=0, concat_axis=0, tiled=True)  17.3 us
    dot_general x1, matrix products, backward_step(): lax.dot_general(slot_hot, backward_term, contract_first, precision=highest)  14.2 us
    dot_general x1, matrix products, backward_step(): lax.dot_general(weights, agg_grad, (((1,), (0,)), ((), ())), precision=hi...  11.5 us
    dot_general x1, matrix products, forward_step(): lax.dot_general(weights, messages, contract_first, precision=highest)  11 us
    all_to_all x1, starting transfers between devices, on_device(): lax.all_to_all(outgoing, 'rows', split_axis=0, concat_axis=0, tiled=True)  9.6 us
  transfers between devices with their start and end apart: 5, of which 4 were waited for; matrix products, arithmetic and copies ran while one was open for 37% of the time, Pallas kernels for 0%

profile of v5, /device:TPU:1, one launch (start us, length us, event | category | flops | bytes accessed | tf_op | source)
XLA Modules:
  0.0 273.0 jit_solution(18151571829817244651)
XLA Ops:
  3.0 2.8 %gather_fusion = bf16[64,128,256]{2,1,0:T(8,128)(2,1)} fusion(bf16[4,128,256]{2,1,0:T(8,128)(2,1)S(1)} %bitcast.111, s32[1024]{0:T(1024)S(1)} %pad_clamp_fusion.1), kind=kCustom, calls=%fused_computation | custom fusion | bytes 8388864 | tf_op jit(solution)/shard_map/gather | solution.py:83
  5.8 3.8 %pad_maximum_fusion = bf16[32,272,256]{2,1,0:T(8,128)(2,1)} fusion(bf16[32,8,256]{2,1,0:T(8,128)(2,1)S(1)} %subtract_convert_fusion.1, bf16[32,8,256]{2,1,0:T(8,128)(2,1)S(1)} %get-tuple-element.285, bf16[32,256,256]{2,1,0:T(8,128)(2,1)} %bitcast.114), kind=kLoop, calls=%fused_computation.30 | loop fusion | flops 13369344 | bytes 8912896 | tf_op jit(solution)/shard_map/concatenate | solution.py:84
  9.6 9.6 %all-to-all-start = ((bf16[32,272,256]{2,1,0:T(8,128)(2,1)}), bf16[32,272,256]{2,1,0:T(8,128)(2,1)}, u32[]{:S(2)}, u32[]{:S(2)}) async-start(bf16[32,272,256]{2,1,0:T(8,128)(2,1)} %pad_maximum_fusion), calls=%async_computation | async-start | bytes 8912896 | tf_op jit(solution)/shard_map/all_to_all | solution.py:85
  19.9 2.7 convolution_bitcast_fusion
  22.6 5.4 %copy.21 = f32[4,8,128,256]{3,2,1,0:T(8,128)} copy(f32[4,8,128,256]{2,3,0,1:T(8,128)} %convolution_bitcast_fusion) | data formatting | bytes 8388608 | tf_op jit(solution)/shard_map/lng,bfg->lbnf/transpose | solution.py:91
  28.2 4.3 %broadcast_in_dim.22 = f32[64,128,256]{2,0,1:T(8,128)} broadcast(f32[]{:T(128)} %constant.53.clone.1), dimensions={} | broadcast | bytes 8388612 | tf_op jit(solution)/shard_map/broadcast_in_dim | solution.py:108
  32.5 42.8 %while.24 = (s32[]{:T(128)}, f32[64,128,256]{2,0,1:T(8,128)}, s32[]{:T(128)}, s32[1,1,64]{2,1,0:T(1,128)S(1)}, s32[1,1,64]{2,1,0:T(1,128)S(1)}, /*index=5*/s32[]...) while((s32[]{:T(128)}, f32[64,128,256]{2,0,1:T(8,128)}, ...), condition=%wide.region_1.2_spmd, body=%wide.region_0.1_spmd.sunk | while | flops 2954894080 | bytes 65016960 | solution.py:109
  33.7 11.5 %fusion.84 = bf16[64,128,256]{2,0,1:T(8,128)(2,1)S(1)} fusion(f32[32,128,256]{2,1,0:T(8,128)} %get-tuple-element.422, f32[64,8]{0,1:T(8,128)S(1)} %get-tuple-element.421, f32[64,4]{0,1:T(4,128)S(1)} %fusion.83), kind=kOutput, calls=%fused_computation.6.clone.1 | convolution fusion | flops 805308416 | bytes 8391680 | tf_op jit(solution)/shard_map/while/body/dot_general | solution.py:97
  45.2 6.6 %fusion.85 = f32[64,256,128]{2,1,0:T(8,128)} fusion(bf16[64,128,128]{2,1,0:T(8,128)(2,1)S(1)} %get-tuple-element.423, bf16[64,128,256]{2,0,1:T(8,128)(2,1)S(1)} %fusion.84), kind=kOutput, calls=%fused_computation.5.clone.1 | convolution fusion | flops 536870912 | bytes 14680064 | tf_op jit(solution)/shard_map/while/body/tij,tif->tjf/dot_general | solution.py:100
  51.8 9.2 %copy.61 = f32[64,256,128]{1,0,2:T(8,128)} copy(f32[64,256,128]{2,1,0:T(8,128)} %fusion.85) | data formatting | bytes 16777216 | tf_op jit(solution)/shard_map/while/body/tij,tif->tjf/dot_general | solution.py:100
  61.0 14.2 %fusion.86 = f32[64,128,256]{2,0,1:T(8,128)} fusion(f32[64,128,256]{2,0,1:T(8,128)} %get-tuple-element.405, f32[64,256,128]{1,0,2:T(8,128)} %copy.61, s32[64]{0:T(128)S(1)} %bitcast.127), kind=kOutput, calls=%fused_computation.8.clone.1 | convolution fusion | flops 1612713984 | bytes 25166080 | tf_op jit(solution)/shard_map/while/body/dot_general | solution.py:104
  75.6 4.9 %slice.50 = bf16[32,256,256]{2,1,0:T(8,128)(2,1)} slice(bf16[32,272,256]{2,1,0:T(8,128)(2,1)} %all-to-all-done), slice={[0:32], [0:256], [0:256]} | slice | bytes 8388608 | tf_op jit(solution)/shard_map/slice | solution.py:88
  81.8 4.5 %copy.54 = bf16[64,128,256]{2,1,0:T(8,128)(2,1)S(1)} copy(f32[64,128,256]{2,0,1:T(8,128)S(1)} %copy-done.1) | data formatting | bytes 12582912 | tf_op jit(solution)/shard_map/optimization_barrier | solution.py:110
  86.3 2.3 pad_maximum_fusion.1
  88.6 7.4 %all-to-all-start.1 = ((bf16[32,272,256]{2,1,0:T(8,128)(2,1)}), bf16[32,272,256]{2,1,0:T(8,128)(2,1)}, u32[]{:S(2)}, u32[]{:S(2)}) async-start(bf16[32,272,256]{2,1,0:T(8,128)(2,1)} %pad_maximum_fusion.1), calls=%async_computation.1 | async-start | bytes 8912896 | tf_op jit(solution)/shard_map/all_to_all | solution.py:117
  96.0 5.1 %gather_fusion.1 = bf16[64,128,256]{2,1,0:T(8,128)(2,1)} fusion(bf16[64,128,256]{2,1,0:T(8,128)(2,1)} %bitcast.113, s32[1024]{0:T(1024)S(1)} %pad_clamp_fusion), kind=kCustom, calls=%fused_computation.1 | custom fusion | bytes 8388864 | tf_op jit(solution)/shard_map/while/body/gather | solution.py:125
  101.1 2.4 broadcast_in_dim.33
  103.5 15.3 %while.25 = (s32[]{:T(128)}, f32[32,128,256]{2,0,1:T(8,128)}, s32[]{:T(128)}, s32[1,1,64]{2,1,0:T(1,128)S(1)}, s32[]{:T(128)}, /*index=5*/f32[64,8]{0,1:T(8,128)...) while((s32[]{:T(128)}, f32[32,128,256]{2,0,1:T(8,128)}, ...), condition=%wide.region_4.5_spmd, body=%wide.region_3.4_spmd.sunk | while | flops 1343228672 | bytes 31462264 | solution.py:135
  104.3 3.4 %fusion.91 = f32[64,128,256]{2,1,0:T(8,128)S(1)} fusion(bf16[64,128,128]{2,1,0:T(8,128)(2,1)S(1)} %get-tuple-element.452, bf16[64,128,256]{2,1,0:T(8,128)(2,1)} %get-tuple-element.453), kind=kOutput, calls=%fused_computation.66.clone.1 | convolution fusion | flops 536870912 | bytes 14680064 | tf_op jit(solution)/shard_map/while/body/tij,tjf->tif/dot_general | solution.py:126
  107.7 11.0 %fusion.93 = f32[32,128,256]{2,0,1:T(8,128)} fusion(f32[32,128,256]{2,0,1:T(8,128)} %get-tuple-element.437, f32[64,128,256]{2,1,0:T(8,128)S(1)} %fusion.91, f32[64,8]{0,1:T(8,128)S(1)} %get-tuple-element.451, f32[64,4]{0,1:T(4,128)S(1)} %fusion.92), kind=kOutput, calls=%fused_computation.21.clone.1 | convolution fusion | flops 806356992 | bytes 16780288 | tf_op jit(solution)/shard_map/while/body/dot_general | solution.py:130
  118.9 8.6 %fusion.32 = f32[8,256,256]{2,1,0:T(8,128)} fusion(bf16[4,128,256,1]{2,1,0,3:T(8,128)(2,1)S(1)} %bitcast.119, f32[4,8,128,256]{3,1,0,2:T(8,128)} %bitcast.28), kind=kOutput, calls=%fused_computation.39 | convolution fusion | flops 3221225472 | bytes 6553600 | tf_op jit(solution)/shard_map/lbnf,lng->bfg/dot_general | solution.py:141
  127.5 6.4 %fusion.35 = f32[4,128,256]{2,1,0:T(8,128)S(1)} fusion(f32[4,8,128,256]{3,1,0,2:T(8,128)} %bitcast.28, bf16[8,256,256]{2,1,0:T(8,128)(2,1)S(1)} %copy-done), kind=kOutput, calls=%fused_computation.40 | convolution fusion | flops 3221225472 | bytes 5767168 | tf_op jit(solution)/shard_map/lbnf,bfg->lng/dot_general | solution.py:140
  133.9 17.3 %all-to-all-done.1 = bf16[32,272,256]{2,1,0:T(8,128)(2,1)} async-done(((bf16[32,272,256]{2,1,0:T(8,128)(2,1)}), bf16[32,272,256]{2,1,0:T(8,128)(2,1)}, u32[]{:S(2)}, u32[]{:S(2)}) %all-to-all-start.1) | async-done | bytes 4456480 | tf_op jit(solution)/shard_map/all_to_all | solution.py:117
  151.3 2.5 slice.53
  153.7 2.6 fusion.26
  156.5 18.3 %all_to_all.30 = f32[4,256,256]{2,1,0:T(8,128)} all-to-all(f32[4,256,256]{2,1,0:T(8,128)S(1)} %bitcast.117), channel_id=1, replica_groups=mesh['rows'=32,'rel'=4] {'rel'}, dimensions={0} | all-to-all | bytes 2097152 | tf_op jit(solution)/shard_map/all_to_all | solution.py:16
  174.8 8.1 %all-to-all-start.4 = ((f32[128,16,256]{2,1,0:T(8,128)}), f32[128,16,256]{2,1,0:T(8,128)S(1)}, u32[]{:S(2)}, u32[]{:S(2)}) async-start(f32[128,16,256]{2,1,0:T(8,128)} %bitcast.41), calls=%async_computation.4 | async-start | bytes 4194304 | tf_op jit(solution)/shard_map/all_to_all | solution.py:16
  184.3 29.6 %all-to-all-done.4 = f32[128,16,256]{2,1,0:T(8,128)S(1)} async-done(((f32[128,16,256]{2,1,0:T(8,128)}), f32[128,16,256]{2,1,0:T(8,128)S(1)}, u32[]{:S(2)}, u32[]{:S(2)}) %all-to-all-start.4) | async-done | bytes 2097184 | tf_op jit(solution)/shard_map/all_to_all | solution.py:16
  214.9 4.2 %all-to-all-start.3 = ((f32[4,256,256]{2,1,0:T(8,128)}), f32[4,256,256]{2,1,0:T(8,128)}, u32[]{:S(2)}, u32[]{:S(2)}) async-start(f32[4,256,256]{2,1,0:T(8,128)} %broadcast_in_dim.34), calls=%async_computation.3 | async-start | bytes 2097152 | tf_op jit(solution)/shard_map/all_to_all | solution.py:18
  219.4 14.9 %all-to-all-done.3 = f32[4,256,256]{2,1,0:T(8,128)} async-done(((f32[4,256,256]{2,1,0:T(8,128)}), f32[4,256,256]{2,1,0:T(8,128)}, u32[]{:S(2)}, u32[]{:S(2)}) %all-to-all-start.3) | async-done | bytes 1048608 | tf_op jit(solution)/shard_map/all_to_all | solution.py:18
  235.9 4.4 %all-to-all-start.5 = ((f32[128,16,256]{2,1,0:T(8,128)}), f32[128,16,256]{2,1,0:T(8,128)S(1)}, u32[]{:S(2)}, u32[]{:S(2)}) async-start(f32[128,16,256]{2,1,0:T(8,128)} %broadcast_in_dim.35), calls=%async_computation.5 | async-start | bytes 4194304 | tf_op jit(solution)/shard_map/all_to_all | solution.py:18
  246.3 25.2 %all-to-all-done.5 = f32[128,16,256]{2,1,0:T(8,128)S(1)} async-done(((f32[128,16,256]{2,1,0:T(8,128)}), f32[128,16,256]{2,1,0:T(8,128)S(1)}, u32[]{:S(2)}, u32[]{:S(2)}) %all-to-all-start.5) | async-done | bytes 2097184 | tf_op jit(solution)/shard_map/all_to_all | solution.py:18
  (57 shorter events, 17.0 us)
Async XLA Ops:
  0.6 19.2 %copy-start = (bf16[8,256,256]{2,1,0:T(8,128)(2,1)S(1)}, bf16[8,256,256]{2,1,0:T(8,128)(2,1)}, u32[]{:S(2)}) copy-start(bf16[8,256,256]{2,1,0:T(8,128)(2,1)} %param.16) | copy-start | bytes 3145732
  0.6 2.3 copy-start.3
  9.6 10.3 %copy-start.5 = (bf16[512,256]{1,0:T(8,128)(2,1)S(1)}, bf16[512,256]{1,0:T(8,128)(2,1)}, u32[]{:S(2)}) copy-start(bf16[512,256]{1,0:T(8,128)(2,1)} %param.25) | copy-start | bytes 786436
  9.6 66.0 %all-to-all-start = ((bf16[32,272,256]{2,1,0:T(8,128)(2,1)}), bf16[32,272,256]{2,1,0:T(8,128)(2,1)}, u32[]{:S(2)}, u32[]{:S(2)}) async-start(bf16[32,272,256]{2,1,0:T(8,128)(2,1)} %pad_maximum_fusion), calls=%async_computation | async-start | bytes 8912896 | tf_op jit(solution)/shard_map/all_to_all | solution.py:85
  22.6 5.4 %copy-start.11 = (f32[200,8]{0,1:T(8,128)S(1)}, f32[200,8]{0,1:T(8,128)}, u32[]{:S(2)}) copy-start(f32[200,8]{0,1:T(8,128)} %param.18) | copy-start | bytes 19204
  22.6 5.4 %copy-start.12 = (s32[1,1,64]{2,1,0:T(1,128)S(1)}, s32[1,1,64]{2,1,0:T(1,128)}, u32[]{:S(2)}) copy-start(s32[1,1,64]{2,1,0:T(1,128)} %param.22) | copy-start | bytes 772
  28.2 4.3 %copy-start.2 = (bf16[1,1,64,128,128]{4,3,2,1,0:T(8,128)(2,1)S(1)}, bf16[1,1,64,128,128]{4,3,2,1,0:T(8,128)(2,1)}, u32[]{:S(2)}) copy-start(bf16[1,1,64,128,128]{4,3,2,1,0:T(8,128)(2,1)} %param.19) | copy-start | bytes 6291460
  28.2 4.3 %copy-start.8 = (s32[1,1,64]{2,1,0:T(1,128)S(1)}, s32[1,1,64]{2,1,0:T(1,128)}, u32[]{:S(2)}) copy-start(s32[1,1,64]{2,1,0:T(1,128)} %param.20) | copy-start | bytes 772
  28.2 4.3 %copy-start.9 = (s32[1,1,64]{2,1,0:T(1,128)S(1)}, s32[1,1,64]{2,1,0:T(1,128)}, u32[]{:S(2)}) copy-start(s32[1,1,64]{2,1,0:T(1,128)} %param.21) | copy-start | bytes 772
  32.5 42.9 %copy-start.10 = (s32[1,1,32,2]{2,3,1,0:T(2,128)S(1)}, s32[1,1,32,2]{2,3,1,0:T(2,128)}, u32[]{:S(2)}) copy-start(s32[1,1,32,2]{2,3,1,0:T(2,128)} %param.24) | copy-start | bytes 772
  75.6 6.2 %copy-start.1 = (f32[64,128,256]{2,0,1:T(8,128)S(1)}, f32[64,128,256]{2,0,1:T(8,128)}, u32[]{:S(2)}) copy-start(f32[64,128,256]{2,0,1:T(8,128)} %get-tuple-element.242) | copy-start | bytes 25165828
  88.6 62.7 %all-to-all-start.1 = ((bf16[32,272,256]{2,1,0:T(8,128)(2,1)}), bf16[32,272,256]{2,1,0:T(8,128)(2,1)}, u32[]{:S(2)}, u32[]{:S(2)}) async-start(bf16[32,272,256]{2,1,0:T(8,128)(2,1)} %pad_maximum_fusion.1), calls=%async_computation.1 | async-start | bytes 8912896 | tf_op jit(solution)/shard_map/all_to_all | solution.py:117
  103.5 15.3 %copy-start.6 = (bf16[512,256]{1,0:T(8,128)(2,1)S(1)}, bf16[512,256]{1,0:T(8,128)(2,1)}, u32[]{:S(2)}) copy-start(bf16[512,256]{1,0:T(8,128)(2,1)} %param.25) | copy-start | bytes 786436
  174.8 39.1 %all-to-all-start.4 = ((f32[128,16,256]{2,1,0:T(8,128)}), f32[128,16,256]{2,1,0:T(8,128)S(1)}, u32[]{:S(2)}, u32[]{:S(2)}) async-start(f32[128,16,256]{2,1,0:T(8,128)} %bitcast.41), calls=%async_computation.4 | async-start | bytes 4194304 | tf_op jit(solution)/shard_map/all_to_all | solution.py:16
  214.9 19.4 %all-to-all-start.3 = ((f32[4,256,256]{2,1,0:T(8,128)}), f32[4,256,256]{2,1,0:T(8,128)}, u32[]{:S(2)}, u32[]{:S(2)}) async-start(f32[4,256,256]{2,1,0:T(8,128)} %broadcast_in_dim.34), calls=%async_computation.3 | async-start | bytes 2097152 | tf_op jit(solution)/shard_map/all_to_all | solution.py:18
  219.4 23.9 %copy-start.4 = (bf16[512,256]{1,0:T(8,128)(2,1)S(1)}, bf16[512,256]{1,0:T(8,128)(2,1)}, u32[]{:S(2)}) copy-start(bf16[512,256]{1,0:T(8,128)(2,1)} %param.15) | copy-start | bytes 786436
  219.4 24.0 %copy-start.7 = (bf16[256,256]{1,0:T(8,128)(2,1)S(1)}, bf16[256,256]{1,0:T(8,128)(2,1)}, u32[]{:S(2)}) copy-start(bf16[256,256]{1,0:T(8,128)(2,1)} %param.17) | copy-start | bytes 393220
  235.9 35.6 %all-to-all-start.5 = ((f32[128,16,256]{2,1,0:T(8,128)}), f32[128,16,256]{2,1,0:T(8,128)S(1)}, u32[]{:S(2)}, u32[]{:S(2)}) async-start(f32[128,16,256]{2,1,0:T(8,128)} %broadcast_in_dim.35), calls=%async_computation.5 | async-start | bytes 4194304 | tf_op jit(solution)/shard_map/all_to_all | solution.py:18

commit v6 on v5

--- a/solution.py
+++ b/solution.py
@@ -17,6 +17,36 @@
     reduced = jnp.sum(pieces, axis=0, keepdims=True)
     gathered = lax.all_to_all(jnp.broadcast_to(reduced, chunked.shape), axes, 0, 0, tiled=True)
     return gathered.reshape(value.shape)
+
+
+def pair_psum(value):
+    rows_n = lax.axis_size("rows")
+    rel_n = lax.axis_size("rel")
+    count = rows_n * rel_n
+    swap = [(index, index ^ 1) for index in range(rows_n)]
+    core = lax.axis_index("rows") % 2
+    half = value.shape[0] // 2
+    first, second = value[:half], value[half:]
+    kept = jnp.where(core == 0, first, second)
+    given = jnp.where(core == 0, second, first)
+    chip_sum = kept + lax.ppermute(given, "rows", swap)
+    pieces = lax.all_to_all(
+        chip_sum.reshape((count, half // count) + value.shape[1:]), ("rows", "rel"), 0, 0, tiled=True
+    )
+    pieces = pieces.reshape((rows_n // 2, 2, rel_n, half // count) + value.shape[1:])
+    reduced = jnp.sum(pieces, axis=(0, 2))
+    outgoing = jnp.broadcast_to(reduced[None, :, None], pieces.shape).reshape(
+        (count, half // count) + value.shape[1:]
+    )
+    own_half = lax.all_to_all(outgoing, ("rows", "rel"), 0, 0, tiled=True).reshape(
+        (half,) + value.shape[1:]
+    )
+    other_half = lax.ppermute(own_half, "rows", swap)
+    return jnp.where(
+        core == 0,
+        jnp.concatenate([own_half, other_half]),
+        jnp.concatenate([other_half, own_half]),
+    )
 
 
 def split_hi_lo(value):
@@ -143,9 +173,9 @@
         (returned, basis_local, projected_part)
     )
 
-    basis_grad = a2a_psum(
-        basis_local.reshape(-1, basis_local.shape[-1]), ("rows", "rel")
-    ).reshape(basis_local.shape)
+    basis_grad = pair_psum(basis_local.reshape(-1, basis_local.shape[-1])).reshape(
+        basis_local.shape
+    )
 
     block_hot = (send_rows.reshape(-1)[None, :] == jnp.arange(local_blocks)[:, None]).astype(
         jnp.float32

time: 277 us -> 264 us (0.953)
  blocking collectives: 18.3 us -> 0 us
  waiting for transfers between devices: 87 us -> 80.9 us
  starting transfers between devices: 33.8 us -> 38.8 us
  other arithmetic: 12.7 us -> 17.5 us
    all_to_all x0 -> x2, waiting for transfers between devices: none -> 32.8 us  [the longest x1 19.1 us: pair_psum(): lax.all_to_all(outgoing, ('rows', 'rel'), 0, 0, tiled=True)]
    all_to_all x2 -> x1, waiting for transfers between devices: 40.1 us -> 13.1 us  [a2a_psum(): lax.all_to_all(jnp.broadcast_to(reduced, chunked.shape), axes, 0, 0, tile...]
    all_to_all x1 -> x0, blocking collectives: 18.3 us -> none  [a2a_psum(): pieces = lax.all_to_all(chunked, axes, 0, 0, tiled=True)]
    all_to_all x1, waiting for transfers between devices: 29.6 us -> 14.9 us  [a2a_psum(): pieces = lax.all_to_all(chunked, axes, 0, 0, tiled=True)]
    all_to_all x0 -> x2, starting transfers between devices: none -> 13.7 us  [the longest x1 9.31 us: pair_psum(): lax.all_to_all(chip_sum.reshape((count, half // count) + value.shape[1:])...]
    all_to_all x2 -> x1, starting transfers between devices: 8.69 us -> 3.52 us  [a2a_psum(): lax.all_to_all(jnp.broadcast_to(reduced, chunked.shape), axes, 0, 0, tile...]
    all_to_all x1, starting transfers between devices: 8.12 us -> 3.52 us  [a2a_psum(): pieces = lax.all_to_all(chunked, axes, 0, 0, tiled=True)]
    select_n x0 -> x2, other arithmetic: none -> 3.36 us  [the longest x1 3.2 us: pair_psum(): jnp.where(core == 0, jnp.concatenate([own_half, other_half]), jnp.concate...]
  transfers between devices with their start and end apart: 5 -> 8, of which waited for: 4 -> 6; matrix products, arithmetic and copies ran while one was open for 37% -> 40% of each run, Pallas kernels for 0% -> 0%
where the time goes in v6:
time: 264 us; the launch traced here: 260 us
  waiting for transfers between devices  80.9 us (31%)
  matrix products  73 us (28%)
  local copies, waits for them, and re-layouts  47 us (18%)
  starting transfers between devices  38.8 us (15%)
  other arithmetic  17.5 us (7%)
    all_to_all x1, waiting for transfers between devices, pair_psum(): lax.all_to_all(outgoing, ('rows', 'rel'), 0, 0, tiled=True)  19.1 us
    all_to_all x1, waiting for transfers between devices, on_device(): lax.all_to_all(slot_out, 'rows', split_axis=0, concat_axis=0, tiled=True)  17.8 us
    all_to_all x1, waiting for transfers between devices, a2a_psum(): pieces = lax.all_to_all(chunked, axes, 0, 0, tiled=True)  14.9 us
    dot_general x1, matrix products, backward_step(): lax.dot_general(slot_hot, backward_term, contract_first, precision=highest)  14.2 us
    all_to_all x1, waiting for transfers between devices, pair_psum(): lax.all_to_all(chip_sum.reshape((count, half // count) + value.shape[1:])...  13.7 us
    all_to_all x1, waiting for transfers between devices, a2a_psum(): lax.all_to_all(jnp.broadcast_to(reduced, chunked.shape), axes, 0, 0, tile...  13.1 us
    dot_general x1, matrix products, backward_step(): lax.dot_general(weights, agg_grad, (((1,), (0,)), ((), ())), precision=hi...  11.5 us
    dot_general x1, matrix products, forward_step(): lax.dot_general(weights, messages, contract_first, precision=highest)  11 us
  transfers between devices with their start and end apart: 8, of which 6 were waited for; matrix products, arithmetic and copies ran while one was open for 40% of the time, Pallas kernels for 0%

profile of v6, /device:TPU:1, one launch (start us, length us, event | category | flops | bytes accessed | tf_op | source)
XLA Modules:
  0.0 260.0 jit_solution(6363023427512766502)
XLA Ops:
  3.0 2.8 %gather_fusion = bf16[64,128,256]{2,1,0:T(8,128)(2,1)} fusion(bf16[4,128,256]{2,1,0:T(8,128)(2,1)S(1)} %bitcast.117, s32[1024]{0:T(1024)S(1)} %pad_clamp_fusion.1), kind=kCustom, calls=%fused_computation | custom fusion | bytes 8388864 | tf_op jit(solution)/shard_map/gather | solution.py:113
  5.8 3.8 %pad_maximum_fusion = bf16[32,272,256]{2,1,0:T(8,128)(2,1)} fusion(bf16[32,8,256]{2,1,0:T(8,128)(2,1)S(1)} %subtract_convert_fusion.1, bf16[32,8,256]{2,1,0:T(8,128)(2,1)S(1)} %get-tuple-element.287, bf16[32,256,256]{2,1,0:T(8,128)(2,1)} %bitcast.121), kind=kLoop, calls=%fused_computation.30 | loop fusion | flops 13369344 | bytes 8912896 | tf_op jit(solution)/shard_map/concatenate | solution.py:114
  9.5 9.6 %all-to-all-start = ((bf16[32,272,256]{2,1,0:T(8,128)(2,1)}), bf16[32,272,256]{2,1,0:T(8,128)(2,1)}, u32[]{:S(2)}, u32[]{:S(2)}) async-start(bf16[32,272,256]{2,1,0:T(8,128)(2,1)} %pad_maximum_fusion), calls=%async_computation | async-start | bytes 8912896 | tf_op jit(solution)/shard_map/all_to_all | solution.py:115
  19.8 2.7 %convolution_bitcast_fusion = f32[4,8,128,256]{2,3,0,1:T(8,128)} fusion(bf16[4,128,256,1]{2,1,0,3:T(8,128)(2,1)S(1)} %bitcast.127, bf16[8,256,256]{2,1,0:T(8,128)(2,1)S(1)} %copy-done), kind=kOutput, calls=%fused_computation.38 | convolution fusion | flops 536870912 | bytes 5505024 | tf_op jit(solution)/shard_map/lng,bfg->lbnf/dot_general | solution.py:121
  22.5 5.4 %copy.21 = f32[4,8,128,256]{3,2,1,0:T(8,128)} copy(f32[4,8,128,256]{2,3,0,1:T(8,128)} %convolution_bitcast_fusion) | data formatting | bytes 8388608 | tf_op jit(solution)/shard_map/lng,bfg->lbnf/transpose | solution.py:121
  28.1 4.3 %broadcast_in_dim.22 = f32[64,128,256]{2,0,1:T(8,128)} broadcast(f32[]{:T(128)} %constant.67.clone.1), dimensions={} | broadcast | bytes 8388612 | tf_op jit(solution)/shard_map/broadcast_in_dim | solution.py:138
  32.5 42.9 %while.24 = (s32[]{:T(128)}, f32[64,128,256]{2,0,1:T(8,128)}, s32[]{:T(128)}, s32[1,1,64]{2,1,0:T(1,128)S(1)}, s32[1,1,64]{2,1,0:T(1,128)S(1)}, /*index=5*/s32[]...) while((s32[]{:T(128)}, f32[64,128,256]{2,0,1:T(8,128)}, ...), condition=%wide.region_1.2_spmd, body=%wide.region_0.1_spmd.sunk | while | flops 2954894080 | bytes 65016960 | solution.py:139
  33.7 11.5 %fusion.84 = bf16[64,128,256]{2,0,1:T(8,128)(2,1)S(1)} fusion(f32[32,128,256]{2,1,0:T(8,128)} %get-tuple-element.424, f32[64,8]{0,1:T(8,128)S(1)} %get-tuple-element.423, f32[64,4]{0,1:T(4,128)S(1)} %fusion.83), kind=kOutput, calls=%fused_computation.6.clone.1 | convolution fusion | flops 805308416 | bytes 8391680 | tf_op jit(solution)/shard_map/while/body/dot_general | solution.py:127
  45.2 6.6 %fusion.85 = f32[64,256,128]{2,1,0:T(8,128)} fusion(bf16[64,128,128]{2,1,0:T(8,128)(2,1)S(1)} %get-tuple-element.425, bf16[64,128,256]{2,0,1:T(8,128)(2,1)S(1)} %fusion.84), kind=kOutput, calls=%fused_computation.5.clone.1 | convolution fusion | flops 536870912 | bytes 14680064 | tf_op jit(solution)/shard_map/while/body/tij,tif->tjf/dot_general | solution.py:130
  51.7 9.2 %copy.61 = f32[64,256,128]{1,0,2:T(8,128)} copy(f32[64,256,128]{2,1,0:T(8,128)} %fusion.85) | data formatting | bytes 16777216 | tf_op jit(solution)/shard_map/while/body/tij,tif->tjf/dot_general | solution.py:130
  61.0 14.2 %fusion.86 = f32[64,128,256]{2,0,1:T(8,128)} fusion(f32[64,128,256]{2,0,1:T(8,128)} %get-tuple-element.407, f32[64,256,128]{1,0,2:T(8,128)} %copy.61, s32[64]{0:T(128)S(1)} %bitcast.138), kind=kOutput, calls=%fused_computation.8.clone.1 | convolution fusion | flops 1612713984 | bytes 25166080 | tf_op jit(solution)/shard_map/while/body/dot_general | solution.py:134
  75.4 4.9 %slice.60 = bf16[32,256,256]{2,1,0:T(8,128)(2,1)} slice(bf16[32,272,256]{2,1,0:T(8,128)(2,1)} %all-to-all-done), slice={[0:32], [0:256], [0:256]} | slice | bytes 8388608 | tf_op jit(solution)/shard_map/slice | solution.py:118
  81.6 4.5 %copy.54 = bf16[64,128,256]{2,1,0:T(8,128)(2,1)S(1)} copy(f32[64,128,256]{2,0,1:T(8,128)S(1)} %copy-done.1) | data formatting | bytes 12582912 | tf_op jit(solution)/shard_map/optimization_barrier | solution.py:140
  88.4 7.4 %all-to-all-start.1 = ((bf16[32,272,256]{2,1,0:T(8,128)(2,1)}), bf16[32,272,256]{2,1,0:T(8,128)(2,1)}, u32[]{:S(2)}, u32[]{:S(2)}) async-start(bf16[32,272,256]{2,1,0:T(8,128)(2,1)} %pad_maximum_fusion.1), calls=%async_computation.1 | async-start | bytes 8912896 | tf_op jit(solution)/shard_map/all_to_all | solution.py:147
  95.8 5.1 %gather_fusion.1 = bf16[64,128,256]{2,1,0:T(8,128)(2,1)} fusion(bf16[64,128,256]{2,1,0:T(8,128)(2,1)} %bitcast.120, s32[1024]{0:T(1024)S(1)} %pad_clamp_fusion), kind=kCustom, calls=%fused_computation.1 | custom fusion | bytes 8388864 | tf_op jit(solution)/shard_map/while/body/gather | solution.py:155
  103.3 15.3 %while.25 = (s32[]{:T(128)}, f32[32,128,256]{2,0,1:T(8,128)}, s32[]{:T(128)}, s32[1,1,64]{2,1,0:T(1,128)S(1)}, s32[]{:T(128)}, /*index=5*/f32[64,8]{0,1:T(8,128)...) while((s32[]{:T(128)}, f32[32,128,256]{2,0,1:T(8,128)}, ...), condition=%wide.region_4.5_spmd, body=%wide.region_3.4_spmd.sunk | while | flops 1343228672 | bytes 31462264 | solution.py:165
  104.1 3.4 %fusion.91 = f32[64,128,256]{2,1,0:T(8,128)S(1)} fusion(bf16[64,128,128]{2,1,0:T(8,128)(2,1)S(1)} %get-tuple-element.454, bf16[64,128,256]{2,1,0:T(8,128)(2,1)} %get-tuple-element.455), kind=kOutput, calls=%fused_computation.70.clone.1 | convolution fusion | flops 536870912 | bytes 14680064 | tf_op jit(solution)/shard_map/while/body/tij,tjf->tif/dot_general | solution.py:156
  107.5 11.0 %fusion.93 = f32[32,128,256]{2,0,1:T(8,128)} fusion(f32[32,128,256]{2,0,1:T(8,128)} %get-tuple-element.439, f32[64,128,256]{2,1,0:T(8,128)S(1)} %fusion.91, f32[64,8]{0,1:T(8,128)S(1)} %get-tuple-element.453, f32[64,4]{0,1:T(4,128)S(1)} %fusion.92), kind=kOutput, calls=%fused_computation.21.clone.1 | convolution fusion | flops 806356992 | bytes 16780288 | tf_op jit(solution)/shard_map/while/body/dot_general | solution.py:160
  118.7 7.3 %fusion.32 = f32[8,256,256]{2,1,0:T(8,128)S(1)} fusion(bf16[4,128,256,1]{2,1,0,3:T(8,128)(2,1)S(1)} %bitcast.128, f32[4,8,128,256]{3,1,0,2:T(8,128)} %bitcast.28), kind=kOutput, calls=%fused_computation.40 | convolution fusion | flops 3221225472 | bytes 6553600 | tf_op jit(solution)/shard_map/lbnf,lng->bfg/dot_general | solution.py:171
  126.0 7.2 %fusion.35 = f32[4,128,256]{2,1,0:T(8,128)} fusion(f32[4,8,128,256]{3,1,0,2:T(8,128)} %bitcast.28, bf16[8,256,256]{2,1,0:T(8,128)(2,1)S(1)} %copy-done), kind=kOutput, calls=%fused_computation.41 | convolution fusion | flops 3221225472 | bytes 5767168 | tf_op jit(solution)/shard_map/lbnf,bfg->lng/dot_general | solution.py:170
  133.2 17.8 %all-to-all-done.1 = bf16[32,272,256]{2,1,0:T(8,128)(2,1)} async-done(((bf16[32,272,256]{2,1,0:T(8,128)(2,1)}), bf16[32,272,256]{2,1,0:T(8,128)(2,1)}, u32[]{:S(2)}, u32[]{:S(2)}) %all-to-all-start.1) | async-done | bytes 4456480 | tf_op jit(solution)/shard_map/all_to_all | solution.py:147
  151.1 4.7 %slice.63 = bf16[32,256,256]{2,1,0:T(8,128)(2,1)} slice(bf16[32,272,256]{2,1,0:T(8,128)(2,1)} %all-to-all-done.1), slice={[0:32], [0:256], [0:256]} | slice | bytes 8388608 | tf_op jit(solution)/shard_map/slice | solution.py:149
  160.1 9.3 %all-to-all-start.4 = ((f32[128,8,256]{2,1,0:T(8,128)}), f32[128,8,256]{2,1,0:T(8,128)S(1)}, u32[]{:S(2)}, u32[]{:S(2)}) async-start(f32[128,8,256]{2,1,0:T(8,128)} %bitcast.43), calls=%async_computation.4 | async-start | bytes 2097152 | tf_op jit(solution)/shard_map/all_to_all | solution.py:33
  169.6 4.5 %fusion.26 = f32[4,128,256]{2,0,1:T(4,128)S(1)} fusion(bf16[64,128,256]{2,1,0:T(8,128)(2,1)} %bitcast.119, s32[64]{0:T(128)S(1)} %eq.123), kind=kOutput, calls=%fused_computation.32 | convolution fusion | flops 16777472 | bytes 4718848 | tf_op jit(solution)/shard_map/dot_general | solution.py:183
  175.3 13.7 %all-to-all-done.4 = f32[128,8,256]{2,1,0:T(8,128)S(1)} async-done(((f32[128,8,256]{2,1,0:T(8,128)}), f32[128,8,256]{2,1,0:T(8,128)S(1)}, u32[]{:S(2)}, u32[]{:S(2)}) %all-to-all-start.4) | async-done | bytes 1048608 | tf_op jit(solution)/shard_map/all_to_all | solution.py:33
  189.0 3.5 %all-to-all-start.2 = ((f32[4,256,256]{2,1,0:T(8,128)}), f32[4,256,256]{2,1,0:T(8,128)S(1)}, u32[]{:S(2)}, u32[]{:S(2)}) async-start(f32[4,256,256]{2,1,0:T(8,128)} %bitcast.125), calls=%async_computation.2 | async-start | bytes 2097152 | tf_op jit(solution)/shard_map/all_to_all | solution.py:16
  192.6 14.9 %all-to-all-done.2 = f32[4,256,256]{2,1,0:T(8,128)S(1)} async-done(((f32[4,256,256]{2,1,0:T(8,128)}), f32[4,256,256]{2,1,0:T(8,128)S(1)}, u32[]{:S(2)}, u32[]{:S(2)}) %all-to-all-start.2) | async-done | bytes 1048608 | tf_op jit(solution)/shard_map/all_to_all | solution.py:16
  208.6 4.4 %all-to-all-start.5 = ((f32[128,8,256]{2,1,0:T(8,128)}), f32[128,8,256]{2,1,0:T(8,128)S(1)}, u32[]{:S(2)}, u32[]{:S(2)}) async-start(f32[128,8,256]{2,1,0:T(8,128)} %bitcast.126), calls=%async_computation.5 | async-start | bytes 2097152 | tf_op jit(solution)/shard_map/all_to_all | solution.py:41
  213.9 19.1 %all-to-all-done.5 = f32[128,8,256]{2,1,0:T(8,128)S(1)} async-done(((f32[128,8,256]{2,1,0:T(8,128)}), f32[128,8,256]{2,1,0:T(8,128)S(1)}, u32[]{:S(2)}, u32[]{:S(2)}) %all-to-all-start.5) | async-done | bytes 1048608 | tf_op jit(solution)/shard_map/all_to_all | solution.py:41
  234.9 3.5 %all-to-all-start.3 = ((f32[4,256,256]{2,1,0:T(8,128)}), f32[4,256,256]{2,1,0:T(8,128)S(1)}, u32[]{:S(2)}, u32[]{:S(2)}) async-start(f32[4,256,256]{2,1,0:T(8,128)} %broadcast_in_dim.34), calls=%async_computation.3 | async-start | bytes 2097152 | tf_op jit(solution)/shard_map/all_to_all | solution.py:18
  240.4 13.1 %all-to-all-done.3 = f32[4,256,256]{2,1,0:T(8,128)S(1)} async-done(((f32[4,256,256]{2,1,0:T(8,128)}), f32[4,256,256]{2,1,0:T(8,128)S(1)}, u32[]{:S(2)}, u32[]{:S(2)}) %all-to-all-start.3) | async-done | bytes 1048608 | tf_op jit(solution)/shard_map/all_to_all | solution.py:18
  256.5 3.2 %maximum_select_fusion = f32[2048,256]{1,0:T(8,128)} fusion(f32[1024,256]{1,0:T(8,128)} %collective-permute-done.1, f32[1024,256]{1,0:T(8,128)S(1)} %bitcast.123, pred[]{:T(512)S(6)} %eq.127), kind=kLoop, calls=%fused_computation.39 | loop fusion | flops 1572864 | bytes 4194305 | tf_op jit(solution)/shard_map/jit(_where)/select_n | solution.py:45
  (66 shorter events, 24.6 us)
Async XLA Ops:
  0.6 19.2 %copy-start = (bf16[8,256,256]{2,1,0:T(8,128)(2,1)S(1)}, bf16[8,256,256]{2,1,0:T(8,128)(2,1)}, u32[]{:S(2)}) copy-start(bf16[8,256,256]{2,1,0:T(8,128)(2,1)} %param.16) | copy-start | bytes 3145732
  0.6 2.3 copy-start.3
  9.5 10.3 %copy-start.5 = (bf16[512,256]{1,0:T(8,128)(2,1)S(1)}, bf16[512,256]{1,0:T(8,128)(2,1)}, u32[]{:S(2)}) copy-start(bf16[512,256]{1,0:T(8,128)(2,1)} %param.25) | copy-start | bytes 786436
  9.5 65.9 %all-to-all-start = ((bf16[32,272,256]{2,1,0:T(8,128)(2,1)}), bf16[32,272,256]{2,1,0:T(8,128)(2,1)}, u32[]{:S(2)}, u32[]{:S(2)}) async-start(bf16[32,272,256]{2,1,0:T(8,128)(2,1)} %pad_maximum_fusion), calls=%async_computation | async-start | bytes 8912896 | tf_op jit(solution)/shard_map/all_to_all | solution.py:115
  22.5 5.4 %copy-start.12 = (f32[200,8]{0,1:T(8,128)S(1)}, f32[200,8]{0,1:T(8,128)}, u32[]{:S(2)}) copy-start(f32[200,8]{0,1:T(8,128)} %param.18) | copy-start | bytes 19204
  22.5 5.4 %copy-start.13 = (s32[1,1,64]{2,1,0:T(1,128)S(1)}, s32[1,1,64]{2,1,0:T(1,128)}, u32[]{:S(2)}) copy-start(s32[1,1,64]{2,1,0:T(1,128)} %param.22) | copy-start | bytes 772
  28.1 4.4 %copy-start.2 = (bf16[1,1,64,128,128]{4,3,2,1,0:T(8,128)(2,1)S(1)}, bf16[1,1,64,128,128]{4,3,2,1,0:T(8,128)(2,1)}, u32[]{:S(2)}) copy-start(bf16[1,1,64,128,128]{4,3,2,1,0:T(8,128)(2,1)} %param.19) | copy-start | bytes 6291460
  28.1 4.4 %copy-start.9 = (s32[1,1,64]{2,1,0:T(1,128)S(1)}, s32[1,1,64]{2,1,0:T(1,128)}, u32[]{:S(2)}) copy-start(s32[1,1,64]{2,1,0:T(1,128)} %param.20) | copy-start | bytes 772
  28.1 4.4 %copy-start.10 = (s32[1,1,64]{2,1,0:T(1,128)S(1)}, s32[1,1,64]{2,1,0:T(1,128)}, u32[]{:S(2)}) copy-start(s32[1,1,64]{2,1,0:T(1,128)} %param.21) | copy-start | bytes 772
  75.4 6.2 %copy-start.1 = (f32[64,128,256]{2,0,1:T(8,128)S(1)}, f32[64,128,256]{2,0,1:T(8,128)}, u32[]{:S(2)}) copy-start(f32[64,128,256]{2,0,1:T(8,128)} %get-tuple-element.242) | copy-start | bytes 25165828
  88.4 62.7 %all-to-all-start.1 = ((bf16[32,272,256]{2,1,0:T(8,128)(2,1)}), bf16[32,272,256]{2,1,0:T(8,128)(2,1)}, u32[]{:S(2)}, u32[]{:S(2)}) async-start(bf16[32,272,256]{2,1,0:T(8,128)(2,1)} %pad_maximum_fusion.1), calls=%async_computation.1 | async-start | bytes 8912896 | tf_op jit(solution)/shard_map/all_to_all | solution.py:147
  103.3 15.3 %copy-start.6 = (bf16[512,256]{1,0:T(8,128)(2,1)S(1)}, bf16[512,256]{1,0:T(8,128)(2,1)}, u32[]{:S(2)}) copy-start(bf16[512,256]{1,0:T(8,128)(2,1)} %param.25) | copy-start | bytes 786436
  155.7 13.7 %copy-start.11 = (s32[1,1,32,2]{2,3,1,0:T(2,128)S(1)}, s32[1,1,32,2]{2,3,1,0:T(2,128)}, u32[]{:S(2)}) copy-start(s32[1,1,32,2]{2,3,1,0:T(2,128)} %param.24) | copy-start | bytes 772
  155.9 3.1 %collective-permute-start = (f32[1024,256]{1,0:T(8,128)S(1)}, f32[1024,256]{1,0:T(8,128)S(1)}, u32[]{:S(2)}, u32[]{:S(2)}) collective-permute-start(f32[1024,256]{1,0:T(8,128)S(1)} %bitcast.134), channel_id=1, source_target_pairs={{0,4},{4,0},{8,12},{12,8},{16,20},{20,16},{24,28},{28,24},{32,36},... | collective-permute-start | bytes 3145736 | tf_op jit(solution)/shard_map/ppermute | solution.py:32
  160.1 14.2 %copy-start.7 = (f32[4,128,256]{2,1,0:T(8,128)S(1)}, f32[4,128,256]{2,1,0:T(8,128)}, u32[]{:S(2)}) copy-start(f32[4,128,256]{2,1,0:T(8,128)} %fusion.35) | copy-start | bytes 1572868
  160.1 28.9 %all-to-all-start.4 = ((f32[128,8,256]{2,1,0:T(8,128)}), f32[128,8,256]{2,1,0:T(8,128)S(1)}, u32[]{:S(2)}, u32[]{:S(2)}) async-start(f32[128,8,256]{2,1,0:T(8,128)} %bitcast.43), calls=%async_computation.4 | async-start | bytes 2097152 | tf_op jit(solution)/shard_map/all_to_all | solution.py:33
  189.0 18.5 %all-to-all-start.2 = ((f32[4,256,256]{2,1,0:T(8,128)}), f32[4,256,256]{2,1,0:T(8,128)S(1)}, u32[]{:S(2)}, u32[]{:S(2)}) async-start(f32[4,256,256]{2,1,0:T(8,128)} %bitcast.125), calls=%async_computation.2 | async-start | bytes 2097152 | tf_op jit(solution)/shard_map/all_to_all | solution.py:16
  208.6 24.3 %all-to-all-start.5 = ((f32[128,8,256]{2,1,0:T(8,128)}), f32[128,8,256]{2,1,0:T(8,128)S(1)}, u32[]{:S(2)}, u32[]{:S(2)}) async-start(f32[128,8,256]{2,1,0:T(8,128)} %bitcast.126), calls=%async_computation.5 | async-start | bytes 2097152 | tf_op jit(solution)/shard_map/all_to_all | solution.py:41
  213.1 40.5 %copy-start.4 = (bf16[512,256]{1,0:T(8,128)(2,1)S(1)}, bf16[512,256]{1,0:T(8,128)(2,1)}, u32[]{:S(2)}) copy-start(bf16[512,256]{1,0:T(8,128)(2,1)} %param.15) | copy-start | bytes 786436
  213.1 40.5 %copy-start.8 = (bf16[256,256]{1,0:T(8,128)(2,1)S(1)}, bf16[256,256]{1,0:T(8,128)(2,1)}, u32[]{:S(2)}) copy-start(bf16[256,256]{1,0:T(8,128)(2,1)} %param.17) | copy-start | bytes 393220
  234.9 18.5 %all-to-all-start.3 = ((f32[4,256,256]{2,1,0:T(8,128)}), f32[4,256,256]{2,1,0:T(8,128)S(1)}, u32[]{:S(2)}, u32[]{:S(2)}) async-start(f32[4,256,256]{2,1,0:T(8,128)} %broadcast_in_dim.34), calls=%async_computation.3 | async-start | bytes 2097152 | tf_op jit(solution)/shard_map/all_to_all | solution.py:18
  238.5 18.1 %collective-permute-start.1 = (f32[1024,256]{1,0:T(8,128)S(1)}, f32[1024,256]{1,0:T(8,128)}, u32[]{:S(2)}, u32[]{:S(2)}) collective-permute-start(f32[1024,256]{1,0:T(8,128)S(1)} %bitcast.122), channel_id=1, source_target_pairs={{0,4},{4,0},{8,12},{12,8},{16,20},{20,16},{24,28},{28,24},{32,36},... | collective-permute-start | bytes 3145736 | tf_op jit(solution)/shard_map/ppermute | solution.py:44

commit v7 on v6

--- a/solution.py
+++ b/solution.py
@@ -47,6 +47,23 @@
         jnp.concatenate([own_half, other_half]),
         jnp.concatenate([other_half, own_half]),
     )
+
+
+def permute_psum(value, axis):
+    size = lax.axis_size(axis)
+    me = lax.axis_index(axis)
+    chunks = value.reshape((size, value.shape[0] // size) + value.shape[1:])
+    total = chunks[me]
+    for shift in range(1, size):
+        pairs = [(index, (index + shift) % size) for index in range(size)]
+        total = total + lax.ppermute(chunks[(me + shift) % size], axis, pairs)
+    parts = [total]
+    for shift in range(1, size):
+        pairs = [(index, (index + shift) % size) for index in range(size)]
+        parts.append(lax.ppermute(total, axis, pairs))
+    stacked = jnp.stack(parts)
+    order = (me - jnp.arange(size)) % size
+    return stacked[order].reshape(value.shape)
 
 
 def split_hi_lo(value):
@@ -189,7 +206,7 @@
     both = jnp.concatenate(
         [projected_part.reshape(-1, feat_width), own_grads.reshape(-1, feat_width)]
     )
-    summed_both = a2a_psum(both, ("rel",))
+    summed_both = permute_psum(both, "rel")
     projected = summed_both[: features.shape[0]]
     summed = summed_both[features.shape[0] :]
     output = (projected + root_term).astype(jnp.bfloat16)

time: 264 us -> 252 us (0.955)
  waiting for transfers between devices: 80.9 us -> 62.4 us
    all_to_all x2 -> x0, waiting for transfers between devices: 28 us -> none  [the longest x1 14.9 us: a2a_psum(): pieces = lax.all_to_all(chunked, axes, 0, 0, tiled=True)]
    ppermute x0 -> x6, waiting for transfers between devices: none -> 22.8 us  [the longest x3 14.5 us: permute_psum(): total = total + lax.ppermute(chunks[(me + shift) % size], axis, pairs)]
    all_to_all x1, waiting for transfers between devices: 19.1 us -> 0.01 us  [pair_psum(): lax.all_to_all(outgoing, ('rows', 'rel'), 0, 0, tiled=True)]
    ppermute x0 -> x6, starting transfers between devices: none -> 8.01 us  [the longest x3 5.06 us: permute_psum(): total = total + lax.ppermute(chunks[(me + shift) % size], axis, pairs)]
    all_to_all x2 -> x0, starting transfers between devices: 7.04 us -> none  [the longest x1 3.52 us: a2a_psum(): pieces = lax.all_to_all(chunked, axes, 0, 0, tiled=True)]
    all_to_all x1, waiting for transfers between devices: 13.7 us -> 19.5 us  [pair_psum(): lax.all_to_all(chip_sum.reshape((count, half // count) + value.shape[1:])...]
  transfers between devices with their start and end apart: 8 -> 12, of which waited for: 6 -> 8; matrix products, arithmetic and copies ran while one was open for 40% -> 44% of each run, Pallas kernels for 0% -> 0%
where the time goes in v7:
time: 252 us; the launch traced here: 248 us
  matrix products  72.9 us (29%)
  waiting for transfers between devices  62.4 us (25%)
  local copies, waits for them, and re-layouts  49.5 us (20%)
  starting transfers between devices  40.5 us (16%)
  other arithmetic  19.9 us (8%)
    all_to_all x1, waiting for transfers between devices, pair_psum(): lax.all_to_all(chip_sum.reshape((count, half // count) + value.shape[1:])...  19.5 us
    all_to_all x1, waiting for transfers between devices, on_device(): lax.all_to_all(slot_out, 'rows', split_axis=0, concat_axis=0, tiled=True)  17.8 us
    ppermute x3, waiting for transfers between devices, permute_psum(): total = total + lax.ppermute(chunks[(me + shift) % size], axis, pairs)  14.5 us
    dot_general x1, matrix products, backward_step(): lax.dot_general(slot_hot, backward_term, contract_first, precision=highest)  14.2 us
    dot_general x1, matrix products, backward_step(): lax.dot_general(weights, agg_grad, (((1,), (0,)), ((), ())), precision=hi...  11.5 us
    dot_general x1, matrix products, forward_step(): lax.dot_general(weights, messages, contract_first, precision=highest)  11 us
    all_to_all x1, starting transfers between devices, on_device(): lax.all_to_all(outgoing, 'rows', split_axis=0, concat_axis=0, tiled=True)  9.6 us
    dot_general x1, local copies, waits for them, and re-layouts, backward_step(): jnp.einsum('tij,tif->tjf', adjacency, spread, preferred_element_type=jnp....  9.25 us
  transfers between devices with their start and end apart: 12, of which 8 were waited for; matrix products, arithmetic and copies ran while one was open for 44% of the time, Pallas kernels for 0%

profile of v7, /device:TPU:1, one launch (start us, length us, event | category | flops | bytes accessed | tf_op | source)
XLA Modules:
  0.0 248.0 jit_solution(12916789389071758131)
XLA Ops:
  3.0 2.8 %gather_fusion = bf16[64,128,256]{2,1,0:T(8,128)(2,1)} fusion(bf16[4,128,256]{2,1,0:T(8,128)(2,1)S(1)} %bitcast.135, s32[1024]{0:T(1024)S(1)} %pad_clamp_fusion.2), kind=kCustom, calls=%fused_computation | custom fusion | bytes 8388864 | tf_op jit(solution)/shard_map/gather | solution.py:130
  5.8 3.8 %pad_maximum_fusion = bf16[32,272,256]{2,1,0:T(8,128)(2,1)} fusion(bf16[32,8,256]{2,1,0:T(8,128)(2,1)S(1)} %subtract_convert_fusion.1, bf16[32,8,256]{2,1,0:T(8,128)(2,1)S(1)} %get-tuple-element.290, bf16[32,256,256]{2,1,0:T(8,128)(2,1)} %bitcast.139), kind=kLoop, calls=%fused_computation.31 | loop fusion | flops 13369344 | bytes 8912896 | tf_op jit(solution)/shard_map/concatenate | solution.py:131
  9.5 9.6 %all-to-all-start = ((bf16[32,272,256]{2,1,0:T(8,128)(2,1)}), bf16[32,272,256]{2,1,0:T(8,128)(2,1)}, u32[]{:S(2)}, u32[]{:S(2)}) async-start(bf16[32,272,256]{2,1,0:T(8,128)(2,1)} %pad_maximum_fusion), calls=%async_computation | async-start | bytes 8912896 | tf_op jit(solution)/shard_map/all_to_all | solution.py:132
  19.8 2.7 %convolution_bitcast_fusion = f32[4,8,128,256]{2,3,0,1:T(8,128)} fusion(bf16[4,128,256,1]{2,1,0,3:T(8,128)(2,1)S(1)} %bitcast.145, bf16[8,256,256]{2,1,0:T(8,128)(2,1)S(1)} %copy-done), kind=kOutput, calls=%fused_computation.39 | convolution fusion | flops 536870912 | bytes 5505024 | tf_op jit(solution)/shard_map/lng,bfg->lbnf/dot_general | solution.py:138
  22.5 5.4 %copy.21 = f32[4,8,128,256]{3,2,1,0:T(8,128)} copy(f32[4,8,128,256]{2,3,0,1:T(8,128)} %convolution_bitcast_fusion) | data formatting | bytes 8388608 | tf_op jit(solution)/shard_map/lng,bfg->lbnf/transpose | solution.py:138
  28.2 4.3 %broadcast_in_dim.20 = f32[64,128,256]{2,0,1:T(8,128)} broadcast(f32[]{:T(128)} %constant.96.clone.1), dimensions={} | broadcast | bytes 8388612 | tf_op jit(solution)/shard_map/broadcast_in_dim | solution.py:155
  32.5 42.8 %while.24 = (s32[]{:T(128)}, f32[64,128,256]{2,0,1:T(8,128)}, s32[]{:T(128)}, s32[1,1,64]{2,1,0:T(1,128)S(1)}, s32[1,1,64]{2,1,0:T(1,128)S(1)}, /*index=5*/s32[]...) while((s32[]{:T(128)}, f32[64,128,256]{2,0,1:T(8,128)}, ...), condition=%wide.region_1.2_spmd, body=%wide.region_0.1_spmd.sunk | while | flops 2954894080 | bytes 65016960 | solution.py:156
  33.8 11.5 %fusion.88 = bf16[64,128,256]{2,0,1:T(8,128)(2,1)S(1)} fusion(f32[32,128,256]{2,1,0:T(8,128)} %get-tuple-element.427, f32[64,8]{0,1:T(8,128)S(1)} %get-tuple-element.426, f32[64,4]{0,1:T(4,128)S(1)} %fusion.87), kind=kOutput, calls=%fused_computation.7.clone.1 | convolution fusion | flops 805308416 | bytes 8391680 | tf_op jit(solution)/shard_map/while/body/dot_general | solution.py:144
  45.2 6.6 %fusion.89 = f32[64,256,128]{2,1,0:T(8,128)} fusion(bf16[64,128,128]{2,1,0:T(8,128)(2,1)S(1)} %get-tuple-element.428, bf16[64,128,256]{2,0,1:T(8,128)(2,1)S(1)} %fusion.88), kind=kOutput, calls=%fused_computation.6.clone.1 | convolution fusion | flops 536870912 | bytes 14680064 | tf_op jit(solution)/shard_map/while/body/tij,tif->tjf/dot_general | solution.py:147
  51.8 9.3 %copy.61 = f32[64,256,128]{1,0,2:T(8,128)} copy(f32[64,256,128]{2,1,0:T(8,128)} %fusion.89) | data formatting | bytes 16777216 | tf_op jit(solution)/shard_map/while/body/tij,tif->tjf/dot_general | solution.py:147
  61.1 14.2 %fusion.90 = f32[64,128,256]{2,0,1:T(8,128)} fusion(f32[64,128,256]{2,0,1:T(8,128)} %get-tuple-element.410, f32[64,256,128]{1,0,2:T(8,128)} %copy.61, s32[64]{0:T(128)S(1)} %bitcast.159), kind=kOutput, calls=%fused_computation.9.clone.1 | convolution fusion | flops 1612713984 | bytes 25166080 | tf_op jit(solution)/shard_map/while/body/dot_general | solution.py:151
  75.4 4.9 %slice.62 = bf16[32,256,256]{2,1,0:T(8,128)(2,1)} slice(bf16[32,272,256]{2,1,0:T(8,128)(2,1)} %all-to-all-done), slice={[0:32], [0:256], [0:256]} | slice | bytes 8388608 | tf_op jit(solution)/shard_map/slice | solution.py:135
  81.6 4.5 %copy.54 = bf16[64,128,256]{2,1,0:T(8,128)(2,1)S(1)} copy(f32[64,128,256]{2,0,1:T(8,128)S(1)} %copy-done.1) | data formatting | bytes 12582912 | tf_op jit(solution)/shard_map/optimization_barrier | solution.py:157
  88.4 7.4 %all-to-all-start.1 = ((bf16[32,272,256]{2,1,0:T(8,128)(2,1)}), bf16[32,272,256]{2,1,0:T(8,128)(2,1)}, u32[]{:S(2)}, u32[]{:S(2)}) async-start(bf16[32,272,256]{2,1,0:T(8,128)(2,1)} %pad_maximum_fusion.1), calls=%async_computation.1 | async-start | bytes 8912896 | tf_op jit(solution)/shard_map/all_to_all | solution.py:164
  95.8 5.1 %gather_fusion.1 = bf16[64,128,256]{2,1,0:T(8,128)(2,1)} fusion(bf16[64,128,256]{2,1,0:T(8,128)(2,1)} %bitcast.138, s32[1024]{0:T(1024)S(1)} %pad_clamp_fusion.1), kind=kCustom, calls=%fused_computation.1 | custom fusion | bytes 8388864 | tf_op jit(solution)/shard_map/while/body/gather | solution.py:172
  103.4 15.3 %while.25 = (s32[]{:T(128)}, f32[32,128,256]{2,0,1:T(8,128)}, s32[]{:T(128)}, s32[1,1,64]{2,1,0:T(1,128)S(1)}, s32[]{:T(128)}, /*index=5*/f32[64,8]{0,1:T(8,128)...) while((s32[]{:T(128)}, f32[32,128,256]{2,0,1:T(8,128)}, ...), condition=%wide.region_4.5_spmd, body=%wide.region_3.4_spmd.sunk | while | flops 1343228672 | bytes 31462264 | solution.py:182
  104.1 3.4 %fusion.95 = f32[64,128,256]{2,1,0:T(8,128)S(1)} fusion(bf16[64,128,128]{2,1,0:T(8,128)(2,1)S(1)} %get-tuple-element.457, bf16[64,128,256]{2,1,0:T(8,128)(2,1)} %get-tuple-element.458), kind=kOutput, calls=%fused_computation.85.clone.1 | convolution fusion | flops 536870912 | bytes 14680064 | tf_op jit(solution)/shard_map/while/body/tij,tjf->tif/dot_general | solution.py:173
  107.5 11.0 %fusion.97 = f32[32,128,256]{2,0,1:T(8,128)} fusion(f32[32,128,256]{2,0,1:T(8,128)} %get-tuple-element.442, f32[64,128,256]{2,1,0:T(8,128)S(1)} %fusion.95, f32[64,8]{0,1:T(8,128)S(1)} %get-tuple-element.456, f32[64,4]{0,1:T(4,128)S(1)} %fusion.96), kind=kOutput, calls=%fused_computation.22.clone.1 | convolution fusion | flops 806356992 | bytes 16780288 | tf_op jit(solution)/shard_map/while/body/dot_general | solution.py:177
  118.7 7.3 %fusion.32 = f32[8,256,256]{2,1,0:T(8,128)S(1)} fusion(bf16[4,128,256,1]{2,1,0,3:T(8,128)(2,1)S(1)} %bitcast.146, f32[4,8,128,256]{3,1,0,2:T(8,128)} %bitcast.28), kind=kOutput, calls=%fused_computation.41 | convolution fusion | flops 3221225472 | bytes 6553600 | tf_op jit(solution)/shard_map/lbnf,lng->bfg/dot_general | solution.py:188
  126.0 7.2 %fusion.35 = f32[4,128,256]{2,1,0:T(8,128)} fusion(f32[4,8,128,256]{3,1,0,2:T(8,128)} %bitcast.28, bf16[8,256,256]{2,1,0:T(8,128)(2,1)S(1)} %copy-done), kind=kOutput, calls=%fused_computation.42 | convolution fusion | flops 3221225472 | bytes 5767168 | tf_op jit(solution)/shard_map/lbnf,bfg->lng/dot_general | solution.py:187
  133.2 17.8 %all-to-all-done.1 = bf16[32,272,256]{2,1,0:T(8,128)(2,1)} async-done(((bf16[32,272,256]{2,1,0:T(8,128)(2,1)}), bf16[32,272,256]{2,1,0:T(8,128)(2,1)}, u32[]{:S(2)}, u32[]{:S(2)}) %all-to-all-start.1) | async-done | bytes 4456480 | tf_op jit(solution)/shard_map/all_to_all | solution.py:164
  151.1 4.7 %slice.65 = bf16[32,256,256]{2,1,0:T(8,128)(2,1)} slice(bf16[32,272,256]{2,1,0:T(8,128)(2,1)} %all-to-all-done.1), slice={[0:32], [0:256], [0:256]} | slice | bytes 8388608 | tf_op jit(solution)/shard_map/slice | solution.py:166
  160.1 8.9 %all-to-all-start.2 = ((f32[128,8,256]{2,1,0:T(8,128)}), f32[128,8,256]{2,1,0:T(8,128)S(1)}, u32[]{:S(2)}, u32[]{:S(2)}) async-start(f32[128,8,256]{2,1,0:T(8,128)} %bitcast.52), calls=%async_computation.2 | async-start | bytes 2097152 | tf_op jit(solution)/shard_map/all_to_all | solution.py:33
  169.2 19.5 %all-to-all-done.2 = f32[128,8,256]{2,1,0:T(8,128)S(1)} async-done(((f32[128,8,256]{2,1,0:T(8,128)}), f32[128,8,256]{2,1,0:T(8,128)S(1)}, u32[]{:S(2)}, u32[]{:S(2)}) %all-to-all-start.2) | async-done | bytes 1048608 | tf_op jit(solution)/shard_map/all_to_all | solution.py:33
  189.9 3.8 %all-to-all-start.3 = ((f32[128,8,256]{2,1,0:T(8,128)}), f32[128,8,256]{2,1,0:T(8,128)S(1)}, u32[]{:S(2)}, u32[]{:S(2)}) async-start(f32[128,8,256]{2,1,0:T(8,128)} %bitcast.54), calls=%async_computation.3 | async-start | bytes 2097152 | tf_op jit(solution)/shard_map/all_to_all | solution.py:41
  193.8 4.5 %fusion.26 = f32[4,128,256]{2,0,1:T(4,128)S(1)} fusion(bf16[64,128,256]{2,1,0:T(8,128)(2,1)} %bitcast.137, s32[64]{0:T(128)S(1)} %eq.128), kind=kOutput, calls=%fused_computation.33 | convolution fusion | flops 16777472 | bytes 4718848 | tf_op jit(solution)/shard_map/dot_general | solution.py:200
  201.8 2.5 %collective-permute-start.1 = (f32[256,256]{1,0:T(8,128)}, f32[256,256]{1,0:T(8,128)}, u32[]{:S(2)}, u32[]{:S(2)}) collective-permute-start(f32[256,256]{1,0:T(8,128)} %get-tuple-element.289), channel_id=1, source_target_pairs={{0,2},{1,3},{2,0},{3,1},{4,6},{5,7},{6,4},{7,5},{8,10},{9,11},{10,... | collective-permute-start | bytes 786440 | tf_op jit(solution)/shard_map/ppermute | solution.py:59
  205.5 8.8 %collective-permute-done = f32[256,256]{1,0:T(8,128)} collective-permute-done((f32[256,256]{1,0:T(8,128)}, f32[256,256]{1,0:T(8,128)}, u32[]{:S(2)}, u32[]{:S(2)}) %collective-permute-start) | collective-permute-done | bytes 262176 | tf_op jit(solution)/shard_map/ppermute | solution.py:59
  214.3 5.7 %collective-permute-done.1 = f32[256,256]{1,0:T(8,128)} collective-permute-done((f32[256,256]{1,0:T(8,128)}, f32[256,256]{1,0:T(8,128)}, u32[]{:S(2)}, u32[]{:S(2)}) %collective-permute-start.1) | collective-permute-done | bytes 262176 | tf_op jit(solution)/shard_map/ppermute | solution.py:59
  221.9 2.5 %collective-permute-start.4 = (f32[256,256]{1,0:T(8,128)}, f32[256,256]{1,0:T(8,128)S(1)}, u32[]{:S(2)}, u32[]{:S(2)}) collective-permute-start(f32[256,256]{1,0:T(8,128)} %fusion.42), channel_id=1, source_target_pairs={{0,2},{1,3},{2,0},{3,1},{4,6},{5,7},{6,4},{7,5},{8,10},{9,11},{10,... | collective-permute-start | bytes 786440 | tf_op jit(solution)/shard_map/ppermute | solution.py:63
  230.4 5.9 %collective-permute-done.4 = f32[256,256]{1,0:T(8,128)S(1)} collective-permute-done((f32[256,256]{1,0:T(8,128)}, f32[256,256]{1,0:T(8,128)S(1)}, u32[]{:S(2)}, u32[]{:S(2)}) %collective-permute-start.4) | collective-permute-done | bytes 262176 | tf_op jit(solution)/shard_map/ppermute | solution.py:63
  244.6 3.2 %maximum_select_fusion = f32[2048,256]{1,0:T(8,128)} fusion(f32[1024,256]{1,0:T(8,128)} %collective-permute-done.7, f32[1024,256]{1,0:T(8,128)S(1)} %bitcast.141, pred[]{:T(512)S(6)} %eq.132), kind=kLoop, calls=%fused_computation.40 | loop fusion | flops 1572864 | bytes 4194305 | tf_op jit(solution)/shard_map/jit(_where)/select_n | solution.py:45
  (82 shorter events, 36.5 us)
Async XLA Ops:
  0.6 19.2 %copy-start = (bf16[8,256,256]{2,1,0:T(8,128)(2,1)S(1)}, bf16[8,256,256]{2,1,0:T(8,128)(2,1)}, u32[]{:S(2)}) copy-start(bf16[8,256,256]{2,1,0:T(8,128)(2,1)} %param.16) | copy-start | bytes 3145732
  0.6 2.3 copy-start.3
  9.5 10.3 %copy-start.5 = (bf16[512,256]{1,0:T(8,128)(2,1)S(1)}, bf16[512,256]{1,0:T(8,128)(2,1)}, u32[]{:S(2)}) copy-start(bf16[512,256]{1,0:T(8,128)(2,1)} %param.25) | copy-start | bytes 786436
  9.5 65.9 %all-to-all-start = ((bf16[32,272,256]{2,1,0:T(8,128)(2,1)}), bf16[32,272,256]{2,1,0:T(8,128)(2,1)}, u32[]{:S(2)}, u32[]{:S(2)}) async-start(bf16[32,272,256]{2,1,0:T(8,128)(2,1)} %pad_maximum_fusion), calls=%async_computation | async-start | bytes 8912896 | tf_op jit(solution)/shard_map/all_to_all | solution.py:132
  22.5 5.4 %copy-start.14 = (f32[200,8]{0,1:T(8,128)S(1)}, f32[200,8]{0,1:T(8,128)}, u32[]{:S(2)}) copy-start(f32[200,8]{0,1:T(8,128)} %param.18) | copy-start | bytes 19204
  22.5 5.4 %copy-start.15 = (s32[1,1,64]{2,1,0:T(1,128)S(1)}, s32[1,1,64]{2,1,0:T(1,128)}, u32[]{:S(2)}) copy-start(s32[1,1,64]{2,1,0:T(1,128)} %param.22) | copy-start | bytes 772
  28.2 4.4 %copy-start.2 = (bf16[1,1,64,128,128]{4,3,2,1,0:T(8,128)(2,1)S(1)}, bf16[1,1,64,128,128]{4,3,2,1,0:T(8,128)(2,1)}, u32[]{:S(2)}) copy-start(bf16[1,1,64,128,128]{4,3,2,1,0:T(8,128)(2,1)} %param.19) | copy-start | bytes 6291460
  28.2 4.4 %copy-start.11 = (s32[1,1,64]{2,1,0:T(1,128)S(1)}, s32[1,1,64]{2,1,0:T(1,128)}, u32[]{:S(2)}) copy-start(s32[1,1,64]{2,1,0:T(1,128)} %param.20) | copy-start | bytes 772
  28.2 4.4 %copy-start.12 = (s32[1,1,64]{2,1,0:T(1,128)S(1)}, s32[1,1,64]{2,1,0:T(1,128)}, u32[]{:S(2)}) copy-start(s32[1,1,64]{2,1,0:T(1,128)} %param.21) | copy-start | bytes 772
  75.4 6.2 %copy-start.1 = (f32[64,128,256]{2,0,1:T(8,128)S(1)}, f32[64,128,256]{2,0,1:T(8,128)}, u32[]{:S(2)}) copy-start(f32[64,128,256]{2,0,1:T(8,128)} %get-tuple-element.242) | copy-start | bytes 25165828
  88.4 62.7 %all-to-all-start.1 = ((bf16[32,272,256]{2,1,0:T(8,128)(2,1)}), bf16[32,272,256]{2,1,0:T(8,128)(2,1)}, u32[]{:S(2)}, u32[]{:S(2)}) async-start(bf16[32,272,256]{2,1,0:T(8,128)(2,1)} %pad_maximum_fusion.1), calls=%async_computation.1 | async-start | bytes 8912896 | tf_op jit(solution)/shard_map/all_to_all | solution.py:164
  103.4 15.3 %copy-start.6 = (bf16[512,256]{1,0:T(8,128)(2,1)S(1)}, bf16[512,256]{1,0:T(8,128)(2,1)}, u32[]{:S(2)}) copy-start(bf16[512,256]{1,0:T(8,128)(2,1)} %param.25) | copy-start | bytes 786436
  155.7 13.3 %copy-start.13 = (s32[1,1,32,2]{2,3,1,0:T(2,128)S(1)}, s32[1,1,32,2]{2,3,1,0:T(2,128)}, u32[]{:S(2)}) copy-start(s32[1,1,32,2]{2,3,1,0:T(2,128)} %param.24) | copy-start | bytes 772
  155.9 3.1 %collective-permute-start.6 = (f32[1024,256]{1,0:T(8,128)S(1)}, f32[1024,256]{1,0:T(8,128)S(1)}, u32[]{:S(2)}, u32[]{:S(2)}) collective-permute-start(f32[1024,256]{1,0:T(8,128)S(1)} %bitcast.152), channel_id=1, source_target_pairs={{0,4},{4,0},{8,12},{12,8},{16,20},{20,16},{24,28},{28,24},{32,36},... | collective-permute-start | bytes 3145736 | tf_op jit(solution)/shard_map/ppermute | solution.py:32
  160.1 28.7 %all-to-all-start.2 = ((f32[128,8,256]{2,1,0:T(8,128)}), f32[128,8,256]{2,1,0:T(8,128)S(1)}, u32[]{:S(2)}, u32[]{:S(2)}) async-start(f32[128,8,256]{2,1,0:T(8,128)} %bitcast.52), calls=%async_computation.2 | async-start | bytes 2097152 | tf_op jit(solution)/shard_map/all_to_all | solution.py:33
  189.9 34.9 %all-to-all-start.3 = ((f32[128,8,256]{2,1,0:T(8,128)}), f32[128,8,256]{2,1,0:T(8,128)S(1)}, u32[]{:S(2)}, u32[]{:S(2)}) async-start(f32[128,8,256]{2,1,0:T(8,128)} %bitcast.54), calls=%async_computation.3 | async-start | bytes 2097152 | tf_op jit(solution)/shard_map/all_to_all | solution.py:41
  200.4 41.2 %copy-start.4 = (bf16[512,256]{1,0:T(8,128)(2,1)S(1)}, bf16[512,256]{1,0:T(8,128)(2,1)}, u32[]{:S(2)}) copy-start(bf16[512,256]{1,0:T(8,128)(2,1)} %param.15) | copy-start | bytes 786436
  200.4 41.2 %copy-start.7 = (bf16[256,256]{1,0:T(8,128)(2,1)S(1)}, bf16[256,256]{1,0:T(8,128)(2,1)}, u32[]{:S(2)}) copy-start(bf16[256,256]{1,0:T(8,128)(2,1)} %param.17) | copy-start | bytes 393220
  200.4 13.9 %collective-permute-start = (f32[256,256]{1,0:T(8,128)}, f32[256,256]{1,0:T(8,128)}, u32[]{:S(2)}, u32[]{:S(2)}) collective-permute-start(f32[256,256]{1,0:T(8,128)} %get-tuple-element.287), channel_id=1, source_target_pairs={{0,1},{1,2},{2,3},{3,0},{4,5},{5,6},{6,7},{7,4},{8,9},{9,10},{10,1... | collective-permute-start | bytes 786440 | tf_op jit(solution)/shard_map/ppermute | solution.py:59
  201.8 18.2 %collective-permute-start.1 = (f32[256,256]{1,0:T(8,128)}, f32[256,256]{1,0:T(8,128)}, u32[]{:S(2)}, u32[]{:S(2)}) collective-permute-start(f32[256,256]{1,0:T(8,128)} %get-tuple-element.289), channel_id=1, source_target_pairs={{0,2},{1,3},{2,0},{3,1},{4,6},{5,7},{6,4},{7,5},{8,10},{9,11},{10,... | collective-permute-start | bytes 786440 | tf_op jit(solution)/shard_map/ppermute | solution.py:59
  204.4 15.6 %collective-permute-start.2 = (f32[256,256]{1,0:T(8,128)}, f32[256,256]{1,0:T(8,128)}, u32[]{:S(2)}, u32[]{:S(2)}) collective-permute-start(f32[256,256]{1,0:T(8,128)} %get-tuple-element.288), channel_id=1, source_target_pairs={{0,3},{1,0},{2,1},{3,2},{4,7},{5,4},{6,5},{7,6},{8,11},{9,8},{10,9... | collective-permute-start | bytes 786440 | tf_op jit(solution)/shard_map/ppermute | solution.py:59
  221.9 8.5 %collective-permute-start.3 = (f32[256,256]{1,0:T(8,128)}, f32[256,256]{1,0:T(8,128)S(1)}, u32[]{:S(2)}, u32[]{:S(2)}) collective-permute-start(f32[256,256]{1,0:T(8,128)} %fusion.42), channel_id=1, source_target_pairs={{0,1},{1,2},{2,3},{3,0},{4,5},{5,6},{6,7},{7,4},{8,9},{9,10},{10,1... | collective-permute-start | bytes 786440 | tf_op jit(solution)/shard_map/ppermute | solution.py:63
  221.9 14.4 %collective-permute-start.4 = (f32[256,256]{1,0:T(8,128)}, f32[256,256]{1,0:T(8,128)S(1)}, u32[]{:S(2)}, u32[]{:S(2)}) collective-permute-start(f32[256,256]{1,0:T(8,128)} %fusion.42), channel_id=1, source_target_pairs={{0,2},{1,3},{2,0},{3,1},{4,6},{5,7},{6,4},{7,5},{8,10},{9,11},{10,... | collective-permute-start | bytes 786440 | tf_op jit(solution)/shard_map/ppermute | solution.py:63
  224.4 12.4 %collective-permute-start.5 = (f32[256,256]{1,0:T(8,128)}, f32[256,256]{1,0:T(8,128)S(1)}, u32[]{:S(2)}, u32[]{:S(2)}) collective-permute-start(f32[256,256]{1,0:T(8,128)} %fusion.42), channel_id=1, source_target_pairs={{0,3},{1,0},{2,1},{3,2},{4,7},{5,4},{6,5},{7,6},{8,11},{9,8},{10,9... | collective-permute-start | bytes 786440 | tf_op jit(solution)/shard_map/ppermute | solution.py:63
  224.9 19.7 %collective-permute-start.7 = (f32[1024,256]{1,0:T(8,128)S(1)}, f32[1024,256]{1,0:T(8,128)}, u32[]{:S(2)}, u32[]{:S(2)}) collective-permute-start(f32[1024,256]{1,0:T(8,128)S(1)} %bitcast.140), channel_id=1, source_target_pairs={{0,4},{4,0},{8,12},{12,8},{16,20},{20,16},{24,28},{28,24},{32,36},... | collective-permute-start | bytes 3145736 | tf_op jit(solution)/shard_map/ppermute | solution.py:44
  230.4 6.4 %copy-start.8 = (f32[256,256]{1,0:T(8,128)}, f32[256,256]{1,0:T(8,128)S(1)}, u32[]{:S(2)}) copy-start(f32[256,256]{1,0:T(8,128)S(1)} %collective-permute-done.3) | copy-start | bytes 786436
  236.3 0.7 copy-start.9
  236.8 0.7 copy-start.10

commit v8 on v7

--- a/solution.py
+++ b/solution.py
@@ -132,7 +132,6 @@
     incoming = lax.all_to_all(outgoing, "rows", split_axis=0, concat_axis=0, tiled=True)
     block_rows = slots_peer * size_block
     root_mine = jnp.sum(join_hi_lo(incoming[:, block_rows:]), axis=0, keepdims=True)
-    incoming = incoming[:, :block_rows]
 
     cot_blocks = cotangent.reshape(local_blocks, size_block, feat_width)
     agg_grad = jnp.einsum("lng,bfg->lbnf", cot_blocks, bases, preferred_element_type=jnp.float32)
@@ -163,9 +162,8 @@
     slot_out = jnp.concatenate([slot_out, split_hi_lo(root_bcast)], axis=1)
     returned = lax.all_to_all(slot_out, "rows", split_axis=0, concat_axis=0, tiled=True)
     root_grad = join_hi_lo(returned[:, block_rows:]).reshape(root_local.shape)
-    returned = returned[:, :block_rows]
-
-    received = incoming.reshape(total_slots, size_block, feat_width)
+
+    received = incoming[:, :block_rows].reshape(total_slots, size_block, feat_width)
 
     def forward_step(block_index, running):
         first_tile = block_index * step_tiles
@@ -199,7 +197,7 @@
     )
     own_grads = lax.dot_general(
         block_hot,
-        returned.astype(jnp.float32).reshape(total_slots, size_block, feat_width),
+        returned[:, :block_rows].astype(jnp.float32).reshape(total_slots, size_block, feat_width),
         (((1,), (0,)), ((), ())),
         precision=highest,
     )

time: 252 us -> 246 us (0.976)
  waiting for transfers between devices: 62.4 us -> 53.2 us
  local copies, waits for them, and re-layouts: 49.5 us -> 52.4 us
    all_to_all x1, waiting for transfers between devices: 19.5 us -> 14.8 us  [pair_psum(): lax.all_to_all(chip_sum.reshape((count, half // count) + value.shape[1:])...]
    all_to_all x1, waiting for transfers between devices: 17.8 us -> 13.2 us  [on_device(): lax.all_to_all(slot_out, 'rows', split_axis=0, concat_axis=0, tiled=True)]
    optimization_barrier x1, local copies, waits for them, and re-layouts: 4.45 us -> 7.83 us  [on_device(): lax.optimization_barrier((incoming, slot_grads, root_mine))]
  transfers between devices with their start and end apart: 12 -> 12, of which waited for: 8 -> 8; matrix products, arithmetic and copies ran while one was open for 44% -> 49% of each run, Pallas kernels for 0% -> 0%
where the time goes in v8:
time: 246 us; the launch traced here: 242 us
  matrix products  73 us (30%)
  waiting for transfers between devices  53.2 us (22%)
  local copies, waits for them, and re-layouts  52.4 us (21%)
  starting transfers between devices  40.5 us (16%)
  other arithmetic  19.7 us (8%)
    all_to_all x1, waiting for transfers between devices, pair_psum(): lax.all_to_all(chip_sum.reshape((count, half // count) + value.shape[1:])...  14.8 us
    ppermute x3, waiting for transfers between devices, permute_psum(): total = total + lax.ppermute(chunks[(me + shift) % size], axis, pairs)  14.5 us
    dot_general x1, matrix products, backward_step(): lax.dot_general(slot_hot, backward_term, contract_first, precision=highest)  14.3 us
    all_to_all x1, waiting for transfers between devices, on_device(): lax.all_to_all(slot_out, 'rows', split_axis=0, concat_axis=0, tiled=True)  13.2 us
    dot_general x1, matrix products, backward_step(): lax.dot_general(weights, agg_grad, (((1,), (0,)), ((), ())), precision=hi...  11.5 us
    dot_general x1, matrix products, forward_step(): lax.dot_general(weights, messages, contract_first, precision=highest)  11 us
    all_to_all x1, starting transfers between devices, on_device(): lax.all_to_all(outgoing, 'rows', split_axis=0, concat_axis=0, tiled=True)  9.6 us
    dot_general x1, local copies, waits for them, and re-layouts, backward_step(): jnp.einsum('tij,tif->tjf', adjacency, spread, preferred_element_type=jnp....  9.18 us
  transfers between devices with their start and end apart: 12, of which 8 were waited for; matrix products, arithmetic and copies ran while one was open for 49% of the time, Pallas kernels for 0%

profile of v8, /device:TPU:1, one launch (start us, length us, event | category | flops | bytes accessed | tf_op | source)
XLA Modules:
  0.0 241.6 jit_solution(9274016371197582052)
XLA Ops:
  3.0 2.8 %gather_fusion = bf16[64,128,256]{2,1,0:T(8,128)(2,1)} fusion(bf16[4,128,256]{2,1,0:T(8,128)(2,1)S(1)} %bitcast.135, s32[1024]{0:T(1024)S(1)} %pad_clamp_fusion.2), kind=kCustom, calls=%fused_computation | custom fusion | bytes 8388864 | tf_op jit(solution)/shard_map/gather | solution.py:130
  5.8 3.8 %pad_maximum_fusion = bf16[32,272,256]{2,1,0:T(8,128)(2,1)} fusion(bf16[32,8,256]{2,1,0:T(8,128)(2,1)S(1)} %subtract_convert_fusion.1, bf16[32,8,256]{2,1,0:T(8,128)(2,1)S(1)} %get-tuple-element.290, bf16[32,256,256]{2,1,0:T(8,128)(2,1)} %bitcast.138), kind=kLoop, calls=%fused_computation.31 | loop fusion | flops 13369344 | bytes 8912896 | tf_op jit(solution)/shard_map/concatenate | solution.py:131
  9.6 9.6 %all-to-all-start = ((bf16[32,272,256]{2,1,0:T(8,128)(2,1)}), bf16[32,272,256]{2,1,0:T(8,128)(2,1)}, u32[]{:S(2)}, u32[]{:S(2)}) async-start(bf16[32,272,256]{2,1,0:T(8,128)(2,1)} %pad_maximum_fusion), calls=%async_computation | async-start | bytes 8912896 | tf_op jit(solution)/shard_map/all_to_all | solution.py:132
  19.8 2.7 %convolution_bitcast_fusion = f32[4,8,128,256]{2,3,0,1:T(8,128)} fusion(bf16[4,128,256,1]{2,1,0,3:T(8,128)(2,1)S(1)} %bitcast.145, bf16[8,256,256]{2,1,0:T(8,128)(2,1)S(1)} %copy-done), kind=kOutput, calls=%fused_computation.39 | convolution fusion | flops 536870912 | bytes 5505024 | tf_op jit(solution)/shard_map/lng,bfg->lbnf/dot_general | solution.py:137
  22.6 5.4 %copy.21 = f32[4,8,128,256]{3,2,1,0:T(8,128)} copy(f32[4,8,128,256]{2,3,0,1:T(8,128)} %convolution_bitcast_fusion) | data formatting | bytes 8388608 | tf_op jit(solution)/shard_map/lng,bfg->lbnf/transpose | solution.py:137
  28.2 4.3 %broadcast_in_dim.20 = f32[64,128,256]{2,0,1:T(8,128)} broadcast(f32[]{:T(128)} %constant.96.clone.1), dimensions={} | broadcast | bytes 8388612 | tf_op jit(solution)/shard_map/broadcast_in_dim | solution.py:154
  32.5 42.8 %while.24 = (s32[]{:T(128)}, f32[64,128,256]{2,0,1:T(8,128)}, s32[]{:T(128)}, s32[1,1,64]{2,1,0:T(1,128)S(1)}, s32[1,1,64]{2,1,0:T(1,128)S(1)}, /*index=5*/s32[]...) while((s32[]{:T(128)}, f32[64,128,256]{2,0,1:T(8,128)}, ...), condition=%wide.region_1.2_spmd, body=%wide.region_0.1_spmd.sunk | while | flops 2954894080 | bytes 65016960 | solution.py:155
  33.7 11.5 %fusion.88 = bf16[64,128,256]{2,0,1:T(8,128)(2,1)S(1)} fusion(f32[32,128,256]{2,1,0:T(8,128)} %get-tuple-element.427, f32[64,8]{0,1:T(8,128)S(1)} %get-tuple-element.426, f32[64,4]{0,1:T(4,128)S(1)} %fusion.87), kind=kOutput, calls=%fused_computation.7.clone.1 | convolution fusion | flops 805308416 | bytes 8391680 | tf_op jit(solution)/shard_map/while/body/dot_general | solution.py:143
  45.2 6.6 %fusion.89 = f32[64,256,128]{2,1,0:T(8,128)} fusion(bf16[64,128,128]{2,1,0:T(8,128)(2,1)S(1)} %get-tuple-element.428, bf16[64,128,256]{2,0,1:T(8,128)(2,1)S(1)} %fusion.88), kind=kOutput, calls=%fused_computation.6.clone.1 | convolution fusion | flops 536870912 | bytes 14680064 | tf_op jit(solution)/shard_map/while/body/tij,tif->tjf/dot_general | solution.py:146
  51.8 9.2 %copy.61 = f32[64,256,128]{1,0,2:T(8,128)} copy(f32[64,256,128]{2,1,0:T(8,128)} %fusion.89) | data formatting | bytes 16777216 | tf_op jit(solution)/shard_map/while/body/tij,tif->tjf/dot_general | solution.py:146
  61.0 14.3 %fusion.90 = f32[64,128,256]{2,0,1:T(8,128)} fusion(f32[64,128,256]{2,0,1:T(8,128)} %get-tuple-element.410, f32[64,256,128]{1,0,2:T(8,128)} %copy.61, s32[64]{0:T(128)S(1)} %bitcast.159), kind=kOutput, calls=%fused_computation.9.clone.1 | convolution fusion | flops 1612713984 | bytes 25166080 | tf_op jit(solution)/shard_map/while/body/dot_general | solution.py:150
  76.5 7.8 %copy.54 = bf16[64,128,256]{2,1,0:T(8,128)(2,1)S(1)} copy(f32[64,128,256]{2,0,1:T(8,128)} %get-tuple-element.242) | data formatting | bytes 12582912 | tf_op jit(solution)/shard_map/optimization_barrier | solution.py:156
  86.6 7.4 %all-to-all-start.1 = ((bf16[32,272,256]{2,1,0:T(8,128)(2,1)}), bf16[32,272,256]{2,1,0:T(8,128)(2,1)}, u32[]{:S(2)}, u32[]{:S(2)}) async-start(bf16[32,272,256]{2,1,0:T(8,128)(2,1)} %pad_maximum_fusion.1), calls=%async_computation.1 | async-start | bytes 8912896 | tf_op jit(solution)/shard_map/all_to_all | solution.py:163
  94.0 4.6 %slice.46 = bf16[32,256,256]{2,1,0:T(8,128)(2,1)} slice(bf16[32,272,256]{2,1,0:T(8,128)(2,1)} %all-to-all-done), slice={[0:32], [0:256], [0:256]} | slice | bytes 8388608 | tf_op jit(solution)/shard_map/slice | solution.py:166
  98.6 5.1 %gather_fusion.1 = bf16[64,128,256]{2,1,0:T(8,128)(2,1)} fusion(bf16[64,128,256]{2,1,0:T(8,128)(2,1)} %bitcast.139, s32[1024]{0:T(1024)S(1)} %pad_clamp_fusion.1), kind=kCustom, calls=%fused_computation.1 | custom fusion | bytes 8388864 | tf_op jit(solution)/shard_map/while/body/gather | solution.py:170
  106.1 15.3 %while.25 = (s32[]{:T(128)}, f32[32,128,256]{2,0,1:T(8,128)}, s32[]{:T(128)}, s32[1,1,64]{2,1,0:T(1,128)S(1)}, s32[]{:T(128)}, /*index=5*/f32[64,8]{0,1:T(8,128)...) while((s32[]{:T(128)}, f32[32,128,256]{2,0,1:T(8,128)}, ...), condition=%wide.region_4.5_spmd, body=%wide.region_3.4_spmd.sunk | while | flops 1343228672 | bytes 31462264 | solution.py:180
  106.9 3.4 %fusion.95 = f32[64,128,256]{2,1,0:T(8,128)S(1)} fusion(bf16[64,128,128]{2,1,0:T(8,128)(2,1)S(1)} %get-tuple-element.457, bf16[64,128,256]{2,1,0:T(8,128)(2,1)} %get-tuple-element.458), kind=kOutput, calls=%fused_computation.85.clone.1 | convolution fusion | flops 536870912 | bytes 14680064 | tf_op jit(solution)/shard_map/while/body/tij,tjf->tif/dot_general | solution.py:171
  110.3 11.0 %fusion.97 = f32[32,128,256]{2,0,1:T(8,128)} fusion(f32[32,128,256]{2,0,1:T(8,128)} %get-tuple-element.442, f32[64,128,256]{2,1,0:T(8,128)S(1)} %fusion.95, f32[64,8]{0,1:T(8,128)S(1)} %get-tuple-element.456, f32[64,4]{0,1:T(4,128)S(1)} %fusion.96), kind=kOutput, calls=%fused_computation.22.clone.1 | convolution fusion | flops 806356992 | bytes 16780288 | tf_op jit(solution)/shard_map/while/body/dot_general | solution.py:175
  121.5 7.3 %fusion.32 = f32[8,256,256]{2,1,0:T(8,128)S(1)} fusion(bf16[4,128,256,1]{2,1,0,3:T(8,128)(2,1)S(1)} %bitcast.146, f32[4,8,128,256]{3,1,0,2:T(8,128)} %bitcast.28), kind=kOutput, calls=%fused_computation.41 | convolution fusion | flops 3221225472 | bytes 6553600 | tf_op jit(solution)/shard_map/lbnf,lng->bfg/dot_general | solution.py:186
  128.8 7.2 %fusion.35 = f32[4,128,256]{2,1,0:T(8,128)} fusion(f32[4,8,128,256]{3,1,0,2:T(8,128)} %bitcast.28, bf16[8,256,256]{2,1,0:T(8,128)(2,1)S(1)} %copy-done), kind=kOutput, calls=%fused_computation.42 | convolution fusion | flops 3221225472 | bytes 5767168 | tf_op jit(solution)/shard_map/lbnf,bfg->lng/dot_general | solution.py:185
  136.0 13.2 %all-to-all-done.1 = bf16[32,272,256]{2,1,0:T(8,128)(2,1)} async-done(((bf16[32,272,256]{2,1,0:T(8,128)(2,1)}), bf16[32,272,256]{2,1,0:T(8,128)(2,1)}, u32[]{:S(2)}, u32[]{:S(2)}) %all-to-all-start.1) | async-done | bytes 4456480 | tf_op jit(solution)/shard_map/all_to_all | solution.py:163
  153.6 8.9 %all-to-all-start.2 = ((f32[128,8,256]{2,1,0:T(8,128)}), f32[128,8,256]{2,1,0:T(8,128)S(1)}, u32[]{:S(2)}, u32[]{:S(2)}) async-start(f32[128,8,256]{2,1,0:T(8,128)} %bitcast.52), calls=%async_computation.2 | async-start | bytes 2097152 | tf_op jit(solution)/shard_map/all_to_all | solution.py:33
  162.8 4.7 %slice.47 = bf16[32,256,256]{2,1,0:T(8,128)(2,1)} slice(bf16[32,272,256]{2,1,0:T(8,128)(2,1)} %all-to-all-done.1), slice={[0:32], [0:256], [0:256]} | slice | bytes 8388608 | tf_op jit(solution)/shard_map/slice | solution.py:200
  167.5 14.8 %all-to-all-done.2 = f32[128,8,256]{2,1,0:T(8,128)S(1)} async-done(((f32[128,8,256]{2,1,0:T(8,128)}), f32[128,8,256]{2,1,0:T(8,128)S(1)}, u32[]{:S(2)}, u32[]{:S(2)}) %all-to-all-start.2) | async-done | bytes 1048608 | tf_op jit(solution)/shard_map/all_to_all | solution.py:33
  183.5 3.8 %all-to-all-start.3 = ((f32[128,8,256]{2,1,0:T(8,128)}), f32[128,8,256]{2,1,0:T(8,128)S(1)}, u32[]{:S(2)}, u32[]{:S(2)}) async-start(f32[128,8,256]{2,1,0:T(8,128)} %bitcast.54), calls=%async_computation.3 | async-start | bytes 2097152 | tf_op jit(solution)/shard_map/all_to_all | solution.py:41
  187.3 4.5 %fusion.26 = f32[4,128,256]{2,0,1:T(4,128)S(1)} fusion(bf16[64,128,256]{2,1,0:T(8,128)(2,1)} %bitcast.137, s32[64]{0:T(128)S(1)} %eq.128), kind=kOutput, calls=%fused_computation.33 | convolution fusion | flops 16777472 | bytes 4718848 | tf_op jit(solution)/shard_map/dot_general | solution.py:198
  195.4 2.5 %collective-permute-start.1 = (f32[256,256]{1,0:T(8,128)}, f32[256,256]{1,0:T(8,128)}, u32[]{:S(2)}, u32[]{:S(2)}) collective-permute-start(f32[256,256]{1,0:T(8,128)} %get-tuple-element.289), channel_id=1, source_target_pairs={{0,2},{1,3},{2,0},{3,1},{4,6},{5,7},{6,4},{7,5},{8,10},{9,11},{10,... | collective-permute-start | bytes 786440 | tf_op jit(solution)/shard_map/ppermute | solution.py:59
  199.1 8.8 %collective-permute-done = f32[256,256]{1,0:T(8,128)} collective-permute-done((f32[256,256]{1,0:T(8,128)}, f32[256,256]{1,0:T(8,128)}, u32[]{:S(2)}, u32[]{:S(2)}) %collective-permute-start) | collective-permute-done | bytes 262176 | tf_op jit(solution)/shard_map/ppermute | solution.py:59
  207.8 5.7 %collective-permute-done.1 = f32[256,256]{1,0:T(8,128)} collective-permute-done((f32[256,256]{1,0:T(8,128)}, f32[256,256]{1,0:T(8,128)}, u32[]{:S(2)}, u32[]{:S(2)}) %collective-permute-start.1) | collective-permute-done | bytes 262176 | tf_op jit(solution)/shard_map/ppermute | solution.py:59
  215.5 2.5 %collective-permute-start.4 = (f32[256,256]{1,0:T(8,128)}, f32[256,256]{1,0:T(8,128)S(1)}, u32[]{:S(2)}, u32[]{:S(2)}) collective-permute-start(f32[256,256]{1,0:T(8,128)} %fusion.42), channel_id=1, source_target_pairs={{0,2},{1,3},{2,0},{3,1},{4,6},{5,7},{6,4},{7,5},{8,10},{9,11},{10,... | collective-permute-start | bytes 786440 | tf_op jit(solution)/shard_map/ppermute | solution.py:63
  223.9 5.9 %collective-permute-done.4 = f32[256,256]{1,0:T(8,128)S(1)} collective-permute-done((f32[256,256]{1,0:T(8,128)}, f32[256,256]{1,0:T(8,128)S(1)}, u32[]{:S(2)}, u32[]{:S(2)}) %collective-permute-start.4) | collective-permute-done | bytes 262176 | tf_op jit(solution)/shard_map/ppermute | solution.py:63
  238.2 3.2 %maximum_select_fusion = f32[2048,256]{1,0:T(8,128)} fusion(f32[1024,256]{1,0:T(8,128)} %collective-permute-done.7, f32[1024,256]{1,0:T(8,128)S(1)} %bitcast.141, pred[]{:T(512)S(6)} %eq.132), kind=kLoop, calls=%fused_computation.40 | loop fusion | flops 1572864 | bytes 4194305 | tf_op jit(solution)/shard_map/jit(_where)/select_n | solution.py:45
  (80 shorter events, 36.2 us)
Async XLA Ops:
  0.6 19.2 %copy-start = (bf16[8,256,256]{2,1,0:T(8,128)(2,1)S(1)}, bf16[8,256,256]{2,1,0:T(8,128)(2,1)}, u32[]{:S(2)}) copy-start(bf16[8,256,256]{2,1,0:T(8,128)(2,1)} %param.16) | copy-start | bytes 3145732
  0.6 2.3 copy-start.2
  9.6 10.3 %copy-start.4 = (bf16[512,256]{1,0:T(8,128)(2,1)S(1)}, bf16[512,256]{1,0:T(8,128)(2,1)}, u32[]{:S(2)}) copy-start(bf16[512,256]{1,0:T(8,128)(2,1)} %param.25) | copy-start | bytes 786436
  9.6 65.9 %all-to-all-start = ((bf16[32,272,256]{2,1,0:T(8,128)(2,1)}), bf16[32,272,256]{2,1,0:T(8,128)(2,1)}, u32[]{:S(2)}, u32[]{:S(2)}) async-start(bf16[32,272,256]{2,1,0:T(8,128)(2,1)} %pad_maximum_fusion), calls=%async_computation | async-start | bytes 8912896 | tf_op jit(solution)/shard_map/all_to_all | solution.py:132
  22.6 5.4 %copy-start.13 = (f32[200,8]{0,1:T(8,128)S(1)}, f32[200,8]{0,1:T(8,128)}, u32[]{:S(2)}) copy-start(f32[200,8]{0,1:T(8,128)} %param.18) | copy-start | bytes 19204
  22.6 5.4 %copy-start.14 = (s32[1,1,64]{2,1,0:T(1,128)S(1)}, s32[1,1,64]{2,1,0:T(1,128)}, u32[]{:S(2)}) copy-start(s32[1,1,64]{2,1,0:T(1,128)} %param.22) | copy-start | bytes 772
  28.2 4.4 %copy-start.1 = (bf16[1,1,64,128,128]{4,3,2,1,0:T(8,128)(2,1)S(1)}, bf16[1,1,64,128,128]{4,3,2,1,0:T(8,128)(2,1)}, u32[]{:S(2)}) copy-start(bf16[1,1,64,128,128]{4,3,2,1,0:T(8,128)(2,1)} %param.19) | copy-start | bytes 6291460
  28.2 4.4 %copy-start.10 = (s32[1,1,64]{2,1,0:T(1,128)S(1)}, s32[1,1,64]{2,1,0:T(1,128)}, u32[]{:S(2)}) copy-start(s32[1,1,64]{2,1,0:T(1,128)} %param.20) | copy-start | bytes 772
  28.2 4.4 %copy-start.11 = (s32[1,1,64]{2,1,0:T(1,128)S(1)}, s32[1,1,64]{2,1,0:T(1,128)}, u32[]{:S(2)}) copy-start(s32[1,1,64]{2,1,0:T(1,128)} %param.21) | copy-start | bytes 772
  86.6 62.7 %all-to-all-start.1 = ((bf16[32,272,256]{2,1,0:T(8,128)(2,1)}), bf16[32,272,256]{2,1,0:T(8,128)(2,1)}, u32[]{:S(2)}, u32[]{:S(2)}) async-start(bf16[32,272,256]{2,1,0:T(8,128)(2,1)} %pad_maximum_fusion.1), calls=%async_computation.1 | async-start | bytes 8912896 | tf_op jit(solution)/shard_map/all_to_all | solution.py:163
  106.1 15.3 %copy-start.5 = (bf16[512,256]{1,0:T(8,128)(2,1)S(1)}, bf16[512,256]{1,0:T(8,128)(2,1)}, u32[]{:S(2)}) copy-start(bf16[512,256]{1,0:T(8,128)(2,1)} %param.25) | copy-start | bytes 786436
  136.0 26.6 %copy-start.12 = (s32[1,1,32,2]{2,3,1,0:T(2,128)S(1)}, s32[1,1,32,2]{2,3,1,0:T(2,128)}, u32[]{:S(2)}) copy-start(s32[1,1,32,2]{2,3,1,0:T(2,128)} %param.24) | copy-start | bytes 772
  149.5 3.1 %collective-permute-start.6 = (f32[1024,256]{1,0:T(8,128)S(1)}, f32[1024,256]{1,0:T(8,128)S(1)}, u32[]{:S(2)}, u32[]{:S(2)}) collective-permute-start(f32[1024,256]{1,0:T(8,128)S(1)} %bitcast.152), channel_id=1, source_target_pairs={{0,4},{4,0},{8,12},{12,8},{16,20},{20,16},{24,28},{28,24},{32,36},... | collective-permute-start | bytes 3145736 | tf_op jit(solution)/shard_map/ppermute | solution.py:32
  153.6 28.7 %all-to-all-start.2 = ((f32[128,8,256]{2,1,0:T(8,128)}), f32[128,8,256]{2,1,0:T(8,128)S(1)}, u32[]{:S(2)}, u32[]{:S(2)}) async-start(f32[128,8,256]{2,1,0:T(8,128)} %bitcast.52), calls=%async_computation.2 | async-start | bytes 2097152 | tf_op jit(solution)/shard_map/all_to_all | solution.py:33
  183.5 34.9 %all-to-all-start.3 = ((f32[128,8,256]{2,1,0:T(8,128)}), f32[128,8,256]{2,1,0:T(8,128)S(1)}, u32[]{:S(2)}, u32[]{:S(2)}) async-start(f32[128,8,256]{2,1,0:T(8,128)} %bitcast.54), calls=%async_computation.3 | async-start | bytes 2097152 | tf_op jit(solution)/shard_map/all_to_all | solution.py:41
  194.0 41.2 %copy-start.3 = (bf16[512,256]{1,0:T(8,128)(2,1)S(1)}, bf16[512,256]{1,0:T(8,128)(2,1)}, u32[]{:S(2)}) copy-start(bf16[512,256]{1,0:T(8,128)(2,1)} %param.15) | copy-start | bytes 786436
  194.0 41.2 %copy-start.6 = (bf16[256,256]{1,0:T(8,128)(2,1)S(1)}, bf16[256,256]{1,0:T(8,128)(2,1)}, u32[]{:S(2)}) copy-start(bf16[256,256]{1,0:T(8,128)(2,1)} %param.17) | copy-start | bytes 393220
  194.0 13.9 %collective-permute-start = (f32[256,256]{1,0:T(8,128)}, f32[256,256]{1,0:T(8,128)}, u32[]{:S(2)}, u32[]{:S(2)}) collective-permute-start(f32[256,256]{1,0:T(8,128)} %get-tuple-element.287), channel_id=1, source_target_pairs={{0,1},{1,2},{2,3},{3,0},{4,5},{5,6},{6,7},{7,4},{8,9},{9,10},{10,1... | collective-permute-start | bytes 786440 | tf_op jit(solution)/shard_map/ppermute | solution.py:59
  195.4 18.2 %collective-permute-start.1 = (f32[256,256]{1,0:T(8,128)}, f32[256,256]{1,0:T(8,128)}, u32[]{:S(2)}, u32[]{:S(2)}) collective-permute-start(f32[256,256]{1,0:T(8,128)} %get-tuple-element.289), channel_id=1, source_target_pairs={{0,2},{1,3},{2,0},{3,1},{4,6},{5,7},{6,4},{7,5},{8,10},{9,11},{10,... | collective-permute-start | bytes 786440 | tf_op jit(solution)/shard_map/ppermute | solution.py:59
  197.9 15.6 %collective-permute-start.2 = (f32[256,256]{1,0:T(8,128)}, f32[256,256]{1,0:T(8,128)}, u32[]{:S(2)}, u32[]{:S(2)}) collective-permute-start(f32[256,256]{1,0:T(8,128)} %get-tuple-element.288), channel_id=1, source_target_pairs={{0,3},{1,0},{2,1},{3,2},{4,7},{5,4},{6,5},{7,6},{8,11},{9,8},{10,9... | collective-permute-start | bytes 786440 | tf_op jit(solution)/shard_map/ppermute | solution.py:59
  215.5 8.5 %collective-permute-start.3 = (f32[256,256]{1,0:T(8,128)}, f32[256,256]{1,0:T(8,128)S(1)}, u32[]{:S(2)}, u32[]{:S(2)}) collective-permute-start(f32[256,256]{1,0:T(8,128)} %fusion.42), channel_id=1, source_target_pairs={{0,1},{1,2},{2,3},{3,0},{4,5},{5,6},{6,7},{7,4},{8,9},{9,10},{10,1... | collective-permute-start | bytes 786440 | tf_op jit(solution)/shard_map/ppermute | solution.py:63
  215.5 14.4 %collective-permute-start.4 = (f32[256,256]{1,0:T(8,128)}, f32[256,256]{1,0:T(8,128)S(1)}, u32[]{:S(2)}, u32[]{:S(2)}) collective-permute-start(f32[256,256]{1,0:T(8,128)} %fusion.42), channel_id=1, source_target_pairs={{0,2},{1,3},{2,0},{3,1},{4,6},{5,7},{6,4},{7,5},{8,10},{9,11},{10,... | collective-permute-start | bytes 786440 | tf_op jit(solution)/shard_map/ppermute | solution.py:63
  218.0 12.4 %collective-permute-start.5 = (f32[256,256]{1,0:T(8,128)}, f32[256,256]{1,0:T(8,128)S(1)}, u32[]{:S(2)}, u32[]{:S(2)}) collective-permute-start(f32[256,256]{1,0:T(8,128)} %fusion.42), channel_id=1, source_target_pairs={{0,3},{1,0},{2,1},{3,2},{4,7},{5,4},{6,5},{7,6},{8,11},{9,8},{10,9... | collective-permute-start | bytes 786440 | tf_op jit(solution)/shard_map/ppermute | solution.py:63
  218.4 19.7 %collective-permute-start.7 = (f32[1024,256]{1,0:T(8,128)S(1)}, f32[1024,256]{1,0:T(8,128)}, u32[]{:S(2)}, u32[]{:S(2)}) collective-permute-start(f32[1024,256]{1,0:T(8,128)S(1)} %bitcast.140), channel_id=1, source_target_pairs={{0,4},{4,0},{8,12},{12,8},{16,20},{20,16},{24,28},{28,24},{32,36},... | collective-permute-start | bytes 3145736 | tf_op jit(solution)/shard_map/ppermute | solution.py:44
  223.9 6.4 %copy-start.7 = (f32[256,256]{1,0:T(8,128)}, f32[256,256]{1,0:T(8,128)S(1)}, u32[]{:S(2)}) copy-start(f32[256,256]{1,0:T(8,128)S(1)} %collective-permute-done.3) | copy-start | bytes 786436
  229.8 0.7 copy-start.8
  230.3 0.7 copy-start.9

commit v9 on v8

--- a/solution.py
+++ b/solution.py
@@ -184,8 +184,9 @@
     root_term = jnp.dot(features, root, preferred_element_type=jnp.float32)
     projected_part = jnp.einsum("lbnf,bfg->lng", partial_value, basis_f32, precision=highest)
     basis_local = jnp.einsum("lbnf,lng->bfg", partial_value, cot_f32, precision=highest)
-    returned, basis_local, projected_part = lax.optimization_barrier(
-        (returned, basis_local, projected_part)
+    projected = permute_psum(projected_part.reshape(-1, feat_width), "rel")
+    returned, basis_local, projected = lax.optimization_barrier(
+        (returned, basis_local, projected)
     )
 
     basis_grad = pair_psum(basis_local.reshape(-1, basis_local.shape[-1])).reshape(
@@ -201,12 +202,7 @@
         (((1,), (0,)), ((), ())),
         precision=highest,
     )
-    both = jnp.concatenate(
-        [projected_part.reshape(-1, feat_width), own_grads.reshape(-1, feat_width)]
-    )
-    summed_both = permute_psum(both, "rel")
-    projected = summed_both[: features.shape[0]]
-    summed = summed_both[features.shape[0] :]
+    summed = permute_psum(own_grads.reshape(-1, feat_width), "rel")
     output = (projected + root_term).astype(jnp.bfloat16)
     root_back = lax.dot_general(
         cotangent, root, (((1,), (1,)), ((), ())), preferred_element_type=jnp.float32

time: 246 us -> 230 us (0.935)
  waiting for transfers between devices: 53.2 us -> 21.2 us
  blocking collectives: 0 us -> 28 us
  other arithmetic: 19.7 us -> 15.3 us
  local copies, waits for them, and re-layouts: 52.4 us -> 48.8 us
    all_to_all x0 -> x1, blocking collectives: none -> 28 us  [pair_psum(): lax.all_to_all(chip_sum.reshape((count, half // count) + value.shape[1:])...]
    all_to_all x1 -> x0, waiting for transfers between devices: 14.8 us -> none  [pair_psum(): lax.all_to_all(chip_sum.reshape((count, half // count) + value.shape[1:])...]
    all_to_all x1, waiting for transfers between devices: 13.2 us -> 0.89 us  [on_device(): lax.all_to_all(slot_out, 'rows', split_axis=0, concat_axis=0, tiled=True)]
    ppermute x3 -> x6, waiting for transfers between devices: 14.5 us -> 5.11 us  [permute_psum(): total = total + lax.ppermute(chunks[(me + shift) % size], axis, pairs)]
    all_to_all x1 -> x0, starting transfers between devices: 8.95 us -> none  [pair_psum(): lax.all_to_all(chip_sum.reshape((count, half // count) + value.shape[1:])...]
    all_to_all x1, waiting for transfers between devices: 0.01 us -> 8.46 us  [pair_psum(): lax.all_to_all(outgoing, ('rows', 'rel'), 0, 0, tiled=True)]
    ppermute x3 -> x6, starting transfers between devices: 5.06 us -> 10.3 us  [permute_psum(): total = total + lax.ppermute(chunks[(me + shift) % size], axis, pairs)]
    ppermute x3 -> x6, starting transfers between devices: 2.95 us -> 7.2 us  [permute_psum(): parts.append(lax.ppermute(total, axis, pairs))]
  transfers between devices with their start and end apart: 12 -> 17, of which waited for: 8 -> 8; matrix products, arithmetic and copies ran while one was open for 49% -> 48% of each run, Pallas kernels for 0% -> 0%
where the time goes in v9:
time: 230 us; the launch traced here: 227 us
  matrix products  71.2 us (31%)
  local copies, waits for them, and re-layouts  48.8 us (21%)
  starting transfers between devices  39.5 us (17%)
  blocking collectives  28 us (12%)
  waiting for transfers between devices  21.2 us (9%)
  other arithmetic  15.3 us (7%)
    all_to_all x1, blocking collectives, pair_psum(): lax.all_to_all(chip_sum.reshape((count, half // count) + value.shape[1:])...  28 us
    dot_general x1, matrix products, backward_step(): lax.dot_general(slot_hot, backward_term, contract_first, precision=highest)  14.3 us
    dot_general x1, matrix products, backward_step(): lax.dot_general(weights, agg_grad, (((1,), (0,)), ((), ())), precision=hi...  11.5 us
    dot_general x1, matrix products, forward_step(): lax.dot_general(weights, messages, contract_first, precision=highest)  11 us
    ppermute x6, starting transfers between devices, permute_psum(): total = total + lax.ppermute(chunks[(me + shift) % size], axis, pairs)  10.3 us
    all_to_all x1, starting transfers between devices, on_device(): lax.all_to_all(outgoing, 'rows', split_axis=0, concat_axis=0, tiled=True)  9.6 us
    dot_general x1, local copies, waits for them, and re-layouts, backward_step(): jnp.einsum('tij,tif->tjf', adjacency, spread, preferred_element_type=jnp....  9.21 us
    all_to_all x1, waiting for transfers between devices, pair_psum(): lax.all_to_all(outgoing, ('rows', 'rel'), 0, 0, tiled=True)  8.46 us
  transfers between devices with their start and end apart: 17, of which 8 were waited for; matrix products, arithmetic and copies ran while one was open for 48% of the time, Pallas kernels for 0%

profile of v9, /device:TPU:1, one launch (start us, length us, event | category | flops | bytes accessed | tf_op | source)
XLA Modules:
  0.0 226.6 jit_solution(13238192524749843638)
XLA Ops:
  3.0 2.8 %gather_fusion = bf16[64,128,256]{2,1,0:T(8,128)(2,1)} fusion(bf16[4,128,256]{2,1,0:T(8,128)(2,1)S(1)} %bitcast.152, s32[1024]{0:T(1024)S(1)} %pad_clamp_fusion.2), kind=kCustom, calls=%fused_computation | custom fusion | bytes 8388864 | tf_op jit(solution)/shard_map/gather | solution.py:130
  5.8 3.8 %pad_maximum_fusion = bf16[32,272,256]{2,1,0:T(8,128)(2,1)} fusion(bf16[32,8,256]{2,1,0:T(8,128)(2,1)S(1)} %subtract_convert_fusion.1, bf16[32,8,256]{2,1,0:T(8,128)(2,1)S(1)} %get-tuple-element.292, bf16[32,256,256]{2,1,0:T(8,128)(2,1)} %bitcast.155), kind=kLoop, calls=%fused_computation.32 | loop fusion | flops 13369344 | bytes 8912896 | tf_op jit(solution)/shard_map/concatenate | solution.py:131
  9.5 9.6 %all-to-all-start = ((bf16[32,272,256]{2,1,0:T(8,128)(2,1)}), bf16[32,272,256]{2,1,0:T(8,128)(2,1)}, u32[]{:S(2)}, u32[]{:S(2)}) async-start(bf16[32,272,256]{2,1,0:T(8,128)(2,1)} %pad_maximum_fusion), calls=%async_computation | async-start | bytes 8912896 | tf_op jit(solution)/shard_map/all_to_all | solution.py:132
  19.8 2.7 %convolution_bitcast_fusion = f32[4,8,128,256]{2,3,0,1:T(8,128)} fusion(bf16[4,128,256,1]{2,1,0,3:T(8,128)(2,1)S(1)} %bitcast.161, bf16[8,256,256]{2,1,0:T(8,128)(2,1)S(1)} %copy-done), kind=kOutput, calls=%fused_computation.40 | convolution fusion | flops 536870912 | bytes 5505024 | tf_op jit(solution)/shard_map/lng,bfg->lbnf/dot_general | solution.py:137
  22.5 5.4 %copy.21 = f32[4,8,128,256]{3,2,1,0:T(8,128)} copy(f32[4,8,128,256]{2,3,0,1:T(8,128)} %convolution_bitcast_fusion) | data formatting | bytes 8388608 | tf_op jit(solution)/shard_map/lng,bfg->lbnf/transpose | solution.py:137
  28.2 4.3 %broadcast_in_dim.20 = f32[64,128,256]{2,0,1:T(8,128)} broadcast(f32[]{:T(128)} %constant.105.clone.1), dimensions={} | broadcast | bytes 8388612 | tf_op jit(solution)/shard_map/broadcast_in_dim | solution.py:154
  32.5 42.8 %while.24 = (s32[]{:T(128)}, f32[64,128,256]{2,0,1:T(8,128)}, s32[]{:T(128)}, s32[1,1,64]{2,1,0:T(1,128)S(1)}, s32[1,1,64]{2,1,0:T(1,128)S(1)}, /*index=5*/s32[]...) while((s32[]{:T(128)}, f32[64,128,256]{2,0,1:T(8,128)}, ...), condition=%wide.region_1.2_spmd, body=%wide.region_0.1_spmd.sunk | while | flops 2954894080 | bytes 65016960 | solution.py:155
  33.4 11.5 %fusion.89 = bf16[64,128,256]{2,0,1:T(8,128)(2,1)S(1)} fusion(f32[32,128,256]{2,1,0:T(8,128)} %get-tuple-element.429, f32[64,8]{0,1:T(8,128)S(1)} %get-tuple-element.428, f32[64,4]{0,1:T(4,128)S(1)} %fusion.88), kind=kOutput, calls=%fused_computation.8.clone.1 | convolution fusion | flops 805308416 | bytes 8391680 | tf_op jit(solution)/shard_map/while/body/dot_general | solution.py:143
  44.9 6.6 %fusion.90 = f32[64,256,128]{2,1,0:T(8,128)} fusion(bf16[64,128,128]{2,1,0:T(8,128)(2,1)S(1)} %get-tuple-element.430, bf16[64,128,256]{2,0,1:T(8,128)(2,1)S(1)} %fusion.89), kind=kOutput, calls=%fused_computation.7.clone.1 | convolution fusion | flops 536870912 | bytes 14680064 | tf_op jit(solution)/shard_map/while/body/tij,tif->tjf/dot_general | solution.py:146
  51.4 9.2 %copy.71 = f32[64,256,128]{1,0,2:T(8,128)} copy(f32[64,256,128]{2,1,0:T(8,128)} %fusion.90) | data formatting | bytes 16777216 | tf_op jit(solution)/shard_map/while/body/tij,tif->tjf/dot_general | solution.py:146
  60.6 14.3 %fusion.91 = f32[64,128,256]{2,0,1:T(8,128)} fusion(f32[64,128,256]{2,0,1:T(8,128)} %get-tuple-element.412, f32[64,256,128]{1,0,2:T(8,128)} %copy.71, s32[64]{0:T(128)S(1)} %bitcast.179), kind=kOutput, calls=%fused_computation.10.clone.1 | convolution fusion | flops 1612713984 | bytes 25166080 | tf_op jit(solution)/shard_map/while/body/dot_general | solution.py:150
  76.4 4.9 %slice.34 = bf16[32,256,256]{2,1,0:T(8,128)(2,1)} slice(bf16[32,272,256]{2,1,0:T(8,128)(2,1)} %all-to-all-done), slice={[0:32], [0:256], [0:256]} | slice | bytes 8388608 | tf_op jit(solution)/shard_map/slice | solution.py:166
  82.6 4.5 %copy.61 = bf16[64,128,256]{2,1,0:T(8,128)(2,1)S(1)} copy(f32[64,128,256]{2,0,1:T(8,128)S(1)} %copy-done.1) | data formatting | bytes 12582912 | tf_op jit(solution)/shard_map/optimization_barrier | solution.py:156
  89.3 7.4 %all-to-all-start.1 = ((bf16[32,272,256]{2,1,0:T(8,128)(2,1)}), bf16[32,272,256]{2,1,0:T(8,128)(2,1)}, u32[]{:S(2)}, u32[]{:S(2)}) async-start(bf16[32,272,256]{2,1,0:T(8,128)(2,1)} %pad_maximum_fusion.1), calls=%async_computation.1 | async-start | bytes 8912896 | tf_op jit(solution)/shard_map/all_to_all | solution.py:163
  96.7 5.1 %gather_fusion.1 = bf16[64,128,256]{2,1,0:T(8,128)(2,1)} fusion(bf16[64,128,256]{2,1,0:T(8,128)(2,1)} %bitcast.154, s32[1024]{0:T(1024)S(1)} %pad_clamp_fusion.1), kind=kCustom, calls=%fused_computation.1 | custom fusion | bytes 8388864 | tf_op jit(solution)/shard_map/while/body/gather | solution.py:170
  101.8 2.5 %broadcast_in_dim.31 = f32[32,128,256]{2,0,1:T(8,128)} broadcast(f32[]{:T(128)} %constant.105.clone.1), dimensions={} | broadcast | bytes 4194308 | tf_op jit(solution)/shard_map/broadcast_in_dim | solution.py:179
  104.3 15.2 %while.25 = (s32[]{:T(128)}, f32[32,128,256]{2,0,1:T(8,128)}, s32[]{:T(128)}, s32[1,1,64]{2,1,0:T(1,128)S(1)}, s32[]{:T(128)}, /*index=5*/f32[64,8]{0,1:T(8,128)...) while((s32[]{:T(128)}, f32[32,128,256]{2,0,1:T(8,128)}, ...), condition=%wide.region_4.5_spmd, body=%wide.region_3.4_spmd.sunk | while | flops 1343228672 | bytes 31462264 | solution.py:180
  104.9 3.4 %fusion.96 = f32[64,128,256]{2,1,0:T(8,128)S(1)} fusion(bf16[64,128,128]{2,1,0:T(8,128)(2,1)S(1)} %get-tuple-element.459, bf16[64,128,256]{2,1,0:T(8,128)(2,1)} %get-tuple-element.460), kind=kOutput, calls=%fused_computation.95.clone.1 | convolution fusion | flops 536870912 | bytes 14680064 | tf_op jit(solution)/shard_map/while/body/tij,tjf->tif/dot_general | solution.py:171
  108.4 11.0 %fusion.98 = f32[32,128,256]{2,0,1:T(8,128)} fusion(f32[32,128,256]{2,0,1:T(8,128)} %get-tuple-element.444, f32[64,128,256]{2,1,0:T(8,128)S(1)} %fusion.96, f32[64,8]{0,1:T(8,128)S(1)} %get-tuple-element.458, f32[64,4]{0,1:T(4,128)S(1)} %fusion.97), kind=kOutput, calls=%fused_computation.23.clone.1 | convolution fusion | flops 806356992 | bytes 16780288 | tf_op jit(solution)/shard_map/while/body/dot_general | solution.py:175
  119.5 6.5 %fusion.35 = f32[4,128,256]{2,1,0:T(8,128)S(1)} fusion(f32[4,8,128,256]{3,1,0,2:T(8,128)} %bitcast.28, bf16[8,256,256]{2,1,0:T(8,128)(2,1)S(1)} %copy-done), kind=kOutput, calls=%fused_computation.43 | convolution fusion | flops 3221225472 | bytes 5767168 | tf_op jit(solution)/shard_map/lbnf,bfg->lng/dot_general | solution.py:185
  127.4 2.6 %collective-permute-start.1 = (f32[128,256]{1,0:T(8,128)S(1)}, f32[128,256]{1,0:T(8,128)S(1)}, u32[]{:S(2)}, u32[]{:S(2)}) collective-permute-start(f32[128,256]{1,0:T(8,128)S(1)} %get-tuple-element.291), channel_id=1, source_target_pairs={{0,2},{1,3},{2,0},{3,1},{4,6},{5,7},{6,4},{7,5},{8,10},{9,11},{10,... | collective-permute-start | bytes 393224 | tf_op jit(solution)/shard_map/ppermute | solution.py:59
  132.3 3.9 %collective-permute-done.1 = f32[128,256]{1,0:T(8,128)S(1)} collective-permute-done((f32[128,256]{1,0:T(8,128)S(1)}, f32[128,256]{1,0:T(8,128)S(1)}, u32[]{:S(2)}, u32[]{:S(2)}) %collective-permute-start.1) | collective-permute-done | bytes 131104 | tf_op jit(solution)/shard_map/ppermute | solution.py:59
  140.5 7.3 %fusion.32 = f32[8,256,256]{2,1,0:T(8,128)S(1)} fusion(bf16[4,128,256,1]{2,1,0,3:T(8,128)(2,1)S(1)} %bitcast.162, f32[4,8,128,256]{3,1,0,2:T(8,128)} %bitcast.28), kind=kOutput, calls=%fused_computation.42 | convolution fusion | flops 3221225472 | bytes 6553600 | tf_op jit(solution)/shard_map/lbnf,lng->bfg/dot_general | solution.py:186
  148.7 2.4 %gather_fusion.2 = f32[4,128,256]{2,1,0:T(8,128)} fusion(f32[4,128,256]{2,1,0:T(8,128)} %pad_maximum_fusion.2, s32[1024]{0:T(1024)S(1)} %pad_clamp_fusion), kind=kCustom, calls=%fused_computation.2 | custom fusion | bytes 1048592 | tf_op jit(solution)/shard_map/gather | solution.py:66
  155.9 28.0 %all_to_all.20 = f32[128,8,256]{2,1,0:T(8,128)S(1)} all-to-all(f32[128,8,256]{2,1,0:T(8,128)S(1)} %bitcast.159), channel_id=1, replica_groups=mesh['rows'=32,'rel'=4] {'rows','rel'}, dimensions={0} | all-to-all | bytes 2097152 | tf_op jit(solution)/shard_map/all_to_all | solution.py:33
  185.0 3.6 %all-to-all-start.3 = ((f32[128,8,256]{2,1,0:T(8,128)}), f32[128,8,256]{2,1,0:T(8,128)S(1)}, u32[]{:S(2)}, u32[]{:S(2)}) async-start(f32[128,8,256]{2,1,0:T(8,128)} %bitcast.55), calls=%async_computation.3 | async-start | bytes 2097152 | tf_op jit(solution)/shard_map/all_to_all | solution.py:41
  188.8 2.5 %slice.35 = bf16[32,256,256]{2,1,0:T(8,128)(2,1)S(1)} slice(bf16[32,272,256]{2,1,0:T(8,128)(2,1)} %all-to-all-done.1), slice={[0:32], [0:256], [0:256]} | slice | bytes 8388608 | tf_op jit(solution)/shard_map/slice | solution.py:201
  191.3 2.3 %fusion.26 = f32[4,128,256]{2,0,1:T(4,128)S(1)} fusion(bf16[64,128,256]{2,1,0:T(8,128)(2,1)S(1)} %bitcast.156, s32[64]{0:T(128)S(1)} %eq.132), kind=kOutput, calls=%fused_computation.34 | convolution fusion | flops 16777472 | bytes 4718848 | tf_op jit(solution)/shard_map/dot_general | solution.py:199
  195.6 2.6 %collective-permute-start.7 = (f32[128,256]{1,0:T(8,128)S(1)}, f32[128,256]{1,0:T(8,128)S(1)}, u32[]{:S(2)}, u32[]{:S(2)}) collective-permute-start(f32[128,256]{1,0:T(8,128)S(1)} %bitcast.169), channel_id=1, source_target_pairs={{0,2},{1,3},{2,0},{3,1},{4,6},{5,7},{6,4},{7,5},{8,10},{9,11},{10,... | collective-permute-start | bytes 393224 | tf_op jit(solution)/shard_map/ppermute | solution.py:59
  200.0 8.5 %all-to-all-done.3 = f32[128,8,256]{2,1,0:T(8,128)S(1)} async-done(((f32[128,8,256]{2,1,0:T(8,128)}), f32[128,8,256]{2,1,0:T(8,128)S(1)}, u32[]{:S(2)}, u32[]{:S(2)}) %all-to-all-start.3) | async-done | bytes 1048608 | tf_op jit(solution)/shard_map/all_to_all | solution.py:41
  216.6 3.1 %collective-permute-done.10 = f32[128,256]{1,0:T(8,128)S(1)} collective-permute-done((f32[128,256]{1,0:T(8,128)S(1)}, f32[128,256]{1,0:T(8,128)S(1)}, u32[]{:S(2)}, u32[]{:S(2)}) %collective-permute-start.10) | collective-permute-done | bytes 131104 | tf_op jit(solution)/shard_map/ppermute | solution.py:63
  223.3 3.2 %maximum_select_fusion = f32[2048,256]{1,0:T(8,128)} fusion(f32[1024,256]{1,0:T(8,128)} %collective-permute-done.13, f32[1024,256]{1,0:T(8,128)S(1)} %bitcast.158, pred[]{:T(512)S(6)} %eq.136), kind=kLoop, calls=%fused_computation.41 | loop fusion | flops 1572864 | bytes 4194305 | tf_op jit(solution)/shard_map/jit(_where)/select_n | solution.py:45
  (91 shorter events, 38.8 us)
Async XLA Ops:
  0.6 19.2 %copy-start = (bf16[8,256,256]{2,1,0:T(8,128)(2,1)S(1)}, bf16[8,256,256]{2,1,0:T(8,128)(2,1)}, u32[]{:S(2)}) copy-start(bf16[8,256,256]{2,1,0:T(8,128)(2,1)} %param.16) | copy-start | bytes 3145732
  0.6 2.3 %copy-start.3 = (bf16[512,256]{1,0:T(8,128)(2,1)S(1)}, bf16[512,256]{1,0:T(8,128)(2,1)}, u32[]{:S(2)}) copy-start(bf16[512,256]{1,0:T(8,128)(2,1)} %param.15) | copy-start | bytes 786436
  9.5 10.3 %copy-start.5 = (bf16[512,256]{1,0:T(8,128)(2,1)S(1)}, bf16[512,256]{1,0:T(8,128)(2,1)}, u32[]{:S(2)}) copy-start(bf16[512,256]{1,0:T(8,128)(2,1)} %param.25) | copy-start | bytes 786436
  9.5 65.8 %all-to-all-start = ((bf16[32,272,256]{2,1,0:T(8,128)(2,1)}), bf16[32,272,256]{2,1,0:T(8,128)(2,1)}, u32[]{:S(2)}, u32[]{:S(2)}) async-start(bf16[32,272,256]{2,1,0:T(8,128)(2,1)} %pad_maximum_fusion), calls=%async_computation | async-start | bytes 8912896 | tf_op jit(solution)/shard_map/all_to_all | solution.py:132
  22.5 5.4 %copy-start.11 = (f32[200,8]{0,1:T(8,128)S(1)}, f32[200,8]{0,1:T(8,128)}, u32[]{:S(2)}) copy-start(f32[200,8]{0,1:T(8,128)} %param.18) | copy-start | bytes 19204
  22.5 5.4 %copy-start.12 = (s32[1,1,64]{2,1,0:T(1,128)S(1)}, s32[1,1,64]{2,1,0:T(1,128)}, u32[]{:S(2)}) copy-start(s32[1,1,64]{2,1,0:T(1,128)} %param.22) | copy-start | bytes 772
  28.1 4.4 %copy-start.2 = (bf16[1,1,64,128,128]{4,3,2,1,0:T(8,128)(2,1)S(1)}, bf16[1,1,64,128,128]{4,3,2,1,0:T(8,128)(2,1)}, u32[]{:S(2)}) copy-start(bf16[1,1,64,128,128]{4,3,2,1,0:T(8,128)(2,1)} %param.19) | copy-start | bytes 6291460
  28.1 4.4 %copy-start.8 = (s32[1,1,64]{2,1,0:T(1,128)S(1)}, s32[1,1,64]{2,1,0:T(1,128)}, u32[]{:S(2)}) copy-start(s32[1,1,64]{2,1,0:T(1,128)} %param.20) | copy-start | bytes 772
  28.1 4.4 %copy-start.9 = (s32[1,1,64]{2,1,0:T(1,128)S(1)}, s32[1,1,64]{2,1,0:T(1,128)}, u32[]{:S(2)}) copy-start(s32[1,1,64]{2,1,0:T(1,128)} %param.21) | copy-start | bytes 772
  76.4 6.2 %copy-start.1 = (f32[64,128,256]{2,0,1:T(8,128)S(1)}, f32[64,128,256]{2,0,1:T(8,128)}, u32[]{:S(2)}) copy-start(f32[64,128,256]{2,0,1:T(8,128)} %get-tuple-element.242) | copy-start | bytes 25165828
  89.3 62.7 %all-to-all-start.1 = ((bf16[32,272,256]{2,1,0:T(8,128)(2,1)}), bf16[32,272,256]{2,1,0:T(8,128)(2,1)}, u32[]{:S(2)}, u32[]{:S(2)}) async-start(bf16[32,272,256]{2,1,0:T(8,128)(2,1)} %pad_maximum_fusion.1), calls=%async_computation.1 | async-start | bytes 8912896 | tf_op jit(solution)/shard_map/all_to_all | solution.py:163
  119.5 21.0 %copy-start.6 = (bf16[512,256]{1,0:T(8,128)(2,1)S(1)}, bf16[512,256]{1,0:T(8,128)(2,1)}, u32[]{:S(2)}) copy-start(bf16[512,256]{1,0:T(8,128)(2,1)} %param.25) | copy-start | bytes 786436
  126.0 6.3 %collective-permute-start = (f32[128,256]{1,0:T(8,128)S(1)}, f32[128,256]{1,0:T(8,128)S(1)}, u32[]{:S(2)}, u32[]{:S(2)}) collective-permute-start(f32[128,256]{1,0:T(8,128)S(1)} %get-tuple-element.289), channel_id=1, source_target_pairs={{0,1},{1,2},{2,3},{3,0},{4,5},{5,6},{6,7},{7,4},{8,9},{9,10},{10,1... | collective-permute-start | bytes 393224 | tf_op jit(solution)/shard_map/ppermute | solution.py:59
  127.4 8.8 %collective-permute-start.1 = (f32[128,256]{1,0:T(8,128)S(1)}, f32[128,256]{1,0:T(8,128)S(1)}, u32[]{:S(2)}, u32[]{:S(2)}) collective-permute-start(f32[128,256]{1,0:T(8,128)S(1)} %get-tuple-element.291), channel_id=1, source_target_pairs={{0,2},{1,3},{2,0},{3,1},{4,6},{5,7},{6,4},{7,5},{8,10},{9,11},{10,... | collective-permute-start | bytes 393224 | tf_op jit(solution)/shard_map/ppermute | solution.py:59
  130.0 6.2 %collective-permute-start.2 = (f32[128,256]{1,0:T(8,128)S(1)}, f32[128,256]{1,0:T(8,128)S(1)}, u32[]{:S(2)}, u32[]{:S(2)}) collective-permute-start(f32[128,256]{1,0:T(8,128)S(1)} %get-tuple-element.290), channel_id=1, source_target_pairs={{0,3},{1,0},{2,1},{3,2},{4,7},{5,4},{6,5},{7,6},{8,11},{9,8},{10,9... | collective-permute-start | bytes 393224 | tf_op jit(solution)/shard_map/ppermute | solution.py:59
  136.3 11.5 %collective-permute-start.3 = (f32[128,256]{1,0:T(8,128)S(1)}, f32[128,256]{1,0:T(8,128)S(1)}, u32[]{:S(2)}, u32[]{:S(2)}) collective-permute-start(f32[128,256]{1,0:T(8,128)S(1)} %fusion.44), channel_id=1, source_target_pairs={{0,1},{1,2},{2,3},{3,0},{4,5},{5,6},{6,7},{7,4},{8,9},{9,10},{10,1... | collective-permute-start | bytes 393224 | tf_op jit(solution)/shard_map/ppermute | solution.py:63
  137.2 10.6 %collective-permute-start.4 = (f32[128,256]{1,0:T(8,128)S(1)}, f32[128,256]{1,0:T(8,128)S(1)}, u32[]{:S(2)}, u32[]{:S(2)}) collective-permute-start(f32[128,256]{1,0:T(8,128)S(1)} %fusion.44), channel_id=1, source_target_pairs={{0,2},{1,3},{2,0},{3,1},{4,6},{5,7},{6,4},{7,5},{8,10},{9,11},{10,... | collective-permute-start | bytes 393224 | tf_op jit(solution)/shard_map/ppermute | solution.py:63
  139.5 8.3 %collective-permute-start.5 = (f32[128,256]{1,0:T(8,128)S(1)}, f32[128,256]{1,0:T(8,128)S(1)}, u32[]{:S(2)}, u32[]{:S(2)}) collective-permute-start(f32[128,256]{1,0:T(8,128)S(1)} %fusion.44), channel_id=1, source_target_pairs={{0,3},{1,0},{2,1},{3,2},{4,7},{5,4},{6,5},{7,6},{8,11},{9,8},{10,9... | collective-permute-start | bytes 393224 | tf_op jit(solution)/shard_map/ppermute | solution.py:63
  152.1 3.6 %collective-permute-start.12 = (f32[1024,256]{1,0:T(8,128)S(1)}, f32[1024,256]{1,0:T(8,128)S(1)}, u32[]{:S(2)}, u32[]{:S(2)}) collective-permute-start(f32[1024,256]{1,0:T(8,128)S(1)} %bitcast.165), channel_id=1, source_target_pairs={{0,4},{4,0},{8,12},{12,8},{16,20},{20,16},{24,28},{28,24},{32,36},... | collective-permute-start | bytes 3145736 | tf_op jit(solution)/shard_map/ppermute | solution.py:32
  155.7 32.9 %copy-start.10 = (s32[1,1,32,2]{2,3,1,0:T(2,128)S(1)}, s32[1,1,32,2]{2,3,1,0:T(2,128)}, u32[]{:S(2)}) copy-start(s32[1,1,32,2]{2,3,1,0:T(2,128)} %param.24) | copy-start | bytes 772
  185.0 23.4 %all-to-all-start.3 = ((f32[128,8,256]{2,1,0:T(8,128)}), f32[128,8,256]{2,1,0:T(8,128)S(1)}, u32[]{:S(2)}, u32[]{:S(2)}) async-start(f32[128,8,256]{2,1,0:T(8,128)} %bitcast.55), calls=%async_computation.3 | async-start | bytes 2097152 | tf_op jit(solution)/shard_map/all_to_all | solution.py:41
  191.3 17.3 %copy-start.4 = (bf16[512,256]{1,0:T(8,128)(2,1)S(1)}, bf16[512,256]{1,0:T(8,128)(2,1)}, u32[]{:S(2)}) copy-start(bf16[512,256]{1,0:T(8,128)(2,1)} %param.15) | copy-start | bytes 786436
  191.3 17.3 %copy-start.7 = (bf16[256,256]{1,0:T(8,128)(2,1)S(1)}, bf16[256,256]{1,0:T(8,128)(2,1)}, u32[]{:S(2)}) copy-start(bf16[256,256]{1,0:T(8,128)(2,1)} %param.17) | copy-start | bytes 393220
  194.1 16.5 %collective-permute-start.6 = (f32[128,256]{1,0:T(8,128)S(1)}, f32[128,256]{1,0:T(8,128)S(1)}, u32[]{:S(2)}, u32[]{:S(2)}) collective-permute-start(f32[128,256]{1,0:T(8,128)S(1)} %bitcast.168), channel_id=1, source_target_pairs={{0,1},{1,2},{2,3},{3,0},{4,5},{5,6},{6,7},{7,4},{8,9},{9,10},{10,1... | collective-permute-start | bytes 393224 | tf_op jit(solution)/shard_map/ppermute | solution.py:59
  195.6 15.0 %collective-permute-start.7 = (f32[128,256]{1,0:T(8,128)S(1)}, f32[128,256]{1,0:T(8,128)S(1)}, u32[]{:S(2)}, u32[]{:S(2)}) collective-permute-start(f32[128,256]{1,0:T(8,128)S(1)} %bitcast.169), channel_id=1, source_target_pairs={{0,2},{1,3},{2,0},{3,1},{4,6},{5,7},{6,4},{7,5},{8,10},{9,11},{10,... | collective-permute-start | bytes 393224 | tf_op jit(solution)/shard_map/ppermute | solution.py:59
  198.9 11.7 %collective-permute-start.8 = (f32[128,256]{1,0:T(8,128)}, f32[128,256]{1,0:T(8,128)S(1)}, u32[]{:S(2)}, u32[]{:S(2)}) collective-permute-start(f32[128,256]{1,0:T(8,128)} %bitcast.126), channel_id=1, source_target_pairs={{0,3},{1,0},{2,1},{3,2},{4,7},{5,4},{6,5},{7,6},{8,11},{9,8},{10,9... | collective-permute-start | bytes 393224 | tf_op jit(solution)/shard_map/ppermute | solution.py:59
  208.5 14.8 %collective-permute-start.13 = (f32[1024,256]{1,0:T(8,128)S(1)}, f32[1024,256]{1,0:T(8,128)}, u32[]{:S(2)}, u32[]{:S(2)}) collective-permute-start(f32[1024,256]{1,0:T(8,128)S(1)} %bitcast.157), channel_id=1, source_target_pairs={{0,4},{4,0},{8,12},{12,8},{16,20},{20,16},{24,28},{28,24},{32,36},... | collective-permute-start | bytes 3145736 | tf_op jit(solution)/shard_map/ppermute | solution.py:44
  210.6 6.0 %collective-permute-start.9 = (f32[128,256]{1,0:T(8,128)S(1)}, f32[128,256]{1,0:T(8,128)S(1)}, u32[]{:S(2)}, u32[]{:S(2)}) collective-permute-start(f32[128,256]{1,0:T(8,128)S(1)} %fusion.42), channel_id=1, source_target_pairs={{0,1},{1,2},{2,3},{3,0},{4,5},{5,6},{6,7},{7,4},{8,9},{9,10},{10,1... | collective-permute-start | bytes 393224 | tf_op jit(solution)/shard_map/ppermute | solution.py:63
  211.2 8.6 %collective-permute-start.10 = (f32[128,256]{1,0:T(8,128)S(1)}, f32[128,256]{1,0:T(8,128)S(1)}, u32[]{:S(2)}, u32[]{:S(2)}) collective-permute-start(f32[128,256]{1,0:T(8,128)S(1)} %fusion.42), channel_id=1, source_target_pairs={{0,2},{1,3},{2,0},{3,1},{4,6},{5,7},{6,4},{7,5},{8,10},{9,11},{10,... | collective-permute-start | bytes 393224 | tf_op jit(solution)/shard_map/ppermute | solution.py:63
  213.3 6.5 %collective-permute-start.11 = (f32[128,256]{1,0:T(8,128)S(1)}, f32[128,256]{1,0:T(8,128)S(1)}, u32[]{:S(2)}, u32[]{:S(2)}) collective-permute-start(f32[128,256]{1,0:T(8,128)S(1)} %fusion.42), channel_id=1, source_target_pairs={{0,3},{1,0},{2,1},{3,2},{4,7},{5,4},{6,5},{7,6},{8,11},{9,8},{10,9... | collective-permute-start | bytes 393224 | tf_op jit(solution)/shard_map/ppermute | solution.py:63

commit v10 on v9

--- a/solution.py
+++ b/solution.py
@@ -19,17 +19,25 @@
     return gathered.reshape(value.shape)
 
 
-def pair_psum(value):
+def pair_first(value):
     rows_n = lax.axis_size("rows")
-    rel_n = lax.axis_size("rel")
-    count = rows_n * rel_n
     swap = [(index, index ^ 1) for index in range(rows_n)]
     core = lax.axis_index("rows") % 2
     half = value.shape[0] // 2
     first, second = value[:half], value[half:]
     kept = jnp.where(core == 0, first, second)
     given = jnp.where(core == 0, second, first)
-    chip_sum = kept + lax.ppermute(given, "rows", swap)
+    return kept + lax.ppermute(given, "rows", swap)
+
+
+def pair_psum(chip_sum, value_shape):
+    value = chip_sum
+    rows_n = lax.axis_size("rows")
+    rel_n = lax.axis_size("rel")
+    count = rows_n * rel_n
+    swap = [(index, index ^ 1) for index in range(rows_n)]
+    core = lax.axis_index("rows") % 2
+    half = value_shape[0] // 2
     pieces = lax.all_to_all(
         chip_sum.reshape((count, half // count) + value.shape[1:]), ("rows", "rel"), 0, 0, tiled=True
     )
@@ -185,13 +193,11 @@
     projected_part = jnp.einsum("lbnf,bfg->lng", partial_value, basis_f32, precision=highest)
     basis_local = jnp.einsum("lbnf,lng->bfg", partial_value, cot_f32, precision=highest)
     projected = permute_psum(projected_part.reshape(-1, feat_width), "rel")
-    returned, basis_local, projected = lax.optimization_barrier(
-        (returned, basis_local, projected)
-    )
-
-    basis_grad = pair_psum(basis_local.reshape(-1, basis_local.shape[-1])).reshape(
-        basis_local.shape
-    )
+    basis_rows = basis_local.reshape(-1, basis_local.shape[-1])
+    chip_sum = pair_first(basis_rows)
+    returned, chip_sum, projected = lax.optimization_barrier((returned, chip_sum, projected))
+
+    basis_grad = pair_psum(chip_sum, basis_rows.shape).reshape(basis_local.shape)
 
     block_hot = (send_rows.reshape(-1)[None, :] == jnp.arange(local_blocks)[:, None]).astype(
         jnp.float32

time: 230 us -> 232 us (level)
  other arithmetic: 15.3 us -> 18.7 us
  matrix products: 71.2 us -> 68.5 us
    ppermute x6, waiting for transfers between devices: 4.47 us -> 7.97 us  [permute_psum(): parts.append(lax.ppermute(total, axis, pairs))]
  transfers between devices with their start and end apart: 17 -> 17, of which waited for: 8 -> 9; matrix products, arithmetic and copies ran while one was open for 48% -> 48% of each run, Pallas kernels for 0% -> 0%
where the time goes in v10:
time: 232 us; the launch traced here: 227 us
  matrix products  68.5 us (30%)
  local copies, waits for them, and re-layouts  48.9 us (21%)
  starting transfers between devices  39.1 us (17%)
  blocking collectives  29.9 us (13%)
  waiting for transfers between devices  19.8 us (9%)
  other arithmetic  18.7 us (8%)
    all_to_all x1, blocking collectives, pair_psum(): lax.all_to_all(chip_sum.reshape((count, half // count) + value.shape[1:])...  29.9 us
    dot_general x1, matrix products, backward_step(): lax.dot_general(slot_hot, backward_term, contract_first, precision=highest)  14.3 us
    dot_general x1, matrix products, backward_step(): lax.dot_general(weights, agg_grad, (((1,), (0,)), ((), ())), precision=hi...  11.5 us
    dot_general x1, matrix products, forward_step(): lax.dot_general(weights, messages, contract_first, precision=highest)  11 us
    ppermute x6, starting transfers between devices, permute_psum(): total = total + lax.ppermute(chunks[(me + shift) % size], axis, pairs)  10.1 us
    all_to_all x1, starting transfers between devices, on_device(): lax.all_to_all(outgoing, 'rows', split_axis=0, concat_axis=0, tiled=True)  9.6 us
    dot_general x1, local copies, waits for them, and re-layouts, backward_step(): jnp.einsum('tij,tif->tjf', adjacency, spread, preferred_element_type=jnp....  9.18 us
    ppermute x6, waiting for transfers between devices, permute_psum(): parts.append(lax.ppermute(total, axis, pairs))  7.97 us
  transfers between devices with their start and end apart: 17, of which 9 were waited for; matrix products, arithmetic and copies ran while one was open for 48% of the time, Pallas kernels for 0%

profile of v10, /device:TPU:1, one launch (start us, length us, event | category | flops | bytes accessed | tf_op | source)
XLA Modules:
  0.0 227.5 jit_solution(4300685473054629882)
XLA Ops:
  3.0 2.8 %gather_fusion = bf16[64,128,256]{2,1,0:T(8,128)(2,1)} fusion(bf16[4,128,256]{2,1,0:T(8,128)(2,1)S(1)} %bitcast.152, s32[1024]{0:T(1024)S(1)} %pad_clamp_fusion.2), kind=kCustom, calls=%fused_computation | custom fusion | bytes 8388864 | tf_op jit(solution)/shard_map/gather | solution.py:138
  5.8 3.8 %pad_maximum_fusion = bf16[32,272,256]{2,1,0:T(8,128)(2,1)} fusion(bf16[32,8,256]{2,1,0:T(8,128)(2,1)S(1)} %subtract_convert_fusion.1, bf16[32,8,256]{2,1,0:T(8,128)(2,1)S(1)} %get-tuple-element.292, bf16[32,256,256]{2,1,0:T(8,128)(2,1)} %bitcast.155), kind=kLoop, calls=%fused_computation.32 | loop fusion | flops 13369344 | bytes 8912896 | tf_op jit(solution)/shard_map/concatenate | solution.py:139
  9.6 9.6 %all-to-all-start = ((bf16[32,272,256]{2,1,0:T(8,128)(2,1)}), bf16[32,272,256]{2,1,0:T(8,128)(2,1)}, u32[]{:S(2)}, u32[]{:S(2)}) async-start(bf16[32,272,256]{2,1,0:T(8,128)(2,1)} %pad_maximum_fusion), calls=%async_computation | async-start | bytes 8912896 | tf_op jit(solution)/shard_map/all_to_all | solution.py:140
  19.8 2.7 %convolution_bitcast_fusion = f32[4,8,128,256]{2,3,0,1:T(8,128)} fusion(bf16[4,128,256,1]{2,1,0,3:T(8,128)(2,1)S(1)} %bitcast.161, bf16[8,256,256]{2,1,0:T(8,128)(2,1)S(1)} %copy-done), kind=kOutput, calls=%fused_computation.40 | convolution fusion | flops 536870912 | bytes 5505024 | tf_op jit(solution)/shard_map/lng,bfg->lbnf/dot_general | solution.py:145
  22.6 5.4 %copy.21 = f32[4,8,128,256]{3,2,1,0:T(8,128)} copy(f32[4,8,128,256]{2,3,0,1:T(8,128)} %convolution_bitcast_fusion) | data formatting | bytes 8388608 | tf_op jit(solution)/shard_map/lng,bfg->lbnf/transpose | solution.py:145
  28.2 4.3 %broadcast_in_dim.20 = f32[64,128,256]{2,0,1:T(8,128)} broadcast(f32[]{:T(128)} %constant.107.clone.1), dimensions={} | broadcast | bytes 8388612 | tf_op jit(solution)/shard_map/broadcast_in_dim | solution.py:162
  32.5 42.7 %while.24 = (s32[]{:T(128)}, f32[64,128,256]{2,0,1:T(8,128)}, s32[]{:T(128)}, s32[1,1,64]{2,1,0:T(1,128)S(1)}, s32[1,1,64]{2,1,0:T(1,128)S(1)}, /*index=5*/s32[]...) while((s32[]{:T(128)}, f32[64,128,256]{2,0,1:T(8,128)}, ...), condition=%wide.region_1.2_spmd, body=%wide.region_0.1_spmd.sunk | while | flops 2954894080 | bytes 65016960 | solution.py:163
  33.4 11.5 %fusion.89 = bf16[64,128,256]{2,0,1:T(8,128)(2,1)S(1)} fusion(f32[32,128,256]{2,1,0:T(8,128)} %get-tuple-element.429, f32[64,8]{0,1:T(8,128)S(1)} %get-tuple-element.428, f32[64,4]{0,1:T(4,128)S(1)} %fusion.88), kind=kOutput, calls=%fused_computation.8.clone.1 | convolution fusion | flops 805308416 | bytes 8391680 | tf_op jit(solution)/shard_map/while/body/dot_general | solution.py:151
  44.8 6.6 %fusion.90 = f32[64,256,128]{2,1,0:T(8,128)} fusion(bf16[64,128,128]{2,1,0:T(8,128)(2,1)S(1)} %get-tuple-element.430, bf16[64,128,256]{2,0,1:T(8,128)(2,1)S(1)} %fusion.89), kind=kOutput, calls=%fused_computation.7.clone.1 | convolution fusion | flops 536870912 | bytes 14680064 | tf_op jit(solution)/shard_map/while/body/tij,tif->tjf/dot_general | solution.py:154
  51.4 9.2 %copy.71 = f32[64,256,128]{1,0,2:T(8,128)} copy(f32[64,256,128]{2,1,0:T(8,128)} %fusion.90) | data formatting | bytes 16777216 | tf_op jit(solution)/shard_map/while/body/tij,tif->tjf/dot_general | solution.py:154
  60.6 14.3 %fusion.91 = f32[64,128,256]{2,0,1:T(8,128)} fusion(f32[64,128,256]{2,0,1:T(8,128)} %get-tuple-element.412, f32[64,256,128]{1,0,2:T(8,128)} %copy.71, s32[64]{0:T(128)S(1)} %bitcast.176), kind=kOutput, calls=%fused_computation.10.clone.1 | convolution fusion | flops 1612713984 | bytes 25166080 | tf_op jit(solution)/shard_map/while/body/dot_general | solution.py:158
  76.4 4.9 %slice.34 = bf16[32,256,256]{2,1,0:T(8,128)(2,1)} slice(bf16[32,272,256]{2,1,0:T(8,128)(2,1)} %all-to-all-done), slice={[0:32], [0:256], [0:256]} | slice | bytes 8388608 | tf_op jit(solution)/shard_map/slice | solution.py:174
  82.5 4.5 %copy.61 = bf16[64,128,256]{2,1,0:T(8,128)(2,1)S(1)} copy(f32[64,128,256]{2,0,1:T(8,128)S(1)} %copy-done.1) | data formatting | bytes 12582912 | tf_op jit(solution)/shard_map/optimization_barrier | solution.py:164
  89.3 7.4 %all-to-all-start.1 = ((bf16[32,272,256]{2,1,0:T(8,128)(2,1)}), bf16[32,272,256]{2,1,0:T(8,128)(2,1)}, u32[]{:S(2)}, u32[]{:S(2)}) async-start(bf16[32,272,256]{2,1,0:T(8,128)(2,1)} %pad_maximum_fusion.1), calls=%async_computation.1 | async-start | bytes 8912896 | tf_op jit(solution)/shard_map/all_to_all | solution.py:171
  96.7 5.1 %gather_fusion.1 = bf16[64,128,256]{2,1,0:T(8,128)(2,1)} fusion(bf16[64,128,256]{2,1,0:T(8,128)(2,1)} %bitcast.154, s32[1024]{0:T(1024)S(1)} %pad_clamp_fusion.1), kind=kCustom, calls=%fused_computation.1 | custom fusion | bytes 8388864 | tf_op jit(solution)/shard_map/while/body/gather | solution.py:178
  101.8 2.5 %broadcast_in_dim.31 = f32[32,128,256]{2,0,1:T(8,128)} broadcast(f32[]{:T(128)} %constant.107.clone.1), dimensions={} | broadcast | bytes 4194308 | tf_op jit(solution)/shard_map/broadcast_in_dim | solution.py:187
  104.3 15.3 %while.25 = (s32[]{:T(128)}, f32[32,128,256]{2,0,1:T(8,128)}, s32[]{:T(128)}, s32[1,1,64]{2,1,0:T(1,128)S(1)}, s32[]{:T(128)}, /*index=5*/f32[64,8]{0,1:T(8,128)...) while((s32[]{:T(128)}, f32[32,128,256]{2,0,1:T(8,128)}, ...), condition=%wide.region_4.5_spmd, body=%wide.region_3.4_spmd.sunk | while | flops 1343228672 | bytes 31462264 | solution.py:188
  105.0 3.4 %fusion.96 = f32[64,128,256]{2,1,0:T(8,128)S(1)} fusion(bf16[64,128,128]{2,1,0:T(8,128)(2,1)S(1)} %get-tuple-element.459, bf16[64,128,256]{2,1,0:T(8,128)(2,1)} %get-tuple-element.460), kind=kOutput, calls=%fused_computation.94.clone.1 | convolution fusion | flops 536870912 | bytes 14680064 | tf_op jit(solution)/shard_map/while/body/tij,tjf->tif/dot_general | solution.py:179
  108.4 11.0 %fusion.98 = f32[32,128,256]{2,0,1:T(8,128)} fusion(f32[32,128,256]{2,0,1:T(8,128)} %get-tuple-element.444, f32[64,128,256]{2,1,0:T(8,128)S(1)} %fusion.96, f32[64,8]{0,1:T(8,128)S(1)} %get-tuple-element.458, f32[64,4]{0,1:T(4,128)S(1)} %fusion.97), kind=kOutput, calls=%fused_computation.23.clone.1 | convolution fusion | flops 806356992 | bytes 16780288 | tf_op jit(solution)/shard_map/while/body/dot_general | solution.py:183
  119.5 7.4 %fusion.32 = f32[8,256,256]{2,1,0:T(8,128)S(1)} fusion(bf16[4,128,256,1]{2,1,0,3:T(8,128)(2,1)S(1)} %bitcast.162, f32[4,8,128,256]{3,1,0,2:T(8,128)} %bitcast.28), kind=kOutput, calls=%fused_computation.42 | convolution fusion | flops 3221225472 | bytes 6553600 | tf_op jit(solution)/shard_map/lbnf,lng->bfg/dot_general | solution.py:194
  128.5 6.4 %fusion.35 = f32[4,128,256]{2,1,0:T(8,128)S(1)} fusion(f32[4,8,128,256]{3,1,0,2:T(8,128)} %bitcast.28, bf16[8,256,256]{2,1,0:T(8,128)(2,1)S(1)} %copy-done), kind=kOutput, calls=%fused_computation.43 | convolution fusion | flops 3221225472 | bytes 5767168 | tf_op jit(solution)/shard_map/lbnf,bfg->lng/dot_general | solution.py:193
  136.3 2.6 %collective-permute-start.2 = (f32[128,256]{1,0:T(8,128)S(1)}, f32[128,256]{1,0:T(8,128)S(1)}, u32[]{:S(2)}, u32[]{:S(2)}) collective-permute-start(f32[128,256]{1,0:T(8,128)S(1)} %get-tuple-element.291), channel_id=1, source_target_pairs={{0,2},{1,3},{2,0},{3,1},{4,6},{5,7},{6,4},{7,5},{8,10},{9,11},{10,... | collective-permute-start | bytes 393224 | tf_op jit(solution)/shard_map/ppermute | solution.py:67
  141.3 3.9 %collective-permute-done.2 = f32[128,256]{1,0:T(8,128)S(1)} collective-permute-done((f32[128,256]{1,0:T(8,128)S(1)}, f32[128,256]{1,0:T(8,128)S(1)}, u32[]{:S(2)}, u32[]{:S(2)}) %collective-permute-start.2) | collective-permute-done | bytes 131104 | tf_op jit(solution)/shard_map/ppermute | solution.py:67
  146.2 2.4 %collective-permute-start.5 = (f32[128,256]{1,0:T(8,128)S(1)}, f32[128,256]{1,0:T(8,128)S(1)}, u32[]{:S(2)}, u32[]{:S(2)}) collective-permute-start(f32[128,256]{1,0:T(8,128)S(1)} %fusion.43), channel_id=1, source_target_pairs={{0,2},{1,3},{2,0},{3,1},{4,6},{5,7},{6,4},{7,5},{8,10},{9,11},{10,... | collective-permute-start | bytes 393224 | tf_op jit(solution)/shard_map/ppermute | solution.py:71
  150.8 3.3 %collective-permute-done.5 = f32[128,256]{1,0:T(8,128)S(1)} collective-permute-done((f32[128,256]{1,0:T(8,128)S(1)}, f32[128,256]{1,0:T(8,128)S(1)}, u32[]{:S(2)}, u32[]{:S(2)}) %collective-permute-start.5) | collective-permute-done | bytes 131104 | tf_op jit(solution)/shard_map/ppermute | solution.py:71
  157.0 29.9 %all_to_all.20 = f32[128,8,256]{2,1,0:T(8,128)S(1)} all-to-all(f32[128,8,256]{2,1,0:T(8,128)S(1)} %bitcast.159), channel_id=1, replica_groups=mesh['rows'=32,'rel'=4] {'rows','rel'}, dimensions={0} | all-to-all | bytes 2097152 | tf_op jit(solution)/shard_map/all_to_all | solution.py:41
  188.0 3.6 %all-to-all-start.3 = ((f32[128,8,256]{2,1,0:T(8,128)}), f32[128,8,256]{2,1,0:T(8,128)S(1)}, u32[]{:S(2)}, u32[]{:S(2)}) async-start(f32[128,8,256]{2,1,0:T(8,128)} %bitcast.55), calls=%async_computation.3 | async-start | bytes 2097152 | tf_op jit(solution)/shard_map/all_to_all | solution.py:49
  192.1 2.5 %slice.37 = bf16[32,256,256]{2,1,0:T(8,128)(2,1)S(1)} slice(bf16[32,272,256]{2,1,0:T(8,128)(2,1)} %all-to-all-done.1), slice={[0:32], [0:256], [0:256]} | slice | bytes 8388608 | tf_op jit(solution)/shard_map/slice | solution.py:207
  200.8 2.5 %collective-permute-start.8 = (f32[128,256]{1,0:T(8,128)}, f32[128,256]{1,0:T(8,128)}, u32[]{:S(2)}, u32[]{:S(2)}) collective-permute-start(f32[128,256]{1,0:T(8,128)} %bitcast.127), channel_id=1, source_target_pairs={{0,2},{1,3},{2,0},{3,1},{4,6},{5,7},{6,4},{7,5},{8,10},{9,11},{10,... | collective-permute-start | bytes 393224 | tf_op jit(solution)/shard_map/ppermute | solution.py:67
  205.0 6.5 %all-to-all-done.3 = f32[128,8,256]{2,1,0:T(8,128)S(1)} async-done(((f32[128,8,256]{2,1,0:T(8,128)}), f32[128,8,256]{2,1,0:T(8,128)S(1)}, u32[]{:S(2)}, u32[]{:S(2)}) %all-to-all-start.3) | async-done | bytes 1048608 | tf_op jit(solution)/shard_map/all_to_all | solution.py:49
  219.3 2.7 %collective-permute-done.11 = f32[128,256]{1,0:T(8,128)S(1)} collective-permute-done((f32[128,256]{1,0:T(8,128)S(1)}, f32[128,256]{1,0:T(8,128)S(1)}, u32[]{:S(2)}, u32[]{:S(2)}) %collective-permute-start.11) | collective-permute-done | bytes 131104 | tf_op jit(solution)/shard_map/ppermute | solution.py:71
  224.1 3.2 %maximum_select_fusion = f32[2048,256]{1,0:T(8,128)} fusion(f32[1024,256]{1,0:T(8,128)} %collective-permute-done.13, f32[1024,256]{1,0:T(8,128)S(1)} %bitcast.158, pred[]{:T(512)S(6)} %eq.133), kind=kLoop, calls=%fused_computation.41 | loop fusion | flops 1572864 | bytes 4194305 | tf_op jit(solution)/shard_map/jit(_where)/select_n | solution.py:53
  (96 shorter events, 39.1 us)
Async XLA Ops:
  0.6 19.2 %copy-start = (bf16[8,256,256]{2,1,0:T(8,128)(2,1)S(1)}, bf16[8,256,256]{2,1,0:T(8,128)(2,1)}, u32[]{:S(2)}) copy-start(bf16[8,256,256]{2,1,0:T(8,128)(2,1)} %param.16) | copy-start | bytes 3145732
  0.6 2.3 %copy-start.3 = (bf16[512,256]{1,0:T(8,128)(2,1)S(1)}, bf16[512,256]{1,0:T(8,128)(2,1)}, u32[]{:S(2)}) copy-start(bf16[512,256]{1,0:T(8,128)(2,1)} %param.15) | copy-start | bytes 786436
  9.6 10.3 %copy-start.5 = (bf16[512,256]{1,0:T(8,128)(2,1)S(1)}, bf16[512,256]{1,0:T(8,128)(2,1)}, u32[]{:S(2)}) copy-start(bf16[512,256]{1,0:T(8,128)(2,1)} %param.25) | copy-start | bytes 786436
  9.6 65.8 %all-to-all-start = ((bf16[32,272,256]{2,1,0:T(8,128)(2,1)}), bf16[32,272,256]{2,1,0:T(8,128)(2,1)}, u32[]{:S(2)}, u32[]{:S(2)}) async-start(bf16[32,272,256]{2,1,0:T(8,128)(2,1)} %pad_maximum_fusion), calls=%async_computation | async-start | bytes 8912896 | tf_op jit(solution)/shard_map/all_to_all | solution.py:140
  22.6 5.4 %copy-start.13 = (f32[200,8]{0,1:T(8,128)S(1)}, f32[200,8]{0,1:T(8,128)}, u32[]{:S(2)}) copy-start(f32[200,8]{0,1:T(8,128)} %param.18) | copy-start | bytes 19204
  22.6 5.4 %copy-start.14 = (s32[1,1,64]{2,1,0:T(1,128)S(1)}, s32[1,1,64]{2,1,0:T(1,128)}, u32[]{:S(2)}) copy-start(s32[1,1,64]{2,1,0:T(1,128)} %param.22) | copy-start | bytes 772
  28.1 4.4 %copy-start.2 = (bf16[1,1,64,128,128]{4,3,2,1,0:T(8,128)(2,1)S(1)}, bf16[1,1,64,128,128]{4,3,2,1,0:T(8,128)(2,1)}, u32[]{:S(2)}) copy-start(bf16[1,1,64,128,128]{4,3,2,1,0:T(8,128)(2,1)} %param.19) | copy-start | bytes 6291460
  28.1 4.4 %copy-start.10 = (s32[1,1,64]{2,1,0:T(1,128)S(1)}, s32[1,1,64]{2,1,0:T(1,128)}, u32[]{:S(2)}) copy-start(s32[1,1,64]{2,1,0:T(1,128)} %param.20) | copy-start | bytes 772
  28.1 4.4 %copy-start.11 = (s32[1,1,64]{2,1,0:T(1,128)S(1)}, s32[1,1,64]{2,1,0:T(1,128)}, u32[]{:S(2)}) copy-start(s32[1,1,64]{2,1,0:T(1,128)} %param.21) | copy-start | bytes 772
  76.4 6.2 %copy-start.1 = (f32[64,128,256]{2,0,1:T(8,128)S(1)}, f32[64,128,256]{2,0,1:T(8,128)}, u32[]{:S(2)}) copy-start(f32[64,128,256]{2,0,1:T(8,128)} %get-tuple-element.242) | copy-start | bytes 25165828
  89.3 67.7 %all-to-all-start.1 = ((bf16[32,272,256]{2,1,0:T(8,128)(2,1)}), bf16[32,272,256]{2,1,0:T(8,128)(2,1)}, u32[]{:S(2)}, u32[]{:S(2)}) async-start(bf16[32,272,256]{2,1,0:T(8,128)(2,1)} %pad_maximum_fusion.1), calls=%async_computation.1 | async-start | bytes 8912896 | tf_op jit(solution)/shard_map/all_to_all | solution.py:171
  104.3 15.3 %copy-start.6 = (bf16[512,256]{1,0:T(8,128)(2,1)S(1)}, bf16[512,256]{1,0:T(8,128)(2,1)}, u32[]{:S(2)}) copy-start(bf16[512,256]{1,0:T(8,128)(2,1)} %param.25) | copy-start | bytes 786436
  128.2 27.4 %collective-permute-start = (f32[1024,256]{1,0:T(8,128)}, f32[1024,256]{1,0:T(8,128)}, u32[]{:S(2)}, u32[]{:S(2)}) collective-permute-start(f32[1024,256]{1,0:T(8,128)} %bitcast.33), channel_id=1, source_target_pairs={{0,4},{4,0},{8,12},{12,8},{16,20},{20,16},{24,28},{28,24},{32,36},... | collective-permute-start | bytes 3145736 | tf_op jit(solution)/shard_map/ppermute | solution.py:30
  135.0 6.4 %collective-permute-start.1 = (f32[128,256]{1,0:T(8,128)S(1)}, f32[128,256]{1,0:T(8,128)S(1)}, u32[]{:S(2)}, u32[]{:S(2)}) collective-permute-start(f32[128,256]{1,0:T(8,128)S(1)} %get-tuple-element.289), channel_id=1, source_target_pairs={{0,1},{1,2},{2,3},{3,0},{4,5},{5,6},{6,7},{7,4},{8,9},{9,10},{10,1... | collective-permute-start | bytes 393224 | tf_op jit(solution)/shard_map/ppermute | solution.py:67
  136.3 8.9 %collective-permute-start.2 = (f32[128,256]{1,0:T(8,128)S(1)}, f32[128,256]{1,0:T(8,128)S(1)}, u32[]{:S(2)}, u32[]{:S(2)}) collective-permute-start(f32[128,256]{1,0:T(8,128)S(1)} %get-tuple-element.291), channel_id=1, source_target_pairs={{0,2},{1,3},{2,0},{3,1},{4,6},{5,7},{6,4},{7,5},{8,10},{9,11},{10,... | collective-permute-start | bytes 393224 | tf_op jit(solution)/shard_map/ppermute | solution.py:67
  138.9 6.3 %collective-permute-start.3 = (f32[128,256]{1,0:T(8,128)S(1)}, f32[128,256]{1,0:T(8,128)S(1)}, u32[]{:S(2)}, u32[]{:S(2)}) collective-permute-start(f32[128,256]{1,0:T(8,128)S(1)} %get-tuple-element.290), channel_id=1, source_target_pairs={{0,3},{1,0},{2,1},{3,2},{4,7},{5,4},{6,5},{7,6},{8,11},{9,8},{10,9... | collective-permute-start | bytes 393224 | tf_op jit(solution)/shard_map/ppermute | solution.py:67
  145.3 5.5 %collective-permute-start.4 = (f32[128,256]{1,0:T(8,128)S(1)}, f32[128,256]{1,0:T(8,128)S(1)}, u32[]{:S(2)}, u32[]{:S(2)}) collective-permute-start(f32[128,256]{1,0:T(8,128)S(1)} %fusion.43), channel_id=1, source_target_pairs={{0,1},{1,2},{2,3},{3,0},{4,5},{5,6},{6,7},{7,4},{8,9},{9,10},{10,1... | collective-permute-start | bytes 393224 | tf_op jit(solution)/shard_map/ppermute | solution.py:71
  146.2 7.9 %collective-permute-start.5 = (f32[128,256]{1,0:T(8,128)S(1)}, f32[128,256]{1,0:T(8,128)S(1)}, u32[]{:S(2)}, u32[]{:S(2)}) collective-permute-start(f32[128,256]{1,0:T(8,128)S(1)} %fusion.43), channel_id=1, source_target_pairs={{0,2},{1,3},{2,0},{3,1},{4,6},{5,7},{6,4},{7,5},{8,10},{9,11},{10,... | collective-permute-start | bytes 393224 | tf_op jit(solution)/shard_map/ppermute | solution.py:71
  148.5 5.6 %collective-permute-start.6 = (f32[128,256]{1,0:T(8,128)S(1)}, f32[128,256]{1,0:T(8,128)S(1)}, u32[]{:S(2)}, u32[]{:S(2)}) collective-permute-start(f32[128,256]{1,0:T(8,128)S(1)} %fusion.43), channel_id=1, source_target_pairs={{0,3},{1,0},{2,1},{3,2},{4,7},{5,4},{6,5},{7,6},{8,11},{9,8},{10,9... | collective-permute-start | bytes 393224 | tf_op jit(solution)/shard_map/ppermute | solution.py:71
  155.6 36.1 %copy-start.12 = (s32[1,1,32,2]{2,3,1,0:T(2,128)S(1)}, s32[1,1,32,2]{2,3,1,0:T(2,128)}, u32[]{:S(2)}) copy-start(s32[1,1,32,2]{2,3,1,0:T(2,128)} %param.24) | copy-start | bytes 772
  155.6 36.3 %copy-start.4 = (bf16[512,256]{1,0:T(8,128)(2,1)S(1)}, bf16[512,256]{1,0:T(8,128)(2,1)}, u32[]{:S(2)}) copy-start(bf16[512,256]{1,0:T(8,128)(2,1)} %param.15) | copy-start | bytes 786436
  155.6 36.3 %copy-start.9 = (bf16[256,256]{1,0:T(8,128)(2,1)S(1)}, bf16[256,256]{1,0:T(8,128)(2,1)}, u32[]{:S(2)}) copy-start(bf16[256,256]{1,0:T(8,128)(2,1)} %param.17) | copy-start | bytes 393220
  188.0 23.5 %all-to-all-start.3 = ((f32[128,8,256]{2,1,0:T(8,128)}), f32[128,8,256]{2,1,0:T(8,128)S(1)}, u32[]{:S(2)}, u32[]{:S(2)}) async-start(f32[128,8,256]{2,1,0:T(8,128)} %bitcast.55), calls=%async_computation.3 | async-start | bytes 2097152 | tf_op jit(solution)/shard_map/all_to_all | solution.py:49
  194.5 17.1 %copy-start.8 = (f32[4,128,256]{2,1,0:T(8,128)S(1)}, f32[4,128,256]{2,1,0:T(8,128)}, u32[]{:S(2)}) copy-start(f32[4,128,256]{2,1,0:T(8,128)} %gather_fusion.2) | copy-start | bytes 1572868
  196.9 26.1 %copy-start.7 = (bf16[512,256]{1,0:T(8,128)(2,1)S(1)}, bf16[512,256]{1,0:T(8,128)(2,1)}, u32[]{:S(2)}) copy-start(bf16[512,256]{1,0:T(8,128)(2,1)} %param.25) | copy-start | bytes 786436
  198.7 13.7 %collective-permute-start.7 = (f32[128,256]{1,0:T(8,128)}, f32[128,256]{1,0:T(8,128)}, u32[]{:S(2)}, u32[]{:S(2)}) collective-permute-start(f32[128,256]{1,0:T(8,128)} %bitcast.128), channel_id=1, source_target_pairs={{0,1},{1,2},{2,3},{3,0},{4,5},{5,6},{6,7},{7,4},{8,9},{9,10},{10,1... | collective-permute-start | bytes 393224 | tf_op jit(solution)/shard_map/ppermute | solution.py:67
  200.8 11.8 %collective-permute-start.8 = (f32[128,256]{1,0:T(8,128)}, f32[128,256]{1,0:T(8,128)}, u32[]{:S(2)}, u32[]{:S(2)}) collective-permute-start(f32[128,256]{1,0:T(8,128)} %bitcast.127), channel_id=1, source_target_pairs={{0,2},{1,3},{2,0},{3,1},{4,6},{5,7},{6,4},{7,5},{8,10},{9,11},{10,... | collective-permute-start | bytes 393224 | tf_op jit(solution)/shard_map/ppermute | solution.py:67
  203.9 8.6 %collective-permute-start.9 = (f32[128,256]{1,0:T(8,128)}, f32[128,256]{1,0:T(8,128)}, u32[]{:S(2)}, u32[]{:S(2)}) collective-permute-start(f32[128,256]{1,0:T(8,128)} %bitcast.126), channel_id=1, source_target_pairs={{0,3},{1,0},{2,1},{3,2},{4,7},{5,4},{6,5},{7,6},{8,11},{9,8},{10,9... | collective-permute-start | bytes 393224 | tf_op jit(solution)/shard_map/ppermute | solution.py:67
  211.5 12.6 %collective-permute-start.13 = (f32[1024,256]{1,0:T(8,128)S(1)}, f32[1024,256]{1,0:T(8,128)}, u32[]{:S(2)}, u32[]{:S(2)}) collective-permute-start(f32[1024,256]{1,0:T(8,128)S(1)} %bitcast.157), channel_id=1, source_target_pairs={{0,4},{4,0},{8,12},{12,8},{16,20},{20,16},{24,28},{28,24},{32,36},... | collective-permute-start | bytes 3145736 | tf_op jit(solution)/shard_map/ppermute | solution.py:52
  213.7 5.6 %collective-permute-start.10 = (f32[128,256]{1,0:T(8,128)S(1)}, f32[128,256]{1,0:T(8,128)S(1)}, u32[]{:S(2)}, u32[]{:S(2)}) collective-permute-start(f32[128,256]{1,0:T(8,128)S(1)} %fusion.41), channel_id=1, source_target_pairs={{0,1},{1,2},{2,3},{3,0},{4,5},{5,6},{6,7},{7,4},{8,9},{9,10},{10,1... | collective-permute-start | bytes 393224 | tf_op jit(solution)/shard_map/ppermute | solution.py:71
  214.6 7.4 %collective-permute-start.11 = (f32[128,256]{1,0:T(8,128)S(1)}, f32[128,256]{1,0:T(8,128)S(1)}, u32[]{:S(2)}, u32[]{:S(2)}) collective-permute-start(f32[128,256]{1,0:T(8,128)S(1)} %fusion.41), channel_id=1, source_target_pairs={{0,2},{1,3},{2,0},{3,1},{4,6},{5,7},{6,4},{7,5},{8,10},{9,11},{10,... | collective-permute-start | bytes 393224 | tf_op jit(solution)/shard_map/ppermute | solution.py:71
  216.2 6.2 %collective-permute-start.12 = (f32[128,256]{1,0:T(8,128)S(1)}, f32[128,256]{1,0:T(8,128)S(1)}, u32[]{:S(2)}, u32[]{:S(2)}) collective-permute-start(f32[128,256]{1,0:T(8,128)S(1)} %fusion.41), channel_id=1, source_target_pairs={{0,3},{1,0},{2,1},{3,2},{4,7},{5,4},{6,5},{7,6},{8,11},{9,8},{10,9... | collective-permute-start | bytes 393224 | tf_op jit(solution)/shard_map/ppermute | solution.py:71
